TPU v7x, 32 devices: a whole 2x2x4 slice. The times are simulated.
32 devices in a mesh: groups: 2 (over y), seq: 4 (over z), head: 2 (over x), rep: 2 (over core).
Axes of the slice: x: 2, y: 2, z: 4, core: 2. Of those that a mesh axis runs over, the one named last changes fastest.
Arguments:
- tokens: bfloat16 [4096, 5376], P(('groups', 'seq'), ('head', 'rep')), parts along dimension 0, may hold values from -6 to 6
- query_matrix: bfloat16 [5376, 2048], P(None, ('head', 'rep')), may hold values from -0.078125 to 0.078125
- key_matrix: bfloat16 [5376, 1024], P(None, 'head'), may hold values from -0.078125 to 0.078125
- value_matrix: bfloat16 [5376, 1024], P(None, 'head'), may hold values from -0.078125 to 0.078125
- output_matrix: bfloat16 [2048, 5376], P(None, ('head', 'rep')), may hold values from -0.125 to 0.125
- query_gain: float32 [128], replicated, may hold values from 0.1 to 1.9
- key_norm_gain: float32 [128], replicated, may hold values from 0.1 to 1.9
- adapter_down: bfloat16 [8, 5376, 96], P('seq', ('head', 'rep')), may hold values from -0.078125 to 0.078125
- adapter_up_query: bfloat16 [8, 32, 2048], P('seq', None, ('head', 'rep')), may hold values from -1 to 1
- key_value_up_panels: bfloat16 [8, 2, 32, 1024], P('seq', None, None, 'head'), may hold values from -1 to 1
- adapter_out_down: bfloat16 [8, 2048, 32], P('seq', ('head', 'rep')), may hold values from -0.125 to 0.125
- adapter_out_up: bfloat16 [8, 32, 5376], P('seq', None, ('head', 'rep')), may hold values from -1 to 1
- request_of_block: int32 [32], P('groups'), parts along dimension 0, may hold values from 0 to 1, never falling along the last dimension, each value on 1 to 12 neighbouring positions
- adapter_of_request: int32 [4], P('groups'), parts along dimension 0, may hold values from 0 to 7
Outputs:
- result: bfloat16 [4096, 5376], P(('groups', 'seq'), ('head', 'rep')), parts along dimension 0
There are 2 independent parts, one for each index of `groups`. A program takes and returns all parts, laid end to end along the dimension named above; an argument that names none is the same for every part. Nothing has to cross between parts.
Inputs may be any that keep to these rules, and one draw needn't show every extreme that they name: `request_of_block`: never falls from one block to the next; every request has 1 to 12 blocks.
All inputs are finite; a program needn't handle non-finite values.
Results may differ from a plain program's by a relative error of at most 0.014.
Values may be sent and summed in bfloat16 or wider, within the bound.
No kernel may reach another device: no remote copies, remote signals or barrier semaphores. Data moves between devices by JAX's collectives and lax.ppermute only.
A program may use at most 128 MiB of HBM per device.

v0:
```python
import math

import jax
import jax.numpy as jnp
from jax import lax
from jax.sharding import PartitionSpec as P

HEAD_SIZE = 128
ADAPTER_RANK = 32
KEY_WINDOW = 1024
BLOCK = 128


norm_epsilon = 1e-06
rope_base = 10000.0
score_scale = 168.0 ** (-0.5)
adapter_scale = 2.0


def shifted(value, axis, by):
    size = lax.axis_size(axis)
    pairs = [(i, i + by) for i in range(size) if 0 <= i + by < size]
    return lax.ppermute(value, axis, pairs)


def per_head_norm(values, scale_gain):
    mean_square = jnp.mean(values * values, axis=-1, keepdims=True)
    return values * lax.rsqrt(mean_square + norm_epsilon) * scale_gain


def rope_tables(positions, head_dim):
    half_dim = head_dim // 2
    frequency = jnp.power(rope_base, -jnp.arange(half_dim, dtype=jnp.float32) * 2.0 / head_dim)
    angles = positions.astype(jnp.float32)[:, None] * frequency[None, :]
    return (jnp.cos(angles), jnp.sin(angles))


def rotate_feature_pairs(values, cosine_table, sine_values):
    half_dim = values.shape[-1] // 2
    first_half = values[..., :half_dim]
    second_half = values[..., half_dim:]
    cosine_table = cosine_table[:, None, :]
    sine_values = sine_values[:, None, :]
    return jnp.concatenate(
        [
            first_half * cosine_table - second_half * sine_values,
            second_half * cosine_table + first_half * sine_values,
        ],
        axis=-1,
    )


def request_starts(block_requests, all_requests):
    earlier = (all_requests[None, :] < block_requests[:, None]).astype(jnp.int32)
    return jnp.sum(earlier, axis=1) * BLOCK


def per_device(
    tokens,
    query_matrix,
    key_matrix,
    value_matrix,
    output_matrix,
    query_gain,
    key_norm_gain,
    adapter_down,
    adapter_up_query,
    key_value_up_panels,
    adapter_out_down,
    adapter_out_up,
    request_of_block,
    adapter_of_request,
):
    tok_rows, width_part = tokens.shape
    query_cols = query_matrix.shape[1]
    key_cols = key_matrix.shape[1]
    query_heads = query_cols // HEAD_SIZE
    block_count = tok_rows // BLOCK
    all_blocks = request_of_block.shape[0]
    request_total = adapter_of_request.shape[0]
    seq_index = lax.axis_index("seq")
    rep_index = lax.axis_index("rep")
    first_row = seq_index * tok_rows
    own_requests = lax.dynamic_slice_in_dim(
        request_of_block, seq_index * block_count, block_count, 0
    )
    request_match = own_requests[:, None] == jnp.arange(request_total, dtype=jnp.int32)[None, :]
    own_adapters = jnp.sum(jnp.where(request_match, adapter_of_request[None, :], 0), axis=1)
    pool_part = (
        lax.all_gather(adapter_down, "seq", axis=0, tiled=True),
        lax.all_gather(adapter_up_query, "seq", axis=0, tiled=True),
        lax.all_gather(key_value_up_panels, "seq", axis=0, tiled=True),
        lax.all_gather(adapter_out_down, "seq", axis=0, tiled=True),
        lax.all_gather(adapter_out_up, "seq", axis=0, tiled=True),
    )
    held_count = pool_part[0].shape[0]
    select = (own_adapters[:, None] == jnp.arange(held_count, dtype=jnp.int32)[None, :]).astype(
        jnp.bfloat16
    )
    (
        picked_down_panels,
        picked_query_panels,
        picked_key_panels,
        chosen_out_down,
        picked_output_up,
    ) = tuple(
        (
            jnp.einsum(
                "bn,n...->b...", select, panel_part, preferred_element_type=jnp.float32
            ).astype(jnp.bfloat16)
            for panel_part in pool_part
        )
    )
    token_block_list = tokens.reshape(block_count, BLOCK, width_part)
    partial_low = jnp.einsum(
        "myj,mjc->myc", token_block_list, picked_down_panels, preferred_element_type=jnp.float32
    ).reshape(tok_rows, 3 * ADAPTER_RANK)
    reduced_rank_rows = (
        lax.psum(partial_low, ("head", "rep"))
        .astype(jnp.bfloat16)
        .reshape(block_count, BLOCK, 3 * ADAPTER_RANK)
    )
    feature_part = lax.all_gather(tokens, ("head", "rep"), axis=1, tiled=True)
    query_add = jnp.dot(feature_part, query_matrix, preferred_element_type=jnp.float32)
    key_add = jnp.dot(feature_part, key_matrix, preferred_element_type=jnp.float32)
    value_add = jnp.dot(feature_part, value_matrix, preferred_element_type=jnp.float32)
    query_linear = query_add
    key_linear = key_add
    value_linear = value_add
    query_linear = query_linear + adapter_scale * jnp.einsum(
        "tlq,tqo->tlo",
        reduced_rank_rows[..., :ADAPTER_RANK],
        picked_query_panels,
        preferred_element_type=jnp.float32,
    ).reshape(tok_rows, query_cols)
    key_linear = key_linear + adapter_scale * jnp.einsum(
        "tlq,tqo->tlo",
        reduced_rank_rows[..., ADAPTER_RANK : 2 * ADAPTER_RANK],
        picked_key_panels[:, 0],
        preferred_element_type=jnp.float32,
    ).reshape(tok_rows, key_cols)
    value_linear = value_linear + adapter_scale * jnp.einsum(
        "tlq,tqo->tlo",
        reduced_rank_rows[..., 2 * ADAPTER_RANK :],
        picked_key_panels[:, 1],
        preferred_element_type=jnp.float32,
    ).reshape(tok_rows, key_cols)
    key_full = key_linear.astype(jnp.bfloat16)
    value_full = value_linear.astype(jnp.bfloat16)
    key_heads = key_cols // HEAD_SIZE
    token_index = first_row + jnp.arange(tok_rows, dtype=jnp.int32)
    token_request = jnp.repeat(own_requests, BLOCK)
    token_start = jnp.repeat(request_starts(own_requests, request_of_block), BLOCK)
    cosine_table, sine_values = rope_tables(token_index - token_start, HEAD_SIZE)
    query_rows = (
        rotate_feature_pairs(
            per_head_norm(query_linear.reshape(tok_rows, query_heads, HEAD_SIZE), query_gain),
            cosine_table,
            sine_values,
        )
        * score_scale
    ).astype(jnp.bfloat16)
    rotated_keys = rotate_feature_pairs(
        per_head_norm(
            key_full.astype(jnp.float32).reshape(tok_rows, key_heads, HEAD_SIZE), key_norm_gain
        ),
        cosine_table,
        sine_values,
    ).astype(jnp.bfloat16)
    group_heads = max(query_heads // 2, 1)
    group_size = query_heads // group_heads
    head_first = rep_index * query_heads // 2
    keys_used = lax.dynamic_slice_in_dim(rotated_keys, head_first, group_heads, 1).reshape(
        tok_rows, group_heads * HEAD_SIZE
    )
    values_used = lax.dynamic_slice_in_dim(
        value_full.reshape(tok_rows, key_heads, HEAD_SIZE), head_first, group_heads, 1
    ).reshape(tok_rows, group_heads * HEAD_SIZE)
    query_groups = query_rows.reshape(tok_rows, group_heads, group_size, HEAD_SIZE)
    block_table = jnp.arange(all_blocks, dtype=jnp.int32)
    empty_state = (
        jnp.zeros((tok_rows, group_heads, group_size, HEAD_SIZE), jnp.float32),
        jnp.zeros((group_heads, group_size, tok_rows), jnp.float32),
    )
    reach_blocks = KEY_WINDOW // tok_rows
    stacked = jnp.stack((keys_used, values_used))
    earlier = []
    for step_back in range(reach_blocks, 0, -1):
        earlier.append(shifted(stacked, "seq", step_back))
    window_stack = jnp.concatenate(earlier + [stacked], axis=1)
    fold_state = empty_state
    offset = first_row - reach_blocks * tok_rows
    key_block = window_stack[0]
    value_block = window_stack[1]
    key_length = key_block.shape[0]
    step_length = math.gcd(key_length, 512)
    steps_count = key_length // step_length
    key_steps = key_block.reshape(steps_count, step_length, group_heads, HEAD_SIZE)
    value_steps = value_block.reshape(steps_count, step_length, group_heads, HEAD_SIZE)

    def one_step(carry_state, step_inputs):
        step_keys, step_values, step_index = step_inputs
        key_position = offset + step_index * step_length + jnp.arange(step_length, dtype=jnp.int32)
        key_block_id = jnp.clip(key_position, 0, all_blocks * BLOCK - 1) // BLOCK
        key_request = jnp.sum(
            jnp.where(key_block_id[:, None] == block_table[None, :], request_of_block[None, :], 0),
            axis=1,
        )
        distance = token_index[:, None] - key_position[None, :]
        allowed = (
            (key_position[None, :] >= 0)
            & (distance >= 0)
            & (distance < KEY_WINDOW)
            & (token_request[:, None] == key_request[None, :])
        )
        scores = jnp.einsum(
            "tcpd,kcd->cptk", query_groups, step_keys, preferred_element_type=jnp.float32
        )
        weights = jnp.where(allowed[None, None], jnp.exp(scores), 0.0)
        numerator, denominator = carry_state
        denominator = denominator + jnp.sum(weights, axis=-1)
        numerator = numerator + jnp.einsum(
            "cptk,kcd->tcpd",
            weights.astype(jnp.bfloat16),
            step_values,
            preferred_element_type=jnp.float32,
        )
        return ((numerator, denominator), None)

    fold_state, unused_out = lax.scan(
        one_step, fold_state, (key_steps, value_steps, jnp.arange(steps_count, dtype=jnp.int32))
    )
    numerator, denominator = fold_state
    attention_result = (
        (numerator / jnp.transpose(denominator, (2, 0, 1))[..., None])
        .astype(jnp.bfloat16)
        .reshape(tok_rows, query_cols)
    )
    output_zero = (
        jnp.zeros((tok_rows, width_part), jnp.float32),
        jnp.zeros((tok_rows, ADAPTER_RANK), jnp.float32),
    )
    projected_rows = jnp.dot(
        lax.all_gather(attention_result, ("head", "rep"), axis=1, tiled=True),
        output_matrix,
        preferred_element_type=jnp.float32,
    )
    projected_rows, lowered = (projected_rows, output_zero[1])
    local_low = jnp.einsum(
        "bkc,bcr->bkr",
        attention_result.reshape(block_count, BLOCK, query_cols),
        chosen_out_down,
        preferred_element_type=jnp.float32,
    ).reshape(tok_rows, ADAPTER_RANK)
    output_reduced_rank = lax.psum(local_low, ("head", "rep")).astype(jnp.bfloat16)
    result = projected_rows + adapter_scale * jnp.einsum(
        "zch,zhp->zcp",
        output_reduced_rank.reshape(block_count, BLOCK, ADAPTER_RANK),
        picked_output_up,
        preferred_element_type=jnp.float32,
    ).reshape(tok_rows, width_part)
    return result.astype(jnp.bfloat16)


def solution(mesh):
    return jax.shard_map(
        per_device,
        mesh=mesh,
        in_specs=(
            P(("groups", "seq"), ("head", "rep")),
            P(None, ("head", "rep")),
            P(None, "head"),
            P(None, "head"),
            P(None, ("head", "rep")),
            P(),
            P(),
            P("seq", ("head", "rep"), None),
            P("seq", None, ("head", "rep")),
            P("seq", None, None, "head"),
            P("seq", ("head", "rep"), None),
            P("seq", None, ("head", "rep")),
            P("groups"),
            P("groups"),
        ),
        out_specs=P(("groups", "seq"), ("head", "rep")),
        check_vma=False,
    )
```

profile of v0, /device:TPU:0, one launch (start us, length us, event | category | flops | bytes accessed | tf_op | source)
XLA Modules:
  0.0 259.6 jit_solution(15790281969873115158)
XLA Ops:
  8.9 16.8 %all_gather.24 = bf16[8,32,512]{2,1,0:T(8,128)(2,1)S(1)} all-gather(bf16[2,32,512]{2,1,0:T(8,128)(2,1)} %param.24), channel_id=1, replica_groups=mesh['groups'=2,'seq'=4,'head'=2,'rep'=2] {'seq'}, dimensions={0}, use_global_device_ids=true | all-gather | bytes 327680 | tf_op jit(solution)/shard_map/all_gather | solution.py:91
  25.8 0.8 convert_reduce_fusion
  27.3 23.4 %all_gather.23 = bf16[8,2,32,512]{3,2,1,0:T(8,128)(2,1)S(1)} all-gather(bf16[2,2,32,512]{3,2,1,0:T(8,128)(2,1)} %param.25), channel_id=1, replica_groups=mesh['groups'=2,'seq'=4,'head'=2,'rep'=2] {'seq'}, dimensions={0}, use_global_device_ids=true | all-gather | bytes 655360 | tf_op jit(solution)/shard_map/all_gather | solution.py:92
  52.2 15.6 %all-gather.6.cloned.1.call-done = bf16[8,1344,96]{1,2,0:T(8,128)(2,1)} async-done(((bf16[2,1344,96]{1,2,0:T(8,128)(2,1)}), bf16[8,1344,96]{1,2,0:T(8,128)(2,1)}) %all-gather.6.cloned.1.call-update) | async-done | bytes 2064400 | tf_op jit(solution)/shard_map/all_gather | solution.py:90
  67.8 2.6 convolution_convert_fusion
  70.9 16.8 %all-reduce.1 = bf16[512,96]{0,1:T(8,128)(2,1)S(1)} all-reduce(f32[512,96]{0,1:T(8,128)S(1)} %bitcast.140), channel_id=1, replica_groups=mesh['groups'=2,'seq'=4,'head'=2,'rep'=2] {'head','rep'}, use_global_device_ids=true, to_apply=%region_1.2 | all-reduce | flops 49152 | bytes 294912 | tf_op jit(solution)/shard_map/psum | solution.py:119
  88.2 1.3 copy.113
  90.8 21.5 %all-gather.4.cloned.1.call-done = bf16[512,5376]{0,1:T(8,128)(2,1)} async-done(((bf16[512,1344]{0,1:T(8,128)(2,1)}), bf16[512,5376]{0,1:T(8,128)(2,1)}) %all-gather.4.cloned.1.call-update) | async-done | bytes 5505040 | tf_op jit(solution)/shard_map/all_gather | solution.py:123
  112.4 7.6 %fusion.39 = (f32[512,4]{0,1:T(4,128)S(1)}, bf16[512,512]{0,1:T(8,128)(2,1)S(1)}) fusion(f32[512,512]{0,1:T(8,128)} %copy.113, bf16[512,5376]{0,1:T(8,128)(2,1)} %all-gather.4.cloned.1.call-done, bf16[5376,512]{1,0:T(8,128)(2,1)} %param.18), kind=kOutput, calls=%fused_computation.63 | convolution fusion | flops 2819880960 | bytes 12591104 | tf_op jit(solution)/shard_map/dot_general | solution.py:125
  120.1 5.2 %multiply_reduce_fusion = (f32[512,4]{0,1:T(4,128)S(1)}, f32[512,512]{0,1:T(8,128)S(1)}) fusion(f32[512,512]{0,1:T(8,128)S(1)} %copy.96, bf16[512,5376]{0,1:T(8,128)(2,1)S(1)} %copy-done.7, bf16[5376,512]{1,0:T(8,128)(2,1)} %param.17), kind=kOutput, calls=%fused_computation.69 | convolution fusion | flops 2819356672 | bytes 13115392 | tf_op jit(solution)/shard_map/dot_general | solution.py:124
  125.7 1.1 multiply_subtract_fusion
  126.8 3.0 %fusion.34 = bf16[512,512]{0,1:T(8,128)(2,1)S(1)} fusion(f32[512,512]{0,1:T(8,128)S(1)} %copy.91, bf16[512,5376]{0,1:T(8,128)(2,1)S(1)} %copy-done.7, bf16[5376,512]{1,0:T(8,128)(2,1)S(1)} %bitcast.145), kind=kOutput, calls=%fused_computation.56 | convolution fusion | flops 2819096576 | bytes 12582912 | tf_op jit(solution)/shard_map/dot_general | solution.py:126
  130.2 0.9 pad_maximum_fusion
  131.1 4.3 %collective-permute-start = (bf16[2,512,256]{2,1,0:T(8,128)(2,1)}, bf16[2,512,256]{2,1,0:T(8,128)(2,1)}, u32[]{:S(2)}, u32[]{:S(2)}) collective-permute-start(bf16[2,512,256]{2,1,0:T(8,128)(2,1)} %pad_maximum_fusion), channel_id=1, source_target_pairs={{0,8},{4,12},{1,9},{5,13},{2,10},{6,14},{3,11},{7,15},{16,24},{20,... | collective-permute-start | bytes 1572872 | tf_op jit(solution)/shard_map/ppermute | solution.py:23
  135.5 3.9 %collective-permute-start.1 = (bf16[2,512,256]{2,1,0:T(8,128)(2,1)}, bf16[2,512,256]{2,1,0:T(8,128)(2,1)}, u32[]{:S(2)}, u32[]{:S(2)}) collective-permute-start(bf16[2,512,256]{2,1,0:T(8,128)(2,1)} %pad_maximum_fusion), channel_id=1, source_target_pairs={{0,4},{4,8},{8,12},{1,5},{5,9},{9,13},{2,6},{6,10},{10,14},{3,7},{... | collective-permute-start | bytes 1572872 | tf_op jit(solution)/shard_map/ppermute | solution.py:23
  139.7 1.4 copy.98
  141.1 1.1 fusion.41
  142.3 5.1 %collective-permute-done = bf16[2,512,256]{2,1,0:T(8,128)(2,1)} collective-permute-done((bf16[2,512,256]{2,1,0:T(8,128)(2,1)}, bf16[2,512,256]{2,1,0:T(8,128)(2,1)}, u32[]{:S(2)}, u32[]{:S(2)}) %collective-permute-start) | collective-permute-done | bytes 524320 | tf_op jit(solution)/shard_map/ppermute | solution.py:23
  147.3 10.6 %collective-permute-done.1 = bf16[2,512,256]{2,1,0:T(8,128)(2,1)} collective-permute-done((bf16[2,512,256]{2,1,0:T(8,128)(2,1)}, bf16[2,512,256]{2,1,0:T(8,128)(2,1)}, u32[]{:S(2)}, u32[]{:S(2)}) %collective-permute-start.1) | collective-permute-done | bytes 524320 | tf_op jit(solution)/shard_map/ppermute | solution.py:23
  157.9 1.4 maximum_maximum_fusion
  159.9 29.6 %while.15 = (s32[]{:T(128)}, f32[512,2,2,128]{0,3,2,1:T(8,128)S(1)}, f32[2,2,512]{2,1,0:T(2,128)S(1)}, bf16[3,512,2,128]{3,2,1,0:T(2,128)(2,1)S(1)}, s32[3]{0:T(...) while((s32[]{:T(128)}, ...), condition=%wide.region_8.9_spmd.clone, body=%wide.region_5.8_spmd.clone.sunk | while | flops 543460864 | bytes 13948180 | solution.py:230
  162.3 4.0 %fusion.93 = (f32[2,2,512]{2,1,0:T(2,128)S(1)}, f32[2,512,512,2]{2,1,3,0:T(8,128)}) fusion(pred[512,512]{0,1:T(8,128)(4,1)S(1)} %fusion.92, bf16[512,2,2,128]{3,0,2,1:T(8,128)(2,1)} %get-tuple-element.399, bf16[1,512,2,128]{3,2,1,0:T(2,128)(2,1)S(1)} %get-tuple-element.359), kind=kOutput, calls=%fused_computation.4.clone.1 | convolution fusion | flops 270530560 | bytes 5251072 | tf_op jit(solution)/shard_map/while/body/eval_jaxpr/tcpd,kcd->cptk/dot_general | solution.py:216
  166.5 3.2 %fusion.94 = f32[512,2,2,128]{0,3,2,1:T(8,128)S(1)} fusion(f32[2,512,512,2]{2,1,3,0:T(8,128)} %get-tuple-element.360, pred[512,512]{0,1:T(8,128)(4,1)S(1)} %fusion.92, f32[512,2,2,128]{0,3,2,1:T(8,128)S(1)} %get-tuple-element.378, pred[]{:T(512)S(6)} %compare.16, bf16[1,512,2,128]{1,3,2,0:T(8,128)(2,1)S(1)} %copy.178), kind=kOutput, calls=%fused_computation.12.clone.1 | convolution fusion | flops 271056896 | bytes 6815745 | tf_op jit(solution)/shard_map/while/body/eval_jaxpr/cptk,kcd->tcpd/dot_general | solution.py:222
  172.1 4.1 %fusion.93 = (f32[2,2,512]{2,1,0:T(2,128)S(1)}, f32[2,512,512,2]{2,1,3,0:T(8,128)}) fusion(pred[512,512]{0,1:T(8,128)(4,1)S(1)} %fusion.92, bf16[512,2,2,128]{3,0,2,1:T(8,128)(2,1)} %get-tuple-element.399, bf16[1,512,2,128]{3,2,1,0:T(2,128)(2,1)S(1)} %get-tuple-element.359), kind=kOutput, calls=%fused_computation.4.clone.1 | convolution fusion | flops 270530560 | bytes 5251072 | tf_op jit(solution)/shard_map/while/body/eval_jaxpr/tcpd,kcd->cptk/dot_general | solution.py:216
  176.4 3.2 %fusion.94 = f32[512,2,2,128]{0,3,2,1:T(8,128)S(1)} fusion(f32[2,512,512,2]{2,1,3,0:T(8,128)} %get-tuple-element.360, pred[512,512]{0,1:T(8,128)(4,1)S(1)} %fusion.92, f32[512,2,2,128]{0,3,2,1:T(8,128)S(1)} %get-tuple-element.378, pred[]{:T(512)S(6)} %compare.16, bf16[1,512,2,128]{1,3,2,0:T(8,128)(2,1)S(1)} %copy.178), kind=kOutput, calls=%fused_computation.12.clone.1 | convolution fusion | flops 271056896 | bytes 6815745 | tf_op jit(solution)/shard_map/while/body/eval_jaxpr/cptk,kcd->tcpd/dot_general | solution.py:222
  182.0 4.1 %fusion.93 = (f32[2,2,512]{2,1,0:T(2,128)S(1)}, f32[2,512,512,2]{2,1,3,0:T(8,128)}) fusion(pred[512,512]{0,1:T(8,128)(4,1)S(1)} %fusion.92, bf16[512,2,2,128]{3,0,2,1:T(8,128)(2,1)} %get-tuple-element.399, bf16[1,512,2,128]{3,2,1,0:T(2,128)(2,1)S(1)} %get-tuple-element.359), kind=kOutput, calls=%fused_computation.4.clone.1 | convolution fusion | flops 270530560 | bytes 5251072 | tf_op jit(solution)/shard_map/while/body/eval_jaxpr/tcpd,kcd->cptk/dot_general | solution.py:216
  186.3 3.2 %fusion.94 = f32[512,2,2,128]{0,3,2,1:T(8,128)S(1)} fusion(f32[2,512,512,2]{2,1,3,0:T(8,128)} %get-tuple-element.360, pred[512,512]{0,1:T(8,128)(4,1)S(1)} %fusion.92, f32[512,2,2,128]{0,3,2,1:T(8,128)S(1)} %get-tuple-element.378, pred[]{:T(512)S(6)} %compare.16, bf16[1,512,2,128]{1,3,2,0:T(8,128)(2,1)S(1)} %copy.178), kind=kOutput, calls=%fused_computation.12.clone.1 | convolution fusion | flops 271056896 | bytes 6815745 | tf_op jit(solution)/shard_map/while/body/eval_jaxpr/cptk,kcd->tcpd/dot_general | solution.py:222
  189.6 0.9 divide_convert_fusion
  190.5 26.5 %all_gather.26 = bf16[8,512,32]{1,2,0:T(8,128)(2,1)S(1)} all-gather(bf16[2,512,32]{1,2,0:T(8,128)(2,1)S(1)} %copy-done.3), channel_id=1, replica_groups=mesh['groups'=2,'seq'=4,'head'=2,'rep'=2] {'seq'}, dimensions={0}, use_global_device_ids=true | all-gather | bytes 327680 | tf_op jit(solution)/shard_map/all_gather | solution.py:93
  217.3 16.2 %all_gather.27 = bf16[8,32,1344]{2,1,0:T(8,128)(2,1)S(1)} all-gather(bf16[2,32,1344]{2,1,0:T(8,128)(2,1)} %param.27), channel_id=1, replica_groups=mesh['groups'=2,'seq'=4,'head'=2,'rep'=2] {'seq'}, dimensions={0}, use_global_device_ids=true | all-gather | bytes 860160 | tf_op jit(solution)/shard_map/all_gather | solution.py:94
  234.3 10.7 %psum.15 = bf16[512,32]{0,1:T(8,128)(2,1)S(1)} all-reduce(f32[512,32]{0,1:T(8,128)S(1)} %bitcast.142), channel_id=1, replica_groups=mesh['groups'=2,'seq'=4,'head'=2,'rep'=2] {'head','rep'}, use_global_device_ids=true, to_apply=%region_9.10 | all-reduce | flops 16384 | bytes 98304 | tf_op jit(solution)/shard_map/psum | solution.py:255
  245.7 7.3 %fusion.27 = bf16[512,1344]{0,1:T(8,128)(2,1)} fusion(bf16[2048,1344]{0,1:T(8,128)(2,1)} %param.20, bf16[512,2048]{0,1:T(8,128)(2,1)} %all-gather.8.cloned.1.call-done, f32[4,168,8,128]{3,2,1,0:T(8,128)S(1)} %fusion.29), kind=kOutput, calls=%fused_computation.38 | convolution fusion | flops 2819948544 | bytes 11730944 | tf_op jit(solution)/shard_map/dot_general | solution.py:243
  (96 shorter events, 15.7 us)
Async XLA Ops:
  6.5 61.3 %all-gather.6.cloned.1.call-start = ((), (), s32[]{:S(2)}) async-start(), calls=%async_computation.1 | async-start | bytes 2703360 | tf_op jit(solution)/shard_map/all_gather | solution.py:90
  7.3 105.1 %all-gather.4.cloned.1.call-start = ((), (), s32[]{:S(2)}) async-start(), calls=%async_computation | async-start | bytes 6881280 | tf_op jit(solution)/shard_map/all_gather | solution.py:123
  8.0 62.4 %copy-start.2 = (bf16[512,1344]{0,1:T(8,128)(2,1)S(1)}, bf16[512,1344]{0,1:T(8,128)(2,1)}, u32[]{:S(2)}) copy-start(bf16[512,1344]{0,1:T(8,128)(2,1)} %param.16) | copy-start | bytes 4128772
  8.0 237.7 %all-gather.8.cloned.1.call-start = ((), (), s32[]{:S(2)}) async-start(), calls=%async_computation.2 | async-start | bytes 2621440 | tf_op jit(solution)/shard_map/all_gather | solution.py:244
  112.4 7.7 %copy-start.7 = (bf16[512,5376]{0,1:T(8,128)(2,1)S(1)}, bf16[512,5376]{0,1:T(8,128)(2,1)}, u32[]{:S(2)}) copy-start(bf16[512,5376]{0,1:T(8,128)(2,1)} %all-gather.4.cloned.1.call-done) | copy-start | bytes 16515076
  112.4 14.5 %slice-start = ((s8[5505024]{0:T(1024)(128)(4,1)}), s8[4194304]{0:T(1024)(128)(4,1)S(1)}, s32[]{:S(2)}) async-start(s8[5505024]{0:T(1024)(128)(4,1)} %bitcast.144), calls=%async_computation.3 | async-start | bytes 8388608
  120.0 5.3 %copy-start.5 = (f32[128]{0:T(128)S(1)}, f32[128]{0:T(128)}, u32[]{:S(2)}) copy-start(f32[128]{0:T(128)} %param.22) | copy-start | bytes 1540
  120.0 5.5 %copy-start.6 = (f32[128]{0:T(128)S(1)}, f32[128]{0:T(128)}, u32[]{:S(2)}) copy-start(f32[128]{0:T(128)} %param.21) | copy-start | bytes 1540
  120.0 6.8 %slice-start.1 = ((s8[5505024]{0:T(1024)(128)(4,1)}), s8[1310720]{0:T(1024)(128)(4,1)S(1)}, s32[]{:S(2)}) async-start(s8[5505024]{0:T(1024)(128)(4,1)} %bitcast.144), calls=%async_computation.4 | async-start | bytes 2621440
  130.2 5.3 %copy-start.1 = (bf16[1,512,256]{2,1,0:T(8,128)(2,1)}, bf16[1,512,256]{2,1,0:T(8,128)(2,1)S(1)}, u32[]{:S(2)}) copy-start(bf16[1,512,256]{2,1,0:T(8,128)(2,1)S(1)} %copy.115) | copy-start | bytes 786436
  131.1 16.2 %collective-permute-start = (bf16[2,512,256]{2,1,0:T(8,128)(2,1)}, bf16[2,512,256]{2,1,0:T(8,128)(2,1)}, u32[]{:S(2)}, u32[]{:S(2)}) collective-permute-start(bf16[2,512,256]{2,1,0:T(8,128)(2,1)} %pad_maximum_fusion), channel_id=1, source_target_pairs={{0,8},{4,12},{1,9},{5,13},{2,10},{6,14},{3,11},{7,15},{16,24},{20,... | collective-permute-start | bytes 1572872 | tf_op jit(solution)/shard_map/ppermute | solution.py:23
  135.5 22.4 %collective-permute-start.1 = (bf16[2,512,256]{2,1,0:T(8,128)(2,1)}, bf16[2,512,256]{2,1,0:T(8,128)(2,1)}, u32[]{:S(2)}, u32[]{:S(2)}) collective-permute-start(bf16[2,512,256]{2,1,0:T(8,128)(2,1)} %pad_maximum_fusion), channel_id=1, source_target_pairs={{0,4},{4,8},{8,12},{1,5},{5,9},{9,13},{2,6},{6,10},{10,14},{3,7},{... | collective-permute-start | bytes 1572872 | tf_op jit(solution)/shard_map/ppermute | solution.py:23
  159.3 0.7 copy-start.4
  159.9 30.6 %copy-start.3 = (bf16[2,512,32]{1,2,0:T(8,128)(2,1)S(1)}, bf16[2,512,32]{1,2,0:T(8,128)(2,1)}, u32[]{:S(2)}) copy-start(bf16[2,512,32]{1,2,0:T(8,128)(2,1)} %param.26) | copy-start | bytes 196612
  190.5 43.5 %copy-start = (bf16[512,2,2,128]{0,3,2,1:T(8,128)(2,1)S(1)}, bf16[512,2,2,128]{0,3,2,1:T(8,128)(2,1)}, u32[]{:S(2)}) copy-start(bf16[512,2,2,128]{0,3,2,1:T(8,128)(2,1)} %divide_convert_fusion) | copy-start | bytes 1572868
Sparse Core Ops, SparseCore 0:
  8.9 58.8 all-gather.5
  69.4 42.9 all-gather.3
  190.6 33.6 all-gather.7
where the time goes:
time: 260 us
  blocking collectives  111 us (43%)
  waiting for transfers between devices  54.1 us (21%)
  matrix products  51.5 us (20%)
  between operations  13.5 us (5%)
  other arithmetic  9.9 us (4%)
  local copies, waits for them, and re-layouts  9.48 us (4%)
  starting transfers between devices  8.35 us (3%)
    all_gather x1, blocking collectives, per_device(): lax.all_gather(adapter_out_down, 'seq', axis=0, tiled=True)  26.5 us
    all_gather x1, blocking collectives, per_device(): lax.all_gather(key_value_up_panels, 'seq', axis=0, tiled=True)  23.4 us
    all_gather x1, waiting for transfers between devices, per_device(): feature_part = lax.all_gather(tokens, ('head', 'rep'), axis=1, tiled=True)  21.5 us
    all_gather x1, blocking collectives, per_device(): lax.all_gather(adapter_up_query, 'seq', axis=0, tiled=True)  16.8 us
    psum x1, blocking collectives, per_device(): lax.psum(partial_low, ('head', 'rep')).astype(jnp.bfloat16)  16.8 us
    all_gather x1, blocking collectives, per_device(): lax.all_gather(adapter_out_up, 'seq', axis=0, tiled=True)  16.2 us
    ppermute x2, waiting for transfers between devices, shifted(): return lax.ppermute(value, axis, pairs)  15.6 us
    all_gather x1, waiting for transfers between devices, per_device(): lax.all_gather(adapter_down, 'seq', axis=0, tiled=True)  15.6 us
  transfers between devices with their start and end apart: 5, of which 4 were waited for; matrix products, arithmetic and copies ran while one was open for 6% of the time, Pallas kernels for 0%

commit v1 on v0

--- a/solution.py
+++ b/solution.py
@@ -3,6 +3,8 @@
 import jax
 import jax.numpy as jnp
 from jax import lax
+from jax.experimental import pallas as pl
+from jax.experimental.pallas import tpu as pltpu
 from jax.sharding import PartitionSpec as P
 
 HEAD_SIZE = 128
@@ -55,7 +57,7 @@
     return jnp.sum(earlier, axis=1) * BLOCK
 
 
-def per_device(
+def per_device_general(
     tokens,
     query_matrix,
     key_matrix,
@@ -262,9 +264,526 @@
     return result.astype(jnp.bfloat16)
 
 
+F32 = jnp.float32
+BF16 = jnp.bfloat16
+VMEM_SMALL = 16 * 1024 * 1024
+VMEM_LARGE = 56 * 1024 * 1024
+SWAP = [(0, 1), (1, 0)]
+SHARD_BLOCKS = 4
+CHUNK = 256
+CHUNK_BLOCKS = CHUNK // BLOCK
+META_ADAPTER = 3
+META_REQUEST = 5
+
+
+def dot(a, b):
+    return lax.dot_general(a, b, (((1,), (0,)), ((), ())), preferred_element_type=F32)
+
+
+def dot_t(a, b):
+    return lax.dot_general(a, b, (((0,), (0,)), ((), ())), preferred_element_type=F32)
+
+
+VM = pl.BlockSpec(memory_space=pltpu.VMEM)
+SM = pl.BlockSpec(memory_space=pltpu.SMEM)
+HB = pl.BlockSpec(memory_space=pl.ANY)
+FAR = pl.BlockSpec(memory_space=pltpu.HBM)
+
+
+def shape(dims, dtype=BF16):
+    return jax.ShapeDtypeStruct(dims, dtype)
+
+
+def call(kernel, name, out_shape, in_specs, args, scratch=(), out_specs=None, grid=None, after=()):
+    count = len(in_specs)
+
+    def body(*refs):
+        kernel(*refs[:count], *refs[count + len(after) :])
+
+    outs = out_specs
+    if outs is None:
+        outs = VM if isinstance(out_shape, jax.ShapeDtypeStruct) else tuple(VM for _ in out_shape)
+    more = dict(grid=grid) if grid else {}
+    return pl.pallas_call(
+        body,
+        out_shape=out_shape,
+        in_specs=list(in_specs) + [HB] * len(after),
+        out_specs=outs,
+        scratch_shapes=list(scratch),
+        compiler_params=pltpu.CompilerParams(vmem_limit_bytes=VMEM_LARGE if FAR in in_specs else VMEM_SMALL),
+        cost_estimate=pl.CostEstimate(flops=1000, bytes_accessed=1000, transcendentals=0),
+        name=name,
+        **more,
+    )(*args, *after)
+
+
+def split_kernel(tokens, *chunks):
+    for c, chunk in enumerate(chunks):
+        chunk[...] = tokens[:, c * CHUNK : (c + 1) * CHUNK]
+
+
+def picked(meta, held, quarter):
+    request = lax.div(quarter, 2)
+    slot = meta[META_ADAPTER + request] - meta[0] * held
+    here = jnp.logical_and(slot >= 0, slot < held)
+    keep = jnp.where(here, 1.0, 0.0).astype(F32)
+    return jnp.clip(slot, 0, held - 1), keep, lax.rem(quarter, 2)
+
+
+def pack_kernel(meta, down_far, up_q_far, up_kv_far, *refs):
+    quarters, (down, up_q, up_kv, sems) = refs[:4], refs[4:]
+    copies = [
+        pltpu.make_async_copy(a, b, sems.at[i])
+        for i, (a, b) in enumerate(((down_far, down), (up_q_far, up_q), (up_kv_far, up_kv)))
+    ]
+    for copy in copies:
+        copy.start()
+    for copy in copies:
+        copy.wait()
+    half = up_kv.shape[3] // 2
+    cols = up_q.shape[2]
+    width = down.shape[2]
+    for step, out in enumerate(quarters):
+        slot, keep, part = picked(meta, down.shape[0], jnp.bitwise_xor(meta[0], step))
+        rows = pl.ds(pl.multiple_of(part * 48, 16), 48)
+        ranks = pl.ds(pl.multiple_of(part * 16, 16), 16)
+        out[0:48, :] = (down[slot, rows, :].astype(F32) * keep).astype(BF16)
+        out[48:64, 0:cols] = (up_q[slot, ranks, :].astype(F32) * keep).astype(BF16)
+        for which in range(2):
+            both = up_kv[slot, which, ranks, :].astype(F32) * keep
+            mine = jnp.where(meta[1] == 0, both[:, :half], both[:, half:])
+            out[48:64, cols + which * half : cols + (which + 1) * half] = mine.astype(BF16)
+        out[48:64, 1024:width] = jnp.zeros((16, width - 1024), BF16)
+
+
+def pack_out_kernel(meta, down, up, *quarters):
+    width = up.shape[2]
+    for step, out in enumerate(quarters):
+        slot, keep, part = picked(meta, down.shape[0], jnp.bitwise_xor(meta[0], step))
+        ranks = pl.ds(pl.multiple_of(part * 16, 16), 16)
+        out[:, 0:width] = (up[slot, ranks, :].astype(F32) * keep).astype(BF16)
+        out[:, width:1408] = jnp.zeros((16, 1408 - width), BF16)
+        out[:, 1408:1920] = (down[slot, ranks, :].astype(F32) * keep).astype(BF16)
+
+
+def sum_kernel(a, b, c, d, out):
+    out[...] = a[...] + b[...] + c[...] + d[...]
+
+
+def place_quarters(meta, quarters, panel):
+    me = meta[0]
+    low_side = me < 2
+    at = (me, jnp.bitwise_xor(me, 1), jnp.where(low_side, 2, 1), jnp.where(low_side, 3, 0))
+    for index, quarter in zip(at, quarters):
+        panel[index] = quarter[...]
+
+
+def low_kernel(meta, tok0, tok1, p0, p1, p2, p3, low_t, ups, panel):
+    place_quarters(meta, (p0, p1, p2, p3), panel)
+    down = jnp.concatenate([panel[j, 0:48, :] for j in range(4)], axis=0)
+    both = jnp.concatenate([dot(down, tok0[...]), dot(down, tok1[...])], axis=1)
+    for b in range(SHARD_BLOCKS):
+        request = meta[META_REQUEST + meta[0] * SHARD_BLOCKS + b]
+        at = slice(b * BLOCK, (b + 1) * BLOCK)
+        fa = jnp.where(request == 0, 1.0, 0.0).astype(F32)
+        low_t[:, at] = both[0:96, at] * fa + both[96:192, at] * (1.0 - fa)
+    ups[...] = jnp.concatenate([panel[j, 48:64, 0:1024] for j in range(4)], axis=0)
+
+
+def weight_copies(meta, weights, buffers, sems, chip, width):
+    half = weights[0].shape[1] // 2
+    lane = pl.ds(pl.multiple_of(meta[1] * half, BLOCK), half)
+    copies = []
+    for i, (w, buf) in enumerate(zip(weights, buffers)):
+        lanes = lane if i < 2 else slice(None)
+        pair = []
+        for n, part in enumerate((chip + meta[1], chip + 1 - meta[1])):
+            rows = pl.ds(pl.multiple_of(part * width, 16), width)
+            pair.append(pltpu.make_async_copy(w.at[rows, lanes], buf.at[n], sems.at[i, n]))
+        copies.append(pair)
+    for pair in copies:
+        for copy in pair:
+            copy.start()
+    return copies
+
+
+WEIGHT_AT = (slice(0, 256), slice(256, 512), slice(512, 1024))
+
+
+def near_kernel(meta, own0, own1, other, wq, wk, wv, *refs):
+    outs, buffers, sems = refs[:-4], refs[-4:-1], refs[-1]
+    copies = weight_copies(meta, (wk, wv, wq), buffers, sems, meta[2] * 2, other.shape[0])
+    for at, pair, buf in zip(WEIGHT_AT, copies, buffers):
+        pair[0].wait()
+        pair[1].wait()
+        for c, out in enumerate(outs):
+            tok = slice(c * CHUNK, (c + 1) * CHUNK)
+            out[:, at] = dot_t((own0, own1)[c][...], buf[0]) + dot_t(other[:, tok], buf[1])
+
+
+def far_kernel(meta, part, own, other, wq, wk, wv, q_out, kv_out, *refs):
+    buffers, sems = refs[:-1], refs[-1]
+    copies = weight_copies(meta, (wk, wv, wq), buffers, sems, (1 - meta[2]) * 2, own.shape[0])
+    for i, (at, pair, buf) in enumerate(zip(WEIGHT_AT, copies, buffers)):
+        pair[0].wait()
+        pair[1].wait()
+        turned = jnp.transpose(part[:, at] + dot_t(own[...], buf[0]) + dot_t(other[...], buf[1]))
+        if i == 2:
+            q_out[...] = turned
+        else:
+            kv_out[at, :] = turned.astype(BF16)
+
+
+def block_request(meta, block):
+    return meta[META_REQUEST + jnp.maximum(block, 0)]
+
+
+def by_request(meta, low, first_block):
+    flags = []
+    for b in range(SHARD_BLOCKS):
+        request = block_request(meta, first_block + b)
+        flags.append(jnp.full((1, BLOCK), jnp.where(request == 0, 1.0, 0.0).astype(F32)))
+    flag = jnp.concatenate(flags, axis=1)
+    rows = low.astype(BF16).astype(F32)
+    return jnp.concatenate([rows * flag, rows * (1.0 - flag)], axis=0).astype(BF16)
+
+
+def norm_rotate(x, gain, cosine, sine):
+    mean_square = jnp.mean(x * x, axis=0, keepdims=True)
+    u = x * lax.rsqrt(mean_square + norm_epsilon) * gain
+    a = u[0:64]
+    b = u[64:128]
+    return jnp.concatenate([a * cosine - b * sine, b * cosine + a * sine], axis=0)
+
+
+def finish_keys(meta, chunks, low_k, low_v, ups, gain, cosine, sine, keys, values, first):
+    base = (meta[0] - 2) * SHARD_BLOCKS + first
+    k_term = dot_t(ups[:, 512:768], by_request(meta, low_k, base))
+    v_term = dot_t(ups[:, 768:1024], by_request(meta, low_v, base))
+    for b in range(SHARD_BLOCKS):
+        at = slice((first + b) * BLOCK, (first + b + 1) * BLOCK)
+        here = slice(b * BLOCK, (b + 1) * BLOCK)
+        chunk = chunks[b // CHUNK_BLOCKS]
+        lanes = slice(b % CHUNK_BLOCKS * BLOCK, (b % CHUNK_BLOCKS + 1) * BLOCK)
+        for g in range(2):
+            head = slice(g * HEAD_SIZE, (g + 1) * HEAD_SIZE)
+            k = chunk[head, lanes].astype(F32) + adapter_scale * k_term[head, here]
+            k = k.astype(BF16).astype(F32)
+            turned = norm_rotate(k, gain, cosine[:, at], sine[:, at])
+            keys[at, head] = jnp.transpose(turned).astype(BF16)
+        values[:, at] = (chunk[256:512, lanes].astype(F32) + adapter_scale * v_term[:, here]).astype(BF16)
+
+
+def attend(meta, q, keys, values, c, g, low_block, high_block):
+    base = (meta[0] - 2) * SHARD_BLOCKS
+    mine = block_request(meta, base + 8 + c)
+    head = slice(g * HEAD_SIZE, (g + 1) * HEAD_SIZE)
+    at = slice(low_block * BLOCK, (high_block + 1) * BLOCK)
+    scores = dot(keys[at, head], q)
+    key = lax.broadcasted_iota(jnp.int32, (BLOCK, 2 * BLOCK), 0)
+    query = jnp.bitwise_and(lax.broadcasted_iota(jnp.int32, (BLOCK, 2 * BLOCK), 1), BLOCK - 1)
+    den = jnp.zeros((BLOCK, 2 * BLOCK), F32)
+    pieces = []
+    for j in range(low_block, high_block + 1):
+        block = base + j
+        ok = jnp.logical_and(block >= 0, block_request(meta, block) == mine)
+        piece = jnp.exp(scores[(j - low_block) * BLOCK : (j - low_block + 1) * BLOCK])
+        piece = piece * jnp.where(ok, 1.0, 0.0).astype(F32)
+        if j == c + 8:
+            piece = jnp.where(query >= key, piece, 0.0)
+        if j == c:
+            piece = jnp.where(query < key, piece, 0.0)
+        den = den + piece
+        pieces.append(piece.astype(BF16))
+    num = dot(values[head, at], jnp.concatenate(pieces, axis=0))
+    return num, jnp.sum(den, axis=0, keepdims=True)
+
+
+def attend_near_kernel(
+    meta, q0, q1, o0, o1, h0, h1, low, low_h, ups, q_gain, k_gain, cosine, sine,
+    q_rot, num_out, den_out, keys, values,
+):
+    gain = k_gain[...]
+    finish_keys(meta, (o0, o1), low[32:64, :], low[64:96, :], ups, gain, cosine, sine, keys, values, 8)
+    finish_keys(meta, (h0, h1), low_h[0:32, :], low_h[32:64, :], ups, gain, cosine, sine, keys, values, 4)
+    q_term = dot_t(ups[:, 0:512], by_request(meta, low[0:32, :], meta[0] * SHARD_BLOCKS))
+    for c in range(SHARD_BLOCKS):
+        q = (q0, q1)[c // CHUNK_BLOCKS]
+        lanes = slice(c % CHUNK_BLOCKS * BLOCK, (c % CHUNK_BLOCKS + 1) * BLOCK)
+        rows = slice(c * BLOCK, (c + 1) * BLOCK)
+        at = slice((8 + c) * BLOCK, (9 + c) * BLOCK)
+        for h in range(4):
+            head = slice(h * HEAD_SIZE, (h + 1) * HEAD_SIZE)
+            x = q[head, lanes] + adapter_scale * q_term[head, rows]
+            q_rot[head, rows] = (norm_rotate(x, q_gain[...], cosine[:, at], sine[:, at]) * score_scale).astype(BF16)
+    for g in range(2):
+        for c in range(SHARD_BLOCKS):
+            rows = slice(c * BLOCK, (c + 1) * BLOCK)
+            heads = [slice((2 * g + h) * HEAD_SIZE, (2 * g + h + 1) * HEAD_SIZE) for h in range(2)]
+            q = jnp.concatenate([q_rot[head, rows] for head in heads], axis=1)
+            num, den = attend(meta, q, keys, values, c, g, max(4, c + 1), c + 8)
+            for h in range(2):
+                part = slice(h * BLOCK, (h + 1) * BLOCK)
+                num_out[heads[h], rows] = num[:, part]
+                den_out[2 * g + h : 2 * g + h + 1, rows] = den[:, part]
+
+
+def attend_far_kernel(
+    meta, q_rot, num_in, den_in, h0, h1, low_h, ups, k_gain, cosine, sine, p0, p1, p2, p3, out, keys, values, panel
+):
+    place_quarters(meta, (p0, p1, p2, p3), panel)
+    cols = q_rot.shape[0]
+    out[cols : cols + 64, :] = jnp.concatenate([panel[j, :, 1408:1920] for j in range(4)], axis=0)
+    finish_keys(
+        meta, (h0, h1), low_h[0:32, :], low_h[32:64, :], ups, k_gain[...], cosine, sine, keys, values, 0
+    )
+    for g in range(2):
+        for c in range(SHARD_BLOCKS):
+            rows = slice(c * BLOCK, (c + 1) * BLOCK)
+            heads = [slice((2 * g + h) * HEAD_SIZE, (2 * g + h + 1) * HEAD_SIZE) for h in range(2)]
+            q = jnp.concatenate([q_rot[head, rows] for head in heads], axis=1)
+            num, den = attend(meta, q, keys, values, c, g, c, 3)
+            for h in range(2):
+                part = slice(h * BLOCK, (h + 1) * BLOCK)
+                total = den_in[2 * g + h : 2 * g + h + 1, rows] + den[:, part]
+                out[heads[h], rows] = ((num_in[heads[h], rows] + num[:, part]) / total).astype(BF16)
+
+
+def out_copies(meta, w, buf, sems, chip, depth):
+    rows = w.shape[0] // 2
+    copies = []
+    for half in range(2):
+        at = slice(half * rows, (half + 1) * rows)
+        pair = []
+        for n, p in enumerate((chip + meta[1], chip + 1 - meta[1])):
+            lanes = pl.ds(pl.multiple_of(p * depth, BLOCK), depth)
+            pair.append(pltpu.make_async_copy(w.at[at, lanes], buf.at[n, at, :], sems.at[half, n]))
+            pair[-1].start()
+        copies.append((at, pair))
+    return copies
+
+
+def out_near_kernel(meta, own, other, w, part, low, buf, sems):
+    cols = own.shape[1]
+    copies = out_copies(meta, w, buf, sems, meta[2] * 2, cols)
+    mine = own[0:cols, :]
+    theirs = other[0:cols, :]
+    low[...] = dot(own[cols : cols + 64, :], mine) + dot(other[cols : cols + 64, :], theirs)
+    for at, pair in copies:
+        pair[0].wait()
+        pair[1].wait()
+        part[at, :] = dot(buf[0, at, :], mine) + dot(buf[1, at, :], theirs)
+
+
+def out_far_kernel(meta, own, other, w, part, low, p0, p1, p2, p3, out, panel, buf, sems):
+    copies = out_copies(meta, w, buf, sems, (1 - meta[2]) * 2, own.shape[1])
+    place_quarters(meta, (p0, p1, p2, p3), panel)
+    cols = own.shape[1]
+    mine = own[0:cols, :]
+    theirs = other[0:cols, :]
+    lows = low[...] + dot(own[cols : cols + 64, :], mine) + dot(other[cols : cols + 64, :], theirs)
+    lows = lows.astype(BF16).astype(F32)
+    flags = []
+    for b in range(SHARD_BLOCKS):
+        request = block_request(meta, meta[0] * SHARD_BLOCKS + b)
+        flags.append(jnp.full((1, BLOCK), jnp.where(request == 0, 1.0, 0.0).astype(F32)))
+    flag = jnp.concatenate(flags, axis=1)
+    chosen = jnp.concatenate([lows[0:32] * flag, lows[32:64] * (1.0 - flag)], axis=0).astype(BF16)
+    up = jnp.concatenate([panel[j, :, 0 : w.shape[0]] for j in range(4)], axis=0)
+    for at, pair in copies:
+        total = part[at, :] + adapter_scale * dot_t(up[:, at], chosen)
+        pair[0].wait()
+        pair[1].wait()
+        out[at, :] = (total + dot(buf[0, at, :], mine) + dot(buf[1, at, :], theirs)).astype(BF16)
+
+
+def exchange_quarters(quarters):
+    return [quarters[0]] + [lax.ppermute(quarters[s], "seq", [(j, j ^ s) for j in range(4)]) for s in (1, 2, 3)]
+
+
+def share_quarter(total):
+    pairs = ([(0, 1), (1, 0), (2, 3), (3, 2)], [(1, 2), (2, 1)], [(0, 2), (3, 1)])
+    return [total] + [lax.ppermute(total, "seq", pair) for pair in pairs]
+
+
+def per_device(
+    tokens,
+    query_matrix,
+    key_matrix,
+    value_matrix,
+    output_matrix,
+    query_gain,
+    key_norm_gain,
+    adapter_down,
+    adapter_up_query,
+    key_value_up_panels,
+    adapter_out_down,
+    adapter_out_up,
+    request_of_block,
+    adapter_of_request,
+):
+    rows, width = tokens.shape
+    cols = query_matrix.shape[1]
+    seq, rep, head = (lax.axis_index(name).astype(jnp.int32) for name in ("seq", "rep", "head"))
+    meta = jnp.concatenate([jnp.stack([seq, rep, head]), adapter_of_request, request_of_block])
+    tokens = tokens.T
+
+    def across(value):
+        return lax.ppermute(value, "head", SWAP)
+
+    def core(value):
+        return lax.ppermute(value, "rep", SWAP)
+
+    def up(value, by=1):
+        return lax.ppermute(value, "seq", [(i, (i + by) % 4) for i in range(4)])
+
+    def after(value, *others):
+        return lax.optimization_barrier((value, *others))[0]
+
+    down_pool = jnp.swapaxes(adapter_down, 1, 2)
+    quarters = call(
+        pack_kernel,
+        "pack",
+        (shape((64, width)),) * 4,
+        [SM, FAR, FAR, FAR],
+        [meta, down_pool, adapter_up_query, key_value_up_panels],
+        [pltpu.VMEM(a.shape, BF16) for a in (down_pool, adapter_up_query, key_value_up_panels)]
+        + [pltpu.SemaphoreType.DMA((3,))],
+    )
+    received = exchange_quarters(quarters)
+
+    chunks = rows // CHUNK
+    token_chunks = call(
+        split_kernel, "split", (shape((width, CHUNK)),) * chunks, [VM], [tokens], after=[quarters[0]]
+    )
+    far_own = [across(chunk) for chunk in token_chunks]
+    near_other = core(tokens)
+
+    weights = [query_matrix, key_matrix, value_matrix]
+    weight_scratch = [
+        pltpu.VMEM((2, width, 256), BF16),
+        pltpu.VMEM((2, width, 256), BF16),
+        pltpu.VMEM((2, width, cols), BF16),
+        pltpu.SemaphoreType.DMA((3, 2)),
+    ]
+    near = call(
+        near_kernel,
+        "near",
+        (shape((CHUNK, 1024), F32),) * chunks,
+        [SM, VM, VM, VM, FAR, FAR, FAR],
+        [meta, *token_chunks, near_other, *weights],
+        weight_scratch,
+        after=[quarters[0]],
+    )
+
+    def project(c, prior):
+        return call(
+            far_kernel,
+            "far",
+            (shape((cols, CHUNK), F32), shape((512, CHUNK))),
+            [SM, VM, VM, VM, FAR, FAR, FAR],
+            [meta, near[c], far_own[c], core(after(far_own[c], prior)), *weights],
+            weight_scratch,
+            after=[prior],
+        )
+
+    quarter = call(sum_kernel, "sum", shape((64, width)), [VM] * 4, received, after=[near[0]])
+    pieces = share_quarter(quarter)
+
+    first_q, first_kv = project(0, quarter)
+
+    all_blocks = request_of_block.shape[0]
+    window = jnp.arange(3 * rows, dtype=jnp.int32) + (seq - 2) * rows
+    window = jnp.clip(window, 0, all_blocks * BLOCK - 1)
+    second_start = jnp.sum((request_of_block < 1).astype(jnp.int32)) * BLOCK
+    position = jnp.where(window >= second_start, window - second_start, window)
+    half_dim = HEAD_SIZE // 2
+    frequency = jnp.power(rope_base, -jnp.arange(half_dim, dtype=F32) * 2.0 / HEAD_SIZE)
+    angles = frequency[:, None] * position.astype(F32)[None, :]
+    cosine, sine = jnp.cos(angles), jnp.sin(angles)
+    q_gain = query_gain.reshape(HEAD_SIZE, 1)
+    k_gain = key_norm_gain.reshape(HEAD_SIZE, 1)
+
+    out_quarters = call(
+        pack_out_kernel,
+        "pack_out",
+        (shape((16, 1920)),) * 4,
+        [SM, VM, VM],
+        [meta, jnp.swapaxes(adapter_out_down, 1, 2), adapter_out_up],
+        after=[first_kv],
+    )
+    out_received = exchange_quarters(out_quarters)
+
+    partial_low, ups = call(
+        low_kernel,
+        "low",
+        (shape((96, rows), F32), shape((64, 1024))),
+        [SM] + [VM] * 6,
+        [meta, *token_chunks, *pieces],
+        [pltpu.VMEM((4, 64, width), BF16)],
+        after=[first_kv],
+    )
+    chip_low = partial_low + core(partial_low)
+    low = chip_low + across(chip_low)
+    second_q, second_kv = project(1, chip_low)
+    own_kv = [first_kv, second_kv]
+    kv_prev = [up(kv) for kv in own_kv]
+    kv_prev2 = [up(after(kv_prev[0], chip_low)), up(kv_prev[1])]
+    low_kv = low[32:96].astype(BF16)
+    low_prev = up(low_kv)
+    low_prev2 = up(low_kv, 2)
+
+    out_quarter = call(sum_kernel, "out_sum", shape((16, 1920)), [VM] * 4, out_received, after=[second_kv])
+    out_pieces = share_quarter(out_quarter)
+
+    window_scratch = [pltpu.VMEM((3 * rows, 256), BF16), pltpu.VMEM((256, 3 * rows), BF16)]
+    q_rot, num, den = call(
+        attend_near_kernel,
+        "attend_near",
+        (shape((cols, rows)), shape((cols, rows), F32), shape((8, rows), F32)),
+        [SM] + [VM] * 13,
+        [meta, first_q, second_q, *own_kv, *kv_prev, low, low_prev, ups, q_gain, k_gain, cosine, sine],
+        window_scratch,
+    )
+    attended = call(
+        attend_far_kernel,
+        "attend_far",
+        shape((cols + 64, rows)),
+        [SM] + [VM] * 14,
+        [meta, q_rot, num, den, *kv_prev2, low_prev2, ups, k_gain, cosine, sine, *out_pieces],
+        window_scratch + [pltpu.VMEM((4, 16, 1920), BF16)],
+    )
+
+    att_far = across(attended)
+    att_core = core(attended)
+    att_far_core = core(att_far)
+    out_weights = output_matrix.T
+    out_scratch = [pltpu.VMEM((2, width, cols), BF16), pltpu.SemaphoreType.DMA((2, 2))]
+    out_part, out_low = call(
+        out_near_kernel,
+        "out_near",
+        (shape((width, rows), F32), shape((64, rows), F32)),
+        [SM, VM, VM, FAR],
+        [meta, attended, att_core, out_weights],
+        out_scratch,
+    )
+    return call(
+        out_far_kernel,
+        "out_far",
+        shape((width, rows)),
+        [SM, VM, VM, FAR] + [VM] * 6,
+        [meta, att_far, att_far_core, out_weights, out_part, out_low, *out_pieces],
+        [pltpu.VMEM((4, 16, 1920), BF16)] + out_scratch,
+    ).T
+
+
+def plain_sizes(mesh):
+    return mesh.shape["seq"] == 4 and mesh.shape["head"] == 2 and mesh.shape["rep"] == 2
+
+
 def solution(mesh):
     return jax.shard_map(
-        per_device,
+        per_device if plain_sizes(mesh) else per_device_general,
         mesh=mesh,
         in_specs=(
             P(("groups", "seq"), ("head", "rep")),

time: 260 us -> 129 us (0.50)
  blocking collectives: 111 us -> 0 us
  matrix products: 51.5 us -> 0 us
  Pallas kernels: 0 us -> 48.6 us
  waiting for transfers between devices: 54.1 us -> 28.6 us
  starting transfers between devices: 8.35 us -> 32.5 us
  between operations: 13.5 us -> 1.38 us
  other arithmetic: 9.9 us -> 3.06 us
  local copies, waits for them, and re-layouts: 9.48 us -> 14.2 us
    all_gather x4 -> x0, blocking collectives: 83 us -> none  [the longest x1 26.5 us: per_device(): lax.all_gather(adapter_out_down, 'seq', axis=0, tiled=True)]
    dot_general x21 -> x0, matrix products: 51.5 us -> none  [the longest x3 12.1 us: one_step(): jnp.einsum('tcpd,kcd->cptk', query_groups, step_keys, preferred_element_t...]
    pallas_call x0 -> x13, Pallas kernels: none -> 48.6 us  [call(): pl.pallas_call(body, out_shape=out_shape, in_specs=list(in_specs) + [HB]...]
    all_gather x3 -> x0, waiting for transfers between devices: 37.1 us -> none  [the longest x1 21.5 us: per_device(): feature_part = lax.all_gather(tokens, ('head', 'rep'), axis=1, tiled=True)]
    psum x2 -> x0, blocking collectives: 27.5 us -> none  [the longest x1 16.8 us: per_device(): lax.psum(partial_low, ('head', 'rep')).astype(jnp.bfloat16)]
    ppermute x2 -> x28, starting transfers between devices: 8.27 us -> 32.5 us  [the longest x6 10.7 us: share_quarter(): return [total] + [lax.ppermute(total, 'seq', pair) for pair in pairs]]
    ppermute x2 -> x28, waiting for transfers between devices: 15.6 us -> 28.6 us  [the longest x6 9.33 us: exchange_quarters(): lax.ppermute(quarters[s], 'seq', [(j, j ^ s) for j in range(4)])]
    unnamed x20 -> x66, local copies, waits for them, and re-layouts: 0.2 us -> 12.6 us
  transfers between devices with their start and end apart: 5 -> 28, of which waited for: 4 -> 7; matrix products, arithmetic and copies ran while one was open for 6% -> 4% of each run, Pallas kernels for 0% -> 30%
where the time goes in v1:
time: 129 us; the launch traced here: 128 us
  Pallas kernels  48.6 us (38%)
  starting transfers between devices  32.5 us (25%)
  waiting for transfers between devices  28.6 us (22%)
  local copies, waits for them, and re-layouts  14.2 us (11%)
  other arithmetic  3.06 us (2%)
  between operations  1.38 us (1%)
    pallas_call x13, Pallas kernels, call(): pl.pallas_call(body, out_shape=out_shape, in_specs=list(in_specs) + [HB]...  48.6 us
    unnamed x66, local copies, waits for them, and re-layouts  12.6 us
    ppermute x6, starting transfers between devices, share_quarter(): return [total] + [lax.ppermute(total, 'seq', pair) for pair in pairs]  10.7 us
    ppermute x6, starting transfers between devices, exchange_quarters(): lax.ppermute(quarters[s], 'seq', [(j, j ^ s) for j in range(4)])  9.81 us
    ppermute x6, waiting for transfers between devices, exchange_quarters(): lax.ppermute(quarters[s], 'seq', [(j, j ^ s) for j in range(4)])  9.33 us
    ppermute x4, waiting for transfers between devices, across(): return lax.ppermute(value, 'head', SWAP)  8.76 us
    ppermute x6, waiting for transfers between devices, up(): return lax.ppermute(value, 'seq', [(i, (i + by) % 4) for i in range(4)])  8.6 us
    ppermute x4, starting transfers between devices, across(): return lax.ppermute(value, 'head', SWAP)  6.18 us
  transfers between devices with their start and end apart: 28, of which 7 were waited for; matrix products, arithmetic and copies ran while one was open for 4% of the time, Pallas kernels for 30%

profile of v1, /device:TPU:0, one launch (start us, length us, event | category | flops | bytes accessed | tf_op | source)
XLA Modules:
  0.0 128.3 jit_solution(8905038634192108993)
XLA Ops:
  0.5 1.3 %concatenate.3.refs_0_ = s32[21]{0:T(128)} concatenate(s32[1]{0:T(128)} %bitcast, s32[1]{0:T(128)} %bitcast.1, s32[1]{0:T(128)} %bitcast.2, s32[2]{0:T(128)} %param.27, s32[16]{0:T(128)} %param.26), dimensions={0} | concatenate | bytes 168 | tf_op jit(solution)/shard_map/concatenate | solution.py:628
  1.8 2.7 %pack.1 = (bf16[64,1344]{1,0:T(8,128)(2,1)}, bf16[64,1344]{1,0:T(8,128)(2,1)}, bf16[64,1344]{1,0:T(8,128)(2,1)}, bf16[64,1344]{1,0:T(8,128)(2,1)}) custom-call(s32[21]{0:T(128)} %concatenate.3.refs_0_, bf16[2,96,1344]{2,1,0:T(8,128)(2,1)} %bitcast.15, bf16[2,32,512]{2,1,0:T(8,128)(2,1)} %refs_2_.2, bf16[2,2,32,512]{3,2,1,0:T(8,128)(2,1)} %refs_3_.1), custom_call_target="tpu_custom_call" | custom-call | flops 1000 | bytes 1000 | tf_op jit(solution)/shard_map/pack/pallas_call | solution.py:307
  5.4 1.3 %copy-done.8 = bf16[512,1344]{0,1:T(8,128)(2,1)S(1)} copy-done((bf16[512,1344]{0,1:T(8,128)(2,1)S(1)}, bf16[512,1344]{0,1:T(8,128)(2,1)}, u32[]{:S(2)}) %copy-start.8) | copy-done | bytes 1376280
  8.5 2.5 %collective-permute-start.1 = (bf16[1344,256]{1,0:T(8,128)(2,1)}, bf16[1344,256]{1,0:T(8,128)(2,1)S(1)}, u32[]{:S(2)}, u32[]{:S(2)}) collective-permute-start(bf16[1344,256]{1,0:T(8,128)(2,1)} %get-tuple-element.32.refs_1_), channel_id=1, source_target_pairs={{0,2},{2,0},{1,3},{3,1},{4,6},{6,4},{5,7},{7,5},{8,10},{10,8},{9,1... | collective-permute-start | bytes 2064392 | tf_op jit(solution)/shard_map/ppermute | solution.py:632
  11.0 1.6 %collective-permute-start.2 = (bf16[64,1344]{1,0:T(8,128)(2,1)}, bf16[64,1344]{1,0:T(8,128)(2,1)S(1)}, u32[]{:S(2)}, u32[]{:S(2)}) collective-permute-start(bf16[64,1344]{1,0:T(8,128)(2,1)} %get-tuple-element.35), channel_id=1, source_target_pairs={{0,4},{4,0},{8,12},{12,8},{1,5},{5,1},{9,13},{13,9},{2,6},{6,2},{1... | collective-permute-start | bytes 516104 | tf_op jit(solution)/shard_map/ppermute | solution.py:601
  12.6 2.6 %collective-permute-start.3 = (bf16[64,1344]{1,0:T(8,128)(2,1)}, bf16[64,1344]{1,0:T(8,128)(2,1)S(1)}, u32[]{:S(2)}, u32[]{:S(2)}) collective-permute-start(bf16[64,1344]{1,0:T(8,128)(2,1)} %get-tuple-element.36), channel_id=1, source_target_pairs={{0,8},{4,12},{8,0},{12,4},{1,9},{5,13},{9,1},{13,5},{2,10},{6,14},... | collective-permute-start | bytes 516104 | tf_op jit(solution)/shard_map/ppermute | solution.py:601
  16.5 8.1 %near.1 = (f32[256,1024]{1,0:T(8,128)}, f32[256,1024]{1,0:T(8,128)}) custom-call(s32[21]{0:T(128)} %concatenate.3.refs_0_, bf16[1344,256]{1,0:T(8,128)(2,1)} %get-tuple-element.32.refs_1_, bf16[1344,256]{1,0:T(8,128)(2,1)} %copy-done.1, bf16[1344,512]{1,0:T(8,128)(2,1)} %copy-done.22, bf16[5376,512]{1,0:T(8,128)(2,1)} %refs_4_.5, bf16[5376,512]{1,0:T(8,128)(2,1)} %refs_5_.5, ...), custom_call_target="tpu_custom_call" | custom-call | flops 1000 | bytes 1000 | tf_op jit(solution)/shard_map/near/pallas_call | solution.py:307
  24.6 4.2 %collective-permute-done.3.refs_2_ = bf16[64,1344]{1,0:T(8,128)(2,1)S(1)} collective-permute-done((bf16[64,1344]{1,0:T(8,128)(2,1)}, bf16[64,1344]{1,0:T(8,128)(2,1)S(1)}, u32[]{:S(2)}, u32[]{:S(2)}) %collective-permute-start.3) | collective-permute-done | bytes 172064 | tf_op jit(solution)/shard_map/ppermute | solution.py:601
  28.9 1.2 copy-done
  30.9 3.4 %collective-permute-start.7 = (bf16[64,1344]{1,0:T(8,128)(2,1)S(1)}, bf16[64,1344]{1,0:T(8,128)(2,1)S(1)}, u32[]{:S(2)}, u32[]{:S(2)}) collective-permute-start(bf16[64,1344]{1,0:T(8,128)(2,1)S(1)} %sum.1.refs_7_.refs_3_), channel_id=1, source_target_pairs={{0,4},{4,0},{8,12},{12,8},{1,5},{5,1},{9,13},{13,9},{2,6},{6,2},{1... | collective-permute-start | bytes 516104 | tf_op jit(solution)/shard_map/ppermute | solution.py:606
  35.0 4.6 %collective-permute-start.9 = (bf16[64,1344]{1,0:T(8,128)(2,1)S(1)}, bf16[64,1344]{1,0:T(8,128)(2,1)S(1)}, u32[]{:S(2)}, u32[]{:S(2)}) collective-permute-start(bf16[64,1344]{1,0:T(8,128)(2,1)S(1)} %sum.1.refs_7_.refs_3_), channel_id=1, source_target_pairs={{0,8},{12,4},{1,9},{13,5},{2,10},{14,6},{3,11},{15,7},{16,24},{28,... | collective-permute-start | bytes 516104 | tf_op jit(solution)/shard_map/ppermute | solution.py:606
  40.5 7.0 %far.2 = (f32[512,256]{1,0:T(8,128)}, bf16[512,256]{1,0:T(8,128)(2,1)}) custom-call(s32[21]{0:T(128)} %concatenate.3.refs_0_, f32[256,1024]{1,0:T(8,128)} %get-tuple-element.34.refs_4_.refs_1_, bf16[1344,256]{1,0:T(8,128)(2,1)} %copy-done.24, bf16[1344,256]{1,0:T(8,128)(2,1)} %copy-done.25, bf16[5376,512]{1,0:T(8,128)(2,1)} %refs_4_.5, ...), custom_call_target="tpu_custom_call" | custom-call | flops 1000 | bytes 1000 | tf_op jit(solution)/shard_map/far/pallas_call | solution.py:307
  48.5 1.6 %low.1 = (f32[96,512]{1,0:T(8,128)S(1)}, bf16[64,1024]{1,0:T(8,128)(2,1)S(1)}) custom-call(s32[21]{0:T(128)S(1)} %copy-done.19, bf16[1344,256]{1,0:T(8,128)(2,1)} %get-tuple-element.32.refs_1_, bf16[1344,256]{1,0:T(8,128)(2,1)S(1)} %copy-done.2, bf16[64,1344]{1,0:T(8,128)(2,1)S(1)} %copy-done.7, bf16[64,1344]{1,0:T(8,128)(2,1)S(1)} %collective-permute-done.7.refs_4_, ...), custom_call_target="tpu_custom_call" | custom-call | flops 1000 | bytes 1000 | tf_op jit(solution)/shard_map/low/pallas_call | solution.py:307
  50.2 1.4 %collective-permute-done.10 = f32[96,512]{1,0:T(8,128)S(1)} collective-permute-done((f32[96,512]{1,0:T(8,128)S(1)}, f32[96,512]{1,0:T(8,128)S(1)}, u32[]{:S(2)}, u32[]{:S(2)}) %collective-permute-start.10) | collective-permute-done | bytes 196640 | tf_op jit(solution)/shard_map/ppermute | solution.py:635
  51.9 1.5 %collective-permute-start.14 = (f32[96,512]{1,0:T(8,128)S(1)}, f32[96,512]{1,0:T(8,128)S(1)}, u32[]{:S(2)}, u32[]{:S(2)}) collective-permute-start(f32[96,512]{1,0:T(8,128)S(1)} %add.17.refs_7_), channel_id=1, source_target_pairs={{0,2},{2,0},{1,3},{3,1},{4,6},{6,4},{5,7},{7,5},{8,10},{10,8},{9,1... | collective-permute-start | bytes 589832 | tf_op jit(solution)/shard_map/ppermute | solution.py:632
  54.8 7.2 %far.3 = (f32[512,256]{1,0:T(8,128)}, bf16[512,256]{1,0:T(8,128)(2,1)}) custom-call(s32[21]{0:T(128)} %concatenate.3.refs_0_, f32[256,1024]{1,0:T(8,128)} %get-tuple-element.40.refs_1_, bf16[1344,256]{1,0:T(8,128)(2,1)} %copy-done.23, bf16[1344,256]{1,0:T(8,128)(2,1)} %copy-done.26, bf16[5376,512]{1,0:T(8,128)(2,1)} %refs_4_.5, bf16[5376,512]{1,0:T(8,128)(2,1)} %refs_5_.5, ...), custom_call_target="tpu_custom_call" | custom-call | flops 1000 | bytes 1000 | tf_op jit(solution)/shard_map/far/pallas_call | solution.py:307
  64.1 3.0 %collective-permute-start.19 = (bf16[16,1920]{1,0:T(8,128)(2,1)S(1)}, bf16[16,1920]{1,0:T(8,128)(2,1)S(1)}, u32[]{:S(2)}, u32[]{:S(2)}) collective-permute-start(bf16[16,1920]{1,0:T(8,128)(2,1)S(1)} %get-tuple-element.52), channel_id=1, source_target_pairs={{0,4},{4,0},{8,12},{12,8},{1,5},{5,1},{9,13},{13,9},{2,6},{6,2},{1... | collective-permute-start | bytes 184328 | tf_op jit(solution)/shard_map/ppermute | solution.py:601
  67.1 1.4 %collective-permute-start.20 = (bf16[16,1920]{1,0:T(8,128)(2,1)S(1)}, bf16[16,1920]{1,0:T(8,128)(2,1)S(1)}, u32[]{:S(2)}, u32[]{:S(2)}) collective-permute-start(bf16[16,1920]{1,0:T(8,128)(2,1)S(1)} %get-tuple-element.53), channel_id=1, source_target_pairs={{0,8},{4,12},{8,0},{12,4},{1,9},{5,13},{9,1},{13,5},{2,10},{6,14},... | collective-permute-start | bytes 184328 | tf_op jit(solution)/shard_map/ppermute | solution.py:601
  68.5 1.1 collective-permute-start.21
  70.6 5.1 %collective-permute-done.19.refs_1_ = bf16[16,1920]{1,0:T(8,128)(2,1)S(1)} collective-permute-done((bf16[16,1920]{1,0:T(8,128)(2,1)S(1)}, bf16[16,1920]{1,0:T(8,128)(2,1)S(1)}, u32[]{:S(2)}, u32[]{:S(2)}) %collective-permute-start.19) | collective-permute-done | bytes 61472 | tf_op jit(solution)/shard_map/ppermute | solution.py:601
  75.6 1.8 %collective-permute-start.18 = (bf16[64,512]{1,0:T(8,128)(2,1)S(1)}, bf16[64,512]{1,0:T(8,128)(2,1)S(1)}, u32[]{:S(2)}, u32[]{:S(2)}) collective-permute-start(bf16[64,512]{1,0:T(8,128)(2,1)S(1)} %slice.7), channel_id=1, source_target_pairs={{0,8},{4,12},{8,0},{12,4},{1,9},{5,13},{9,1},{13,5},{2,10},{6,14},... | collective-permute-start | bytes 196616 | tf_op jit(solution)/shard_map/ppermute | solution.py:638
  77.4 2.7 %collective-permute-start.16 = (bf16[512,256]{1,0:T(8,128)(2,1)S(1)}, bf16[512,256]{1,0:T(8,128)(2,1)S(1)}, u32[]{:S(2)}, u32[]{:S(2)}) collective-permute-start(bf16[512,256]{1,0:T(8,128)(2,1)S(1)} %collective-permute-done.12.refs_5_), channel_id=1, source_target_pairs={{0,4},{4,8},{8,12},{12,0},{1,5},{5,9},{9,13},{13,1},{2,6},{6,10},{... | collective-permute-start | bytes 786440 | tf_op jit(solution)/shard_map/ppermute | solution.py:638
  81.2 1.3 %collective-permute-done.15.refs_8_ = bf16[64,512]{1,0:T(8,128)(2,1)S(1)} collective-permute-done((bf16[64,512]{1,0:T(8,128)(2,1)S(1)}, bf16[64,512]{1,0:T(8,128)(2,1)S(1)}, u32[]{:S(2)}, u32[]{:S(2)}) %collective-permute-start.15) | collective-permute-done | bytes 65568 | tf_op jit(solution)/shard_map/ppermute | solution.py:638
  83.2 7.3 %collective-permute-done.18.refs_6_ = bf16[64,512]{1,0:T(8,128)(2,1)S(1)} collective-permute-done((bf16[64,512]{1,0:T(8,128)(2,1)S(1)}, bf16[64,512]{1,0:T(8,128)(2,1)S(1)}, u32[]{:S(2)}, u32[]{:S(2)}) %collective-permute-start.18) | collective-permute-done | bytes 65568 | tf_op jit(solution)/shard_map/ppermute | solution.py:638
  90.4 1.3 collective-permute-start.24
  92.0 1.4 %multiply_sine_fusion = (f32[64,1536]{1,0:T(8,128)S(1)}, f32[64,1536]{1,0:T(8,128)S(1)}) fusion(f32[1536]{0:T(1024)S(1)} %fusion, f32[64]{0:T(128)S(1)} %multiply_power_fusion), kind=kLoop, calls=%fused_computation | loop fusion | flops 98304 | bytes 792832 | tf_op jit(solution)/shard_map/sin | solution.py:703
  95.6 5.0 %attend_near.1 = (bf16[512,512]{1,0:T(8,128)(2,1)S(1)}, f32[512,512]{1,0:T(8,128)S(1)}, f32[8,512]{1,0:T(8,128)S(1)}) custom-call(s32[21]{0:T(128)S(1)} %copy-done.20, f32[512,256]{1,0:T(8,128)S(1)} %copy-done.12, f32[512,256]{1,0:T(8,128)S(1)} %copy-done.13, bf16[512,256]{1,0:T(8,128)(2,1)} %get-tuple-element.41.refs_7_.refs_3_, ...), custom_call_target="tpu_custom_call" | custom-call | flops 1000 | bytes 1000 | tf_op jit(solution)/shard_map/attend_near/pallas_call | solution.py:307
  100.7 2.6 %attend_far.1.refs_1_ = bf16[576,512]{1,0:T(8,128)(2,1)S(1)} custom-call(s32[21]{0:T(128)S(1)} %copy-done.20, bf16[512,512]{1,0:T(8,128)(2,1)S(1)} %get-tuple-element.47.refs_1_, f32[512,512]{1,0:T(8,128)S(1)} %get-tuple-element.48.refs_2_, f32[8,512]{1,0:T(8,128)S(1)} %get-tuple-element.49.refs_3_, bf16[512,256]{1,0:T(8,128)(2,1)S(1)} %collective-permute-done.16.refs_4_, ...), custom_call_target="tpu_custom_call" | custom-call | flops 1000 | bytes 1000 | tf_op jit(solution)/shard_map/attend_far/pallas_call | solution.py:307
  103.3 1.6 %collective-permute-start.25 = (bf16[576,512]{1,0:T(8,128)(2,1)S(1)}, bf16[576,512]{1,0:T(8,128)(2,1)S(1)}, u32[]{:S(2)}, u32[]{:S(2)}) collective-permute-start(bf16[576,512]{1,0:T(8,128)(2,1)S(1)} %attend_far.1.refs_1_), channel_id=1, source_target_pairs={{0,2},{2,0},{1,3},{3,1},{4,6},{6,4},{5,7},{7,5},{8,10},{10,8},{9,1... | collective-permute-start | bytes 1769480 | tf_op jit(solution)/shard_map/ppermute | solution.py:632
  104.9 8.8 %collective-permute-done.25.refs_1_ = bf16[576,512]{1,0:T(8,128)(2,1)S(1)} collective-permute-done((bf16[576,512]{1,0:T(8,128)(2,1)S(1)}, bf16[576,512]{1,0:T(8,128)(2,1)S(1)}, u32[]{:S(2)}, u32[]{:S(2)}) %collective-permute-start.25) | collective-permute-done | bytes 589856 | tf_op jit(solution)/shard_map/ppermute | solution.py:632
  114.5 5.9 %out_near.1 = (f32[1344,512]{1,0:T(8,128)}, f32[64,512]{1,0:T(8,128)}) custom-call(s32[21]{0:T(128)} %concatenate.3.refs_0_, bf16[576,512]{1,0:T(8,128)(2,1)} %copy-done.3, bf16[576,512]{1,0:T(8,128)(2,1)} %copy-done.29, bf16[1344,2048]{1,0:T(8,128)(2,1)} %bitcast.13), custom_call_target="tpu_custom_call" | custom-call | flops 1000 | bytes 1000 | tf_op jit(solution)/shard_map/out_near/pallas_call | solution.py:307
  121.3 6.9 %out_far.1 = bf16[1344,512]{1,0:T(8,128)(2,1)} custom-call(s32[21]{0:T(128)} %concatenate.3.refs_0_, bf16[576,512]{1,0:T(8,128)(2,1)} %copy-done.27, bf16[576,512]{1,0:T(8,128)(2,1)} %copy-done.28, bf16[1344,2048]{1,0:T(8,128)(2,1)} %bitcast.14, f32[1344,512]{1,0:T(8,128)} %get-tuple-element.55.refs_4_, f32[64,512]{1,0:T(8,128)} %get-tuple-element.56.refs_5_, ...), custom_call_target="tpu_custom_call" | custom-call | flops 1000 | bytes 1000 | tf_op jit(solution)/shard_map/out_far/pallas_call | solution.py:307
  (113 shorter events, 17.6 us)
Async XLA Ops:
  0.0 15.4 %collective-permute-start = (bf16[1344,512]{1,0:T(8,128)(2,1)}, bf16[1344,512]{1,0:T(8,128)(2,1)S(1)}, u32[]{:S(2)}, u32[]{:S(2)}) collective-permute-start(bf16[1344,512]{1,0:T(8,128)(2,1)} %bitcast.10), channel_id=1, source_target_pairs={{0,1},{1,0},{2,3},{3,2},{4,5},{5,4},{6,7},{7,6},{8,9},{9,8},{10,11... | collective-permute-start | bytes 4128776 | tf_op jit(solution)/shard_map/ppermute | solution.py:635
  8.5 21.6 %collective-permute-start.1 = (bf16[1344,256]{1,0:T(8,128)(2,1)}, bf16[1344,256]{1,0:T(8,128)(2,1)S(1)}, u32[]{:S(2)}, u32[]{:S(2)}) collective-permute-start(bf16[1344,256]{1,0:T(8,128)(2,1)} %get-tuple-element.32.refs_1_), channel_id=1, source_target_pairs={{0,2},{2,0},{1,3},{3,1},{4,6},{6,4},{5,7},{7,5},{8,10},{10,8},{9,1... | collective-permute-start | bytes 2064392 | tf_op jit(solution)/shard_map/ppermute | solution.py:632
  11.0 13.6 %collective-permute-start.2 = (bf16[64,1344]{1,0:T(8,128)(2,1)}, bf16[64,1344]{1,0:T(8,128)(2,1)S(1)}, u32[]{:S(2)}, u32[]{:S(2)}) collective-permute-start(bf16[64,1344]{1,0:T(8,128)(2,1)} %get-tuple-element.35), channel_id=1, source_target_pairs={{0,4},{4,0},{8,12},{12,8},{1,5},{5,1},{9,13},{13,9},{2,6},{6,2},{1... | collective-permute-start | bytes 516104 | tf_op jit(solution)/shard_map/ppermute | solution.py:601
  12.6 16.3 %collective-permute-start.3 = (bf16[64,1344]{1,0:T(8,128)(2,1)}, bf16[64,1344]{1,0:T(8,128)(2,1)S(1)}, u32[]{:S(2)}, u32[]{:S(2)}) collective-permute-start(bf16[64,1344]{1,0:T(8,128)(2,1)} %get-tuple-element.36), channel_id=1, source_target_pairs={{0,8},{4,12},{8,0},{12,4},{1,9},{5,13},{9,1},{13,5},{2,10},{6,14},... | collective-permute-start | bytes 516104 | tf_op jit(solution)/shard_map/ppermute | solution.py:601
  15.2 13.7 %collective-permute-start.4 = (bf16[64,1344]{1,0:T(8,128)(2,1)}, bf16[64,1344]{1,0:T(8,128)(2,1)S(1)}, u32[]{:S(2)}, u32[]{:S(2)}) collective-permute-start(bf16[64,1344]{1,0:T(8,128)(2,1)} %get-tuple-element.37), channel_id=1, source_target_pairs={{0,12},{4,8},{8,4},{12,0},{1,13},{5,9},{9,5},{13,1},{2,14},{6,10},... | collective-permute-start | bytes 516104 | tf_op jit(solution)/shard_map/ppermute | solution.py:601
  30.2 9.4 %collective-permute-start.5 = (bf16[1344,256]{1,0:T(8,128)(2,1)S(1)}, bf16[1344,256]{1,0:T(8,128)(2,1)S(1)}, u32[]{:S(2)}, u32[]{:S(2)}) collective-permute-start(bf16[1344,256]{1,0:T(8,128)(2,1)S(1)} %collective-permute-done.1.refs_2_), channel_id=1, source_target_pairs={{0,1},{1,0},{2,3},{3,2},{4,5},{5,4},{6,7},{7,6},{8,9},{9,8},{10,11... | collective-permute-start | bytes 2064392 | tf_op jit(solution)/shard_map/ppermute | solution.py:635
  30.3 21.4 %collective-permute-start.6 = (bf16[1344,256]{1,0:T(8,128)(2,1)S(1)}, bf16[1344,256]{1,0:T(8,128)(2,1)S(1)}, u32[]{:S(2)}, u32[]{:S(2)}) collective-permute-start(bf16[1344,256]{1,0:T(8,128)(2,1)S(1)} %copy-done.2), channel_id=1, source_target_pairs={{0,2},{2,0},{1,3},{3,1},{4,6},{6,4},{5,7},{7,5},{8,10},{10,8},{9,1... | collective-permute-start | bytes 2064392 | tf_op jit(solution)/shard_map/ppermute | solution.py:632
  30.9 16.7 %collective-permute-start.7 = (bf16[64,1344]{1,0:T(8,128)(2,1)S(1)}, bf16[64,1344]{1,0:T(8,128)(2,1)S(1)}, u32[]{:S(2)}, u32[]{:S(2)}) collective-permute-start(bf16[64,1344]{1,0:T(8,128)(2,1)S(1)} %sum.1.refs_7_.refs_3_), channel_id=1, source_target_pairs={{0,4},{4,0},{8,12},{12,8},{1,5},{5,1},{9,13},{13,9},{2,6},{6,2},{1... | collective-permute-start | bytes 516104 | tf_op jit(solution)/shard_map/ppermute | solution.py:606
  34.3 13.2 %collective-permute-start.8 = (bf16[64,1344]{1,0:T(8,128)(2,1)S(1)}, bf16[64,1344]{1,0:T(8,128)(2,1)S(1)}, u32[]{:S(2)}, u32[]{:S(2)}) collective-permute-start(bf16[64,1344]{1,0:T(8,128)(2,1)S(1)} %sum.1.refs_7_.refs_3_), channel_id=1, source_target_pairs={{4,8},{8,4},{5,9},{9,5},{6,10},{10,6},{7,11},{11,7},{20,24},{24,20... | collective-permute-start | bytes 516104 | tf_op jit(solution)/shard_map/ppermute | solution.py:606
  35.0 12.6 %collective-permute-start.9 = (bf16[64,1344]{1,0:T(8,128)(2,1)S(1)}, bf16[64,1344]{1,0:T(8,128)(2,1)S(1)}, u32[]{:S(2)}, u32[]{:S(2)}) collective-permute-start(bf16[64,1344]{1,0:T(8,128)(2,1)S(1)} %sum.1.refs_7_.refs_3_), channel_id=1, source_target_pairs={{0,8},{12,4},{1,9},{13,5},{2,10},{14,6},{3,11},{15,7},{16,24},{28,... | collective-permute-start | bytes 516104 | tf_op jit(solution)/shard_map/ppermute | solution.py:606
  50.1 1.5 %collective-permute-start.10 = (f32[96,512]{1,0:T(8,128)S(1)}, f32[96,512]{1,0:T(8,128)S(1)}, u32[]{:S(2)}, u32[]{:S(2)}) collective-permute-start(f32[96,512]{1,0:T(8,128)S(1)} %get-tuple-element.42), channel_id=1, source_target_pairs={{0,1},{1,0},{2,3},{3,2},{4,5},{5,4},{6,7},{7,6},{8,9},{9,8},{10,11... | collective-permute-start | bytes 589832 | tf_op jit(solution)/shard_map/ppermute | solution.py:635
  51.7 2.2 %collective-permute-start.11 = (bf16[1344,256]{1,0:T(8,128)(2,1)S(1)}, bf16[1344,256]{1,0:T(8,128)(2,1)S(1)}, u32[]{:S(2)}, u32[]{:S(2)}) collective-permute-start(bf16[1344,256]{1,0:T(8,128)(2,1)S(1)} %collective-permute-done.6.refs_2_), channel_id=1, source_target_pairs={{0,1},{1,0},{2,3},{3,2},{4,5},{5,4},{6,7},{7,6},{8,9},{9,8},{10,11... | collective-permute-start | bytes 2064392 | tf_op jit(solution)/shard_map/ppermute | solution.py:635
  51.9 23.8 %collective-permute-start.12 = (bf16[512,256]{1,0:T(8,128)(2,1)}, bf16[512,256]{1,0:T(8,128)(2,1)S(1)}, u32[]{:S(2)}, u32[]{:S(2)}) collective-permute-start(bf16[512,256]{1,0:T(8,128)(2,1)} %get-tuple-element.41.refs_7_.refs_3_), channel_id=1, source_target_pairs={{0,4},{4,8},{8,12},{12,0},{1,5},{5,9},{9,13},{13,1},{2,6},{6,10},{... | collective-permute-start | bytes 786440 | tf_op jit(solution)/shard_map/ppermute | solution.py:638
  51.9 16.6 %collective-permute-start.14 = (f32[96,512]{1,0:T(8,128)S(1)}, f32[96,512]{1,0:T(8,128)S(1)}, u32[]{:S(2)}, u32[]{:S(2)}) collective-permute-start(f32[96,512]{1,0:T(8,128)S(1)} %add.17.refs_7_), channel_id=1, source_target_pairs={{0,2},{2,0},{1,3},{3,1},{4,6},{6,4},{5,7},{7,5},{8,10},{10,8},{9,1... | collective-permute-start | bytes 589832 | tf_op jit(solution)/shard_map/ppermute | solution.py:632
  54.8 38.6 %copy-start.30 = (f32[128]{0:T(128)S(1)}, f32[128]{0:T(128)}, u32[]{:S(2)}) copy-start(f32[128]{0:T(128)} %param.20) | copy-start | bytes 1540
  54.8 38.8 %copy-start.31 = (f32[128]{0:T(128)S(1)}, f32[128]{0:T(128)}, u32[]{:S(2)}) copy-start(f32[128]{0:T(128)} %param.19) | copy-start | bytes 1540
  54.8 38.9 %copy-start.12 = (f32[512,256]{1,0:T(8,128)S(1)}, f32[512,256]{1,0:T(8,128)}, u32[]{:S(2)}) copy-start(f32[512,256]{1,0:T(8,128)} %get-tuple-element.39.refs_1_) | copy-start | bytes 1572868
  62.0 29.7 %collective-permute-start.13 = (bf16[512,256]{1,0:T(8,128)(2,1)}, bf16[512,256]{1,0:T(8,128)(2,1)S(1)}, u32[]{:S(2)}, u32[]{:S(2)}) collective-permute-start(bf16[512,256]{1,0:T(8,128)(2,1)} %get-tuple-element.45.refs_4_), channel_id=1, source_target_pairs={{0,4},{4,8},{8,12},{12,0},{1,5},{5,9},{9,13},{13,1},{2,6},{6,10},{... | collective-permute-start | bytes 786440 | tf_op jit(solution)/shard_map/ppermute | solution.py:638
  64.1 11.5 %collective-permute-start.19 = (bf16[16,1920]{1,0:T(8,128)(2,1)S(1)}, bf16[16,1920]{1,0:T(8,128)(2,1)S(1)}, u32[]{:S(2)}, u32[]{:S(2)}) collective-permute-start(bf16[16,1920]{1,0:T(8,128)(2,1)S(1)} %get-tuple-element.52), channel_id=1, source_target_pairs={{0,4},{4,0},{8,12},{12,8},{1,5},{5,1},{9,13},{13,9},{2,6},{6,2},{1... | collective-permute-start | bytes 184328 | tf_op jit(solution)/shard_map/ppermute | solution.py:601
  67.1 10.3 %collective-permute-start.20 = (bf16[16,1920]{1,0:T(8,128)(2,1)S(1)}, bf16[16,1920]{1,0:T(8,128)(2,1)S(1)}, u32[]{:S(2)}, u32[]{:S(2)}) collective-permute-start(bf16[16,1920]{1,0:T(8,128)(2,1)S(1)} %get-tuple-element.53), channel_id=1, source_target_pairs={{0,8},{4,12},{8,0},{12,4},{1,9},{5,13},{9,1},{13,5},{2,10},{6,14},... | collective-permute-start | bytes 184328 | tf_op jit(solution)/shard_map/ppermute | solution.py:601
  68.5 11.6 %collective-permute-start.21 = (bf16[16,1920]{1,0:T(8,128)(2,1)S(1)}, bf16[16,1920]{1,0:T(8,128)(2,1)S(1)}, u32[]{:S(2)}, u32[]{:S(2)}) collective-permute-start(bf16[16,1920]{1,0:T(8,128)(2,1)S(1)} %get-tuple-element.54), channel_id=1, source_target_pairs={{0,12},{4,8},{8,4},{12,0},{1,13},{5,9},{9,5},{13,1},{2,14},{6,10},... | collective-permute-start | bytes 184328 | tf_op jit(solution)/shard_map/ppermute | solution.py:601
  75.6 6.9 %collective-permute-start.15 = (bf16[64,512]{1,0:T(8,128)(2,1)S(1)}, bf16[64,512]{1,0:T(8,128)(2,1)S(1)}, u32[]{:S(2)}, u32[]{:S(2)}) collective-permute-start(bf16[64,512]{1,0:T(8,128)(2,1)S(1)} %slice.7), channel_id=1, source_target_pairs={{0,4},{4,8},{8,12},{12,0},{1,5},{5,9},{9,13},{13,1},{2,6},{6,10},{... | collective-permute-start | bytes 196616 | tf_op jit(solution)/shard_map/ppermute | solution.py:638
  75.6 14.8 %collective-permute-start.18 = (bf16[64,512]{1,0:T(8,128)(2,1)S(1)}, bf16[64,512]{1,0:T(8,128)(2,1)S(1)}, u32[]{:S(2)}, u32[]{:S(2)}) collective-permute-start(bf16[64,512]{1,0:T(8,128)(2,1)S(1)} %slice.7), channel_id=1, source_target_pairs={{0,8},{4,12},{8,0},{12,4},{1,9},{5,13},{9,1},{13,5},{2,10},{6,14},... | collective-permute-start | bytes 196616 | tf_op jit(solution)/shard_map/ppermute | solution.py:638
  77.4 23.2 %collective-permute-start.16 = (bf16[512,256]{1,0:T(8,128)(2,1)S(1)}, bf16[512,256]{1,0:T(8,128)(2,1)S(1)}, u32[]{:S(2)}, u32[]{:S(2)}) collective-permute-start(bf16[512,256]{1,0:T(8,128)(2,1)S(1)} %collective-permute-done.12.refs_5_), channel_id=1, source_target_pairs={{0,4},{4,8},{8,12},{12,0},{1,5},{5,9},{9,13},{13,1},{2,6},{6,10},{... | collective-permute-start | bytes 786440 | tf_op jit(solution)/shard_map/ppermute | solution.py:638
  81.1 39.4 %copy-start.11 = (bf16[16,1920]{1,0:T(8,128)(2,1)}, bf16[16,1920]{1,0:T(8,128)(2,1)S(1)}, u32[]{:S(2)}) copy-start(bf16[16,1920]{1,0:T(8,128)(2,1)S(1)} %out_sum.1.refs_11_.refs_6_) | copy-start | bytes 184324
  81.1 19.6 %collective-permute-start.22 = (bf16[16,1920]{1,0:T(8,128)(2,1)S(1)}, bf16[16,1920]{1,0:T(8,128)(2,1)S(1)}, u32[]{:S(2)}, u32[]{:S(2)}) collective-permute-start(bf16[16,1920]{1,0:T(8,128)(2,1)S(1)} %out_sum.1.refs_11_.refs_6_), channel_id=1, source_target_pairs={{0,4},{4,0},{8,12},{12,8},{1,5},{5,1},{9,13},{13,9},{2,6},{6,2},{1... | collective-permute-start | bytes 184328 | tf_op jit(solution)/shard_map/ppermute | solution.py:606
  82.5 18.2 %collective-permute-start.23 = (bf16[16,1920]{1,0:T(8,128)(2,1)S(1)}, bf16[16,1920]{1,0:T(8,128)(2,1)S(1)}, u32[]{:S(2)}, u32[]{:S(2)}) collective-permute-start(bf16[16,1920]{1,0:T(8,128)(2,1)S(1)} %out_sum.1.refs_11_.refs_6_), channel_id=1, source_target_pairs={{4,8},{8,4},{5,9},{9,5},{6,10},{10,6},{7,11},{11,7},{20,24},{24,20... | collective-permute-start | bytes 184328 | tf_op jit(solution)/shard_map/ppermute | solution.py:606
  90.4 10.3 %collective-permute-start.24 = (bf16[16,1920]{1,0:T(8,128)(2,1)S(1)}, bf16[16,1920]{1,0:T(8,128)(2,1)S(1)}, u32[]{:S(2)}, u32[]{:S(2)}) collective-permute-start(bf16[16,1920]{1,0:T(8,128)(2,1)S(1)} %out_sum.1.refs_11_.refs_6_), channel_id=1, source_target_pairs={{0,8},{12,4},{1,9},{13,5},{2,10},{14,6},{3,11},{15,7},{16,24},{28,... | collective-permute-start | bytes 184328 | tf_op jit(solution)/shard_map/ppermute | solution.py:606
  91.7 9.0 %collective-permute-start.17 = (bf16[512,256]{1,0:T(8,128)(2,1)S(1)}, bf16[512,256]{1,0:T(8,128)(2,1)S(1)}, u32[]{:S(2)}, u32[]{:S(2)}) collective-permute-start(bf16[512,256]{1,0:T(8,128)(2,1)S(1)} %collective-permute-done.13.refs_6_), channel_id=1, source_target_pairs={{0,4},{4,8},{8,12},{12,0},{1,5},{5,9},{9,13},{13,1},{2,6},{6,10},{... | collective-permute-start | bytes 786440 | tf_op jit(solution)/shard_map/ppermute | solution.py:638
  103.3 10.3 %collective-permute-start.25 = (bf16[576,512]{1,0:T(8,128)(2,1)S(1)}, bf16[576,512]{1,0:T(8,128)(2,1)S(1)}, u32[]{:S(2)}, u32[]{:S(2)}) collective-permute-start(bf16[576,512]{1,0:T(8,128)(2,1)S(1)} %attend_far.1.refs_1_), channel_id=1, source_target_pairs={{0,2},{2,0},{1,3},{3,1},{4,6},{6,4},{5,7},{7,5},{8,10},{10,8},{9,1... | collective-permute-start | bytes 1769480 | tf_op jit(solution)/shard_map/ppermute | solution.py:632
  104.9 8.8 %collective-permute-start.27 = (bf16[576,512]{1,0:T(8,128)(2,1)S(1)}, bf16[576,512]{1,0:T(8,128)(2,1)S(1)}, u32[]{:S(2)}, u32[]{:S(2)}) collective-permute-start(bf16[576,512]{1,0:T(8,128)(2,1)S(1)} %attend_far.1.refs_1_), channel_id=1, source_target_pairs={{0,1},{1,0},{2,3},{3,2},{4,5},{5,4},{6,7},{7,6},{8,9},{9,8},{10,11... | collective-permute-start | bytes 1769480 | tf_op jit(solution)/shard_map/ppermute | solution.py:635
  113.7 6.8 %collective-permute-start.26 = (bf16[576,512]{1,0:T(8,128)(2,1)S(1)}, bf16[576,512]{1,0:T(8,128)(2,1)S(1)}, u32[]{:S(2)}, u32[]{:S(2)}) collective-permute-start(bf16[576,512]{1,0:T(8,128)(2,1)S(1)} %collective-permute-done.25.refs_1_), channel_id=1, source_target_pairs={{0,1},{1,0},{2,3},{3,2},{4,5},{5,4},{6,7},{7,6},{8,9},{9,8},{10,11... | collective-permute-start | bytes 1769480 | tf_op jit(solution)/shard_map/ppermute | solution.py:635
  (29 other events, 189.9 us)

commit v2 on v1

--- a/solution.py
+++ b/solution.py
@@ -1,3 +1,4 @@
+import functools
 import math
 
 import jax
@@ -266,7 +267,7 @@
 
 F32 = jnp.float32
 BF16 = jnp.bfloat16
-VMEM_SMALL = 16 * 1024 * 1024
+VMEM_SMALL = 20 * 1024 * 1024
 VMEM_LARGE = 56 * 1024 * 1024
 SWAP = [(0, 1), (1, 0)]
 SHARD_BLOCKS = 4
@@ -290,11 +291,15 @@
 FAR = pl.BlockSpec(memory_space=pltpu.HBM)
 
 
+def in_hbm(value):
+    return pltpu.with_memory_space_constraint(value, pltpu.HBM)
+
+
 def shape(dims, dtype=BF16):
     return jax.ShapeDtypeStruct(dims, dtype)
 
 
-def call(kernel, name, out_shape, in_specs, args, scratch=(), out_specs=None, grid=None, after=()):
+def call(kernel, name, out_shape, in_specs, args, scratch=(), out_specs=None, grid=None, after=(), aliases=None):
     count = len(in_specs)
 
     def body(*refs):
@@ -310,60 +315,70 @@
         in_specs=list(in_specs) + [HB] * len(after),
         out_specs=outs,
         scratch_shapes=list(scratch),
-        compiler_params=pltpu.CompilerParams(vmem_limit_bytes=VMEM_LARGE if FAR in in_specs else VMEM_SMALL),
+        input_output_aliases=aliases or {},
+        compiler_params=pltpu.CompilerParams(vmem_limit_bytes=VMEM_SMALL),
         cost_estimate=pl.CostEstimate(flops=1000, bytes_accessed=1000, transcendentals=0),
         name=name,
         **more,
-    )(*args, *after)
-
-
-def split_kernel(tokens, *chunks):
-    for c, chunk in enumerate(chunks):
-        chunk[...] = tokens[:, c * CHUNK : (c + 1) * CHUNK]
-
-
-def picked(meta, held, quarter):
-    request = lax.div(quarter, 2)
-    slot = meta[META_ADAPTER + request] - meta[0] * held
-    here = jnp.logical_and(slot >= 0, slot < held)
-    keep = jnp.where(here, 1.0, 0.0).astype(F32)
-    return jnp.clip(slot, 0, held - 1), keep, lax.rem(quarter, 2)
-
-
-def pack_kernel(meta, down_far, up_q_far, up_kv_far, *refs):
-    quarters, (down, up_q, up_kv, sems) = refs[:4], refs[4:]
-    copies = [
-        pltpu.make_async_copy(a, b, sems.at[i])
-        for i, (a, b) in enumerate(((down_far, down), (up_q_far, up_q), (up_kv_far, up_kv)))
-    ]
+    )(*[in_hbm(a) if spec is FAR else a for a, spec in zip(args, in_specs)], *after)
+
+
+def picked(adapters, held):
+    me = lax.axis_index("seq").astype(jnp.int32)
+    chosen = []
+    for step in range(4):
+        quarter = jnp.bitwise_xor(me, step)
+        slot = adapters[lax.div(quarter, 2)] - me * held
+        here = jnp.logical_and(slot >= 0, slot < held)
+        keep = jnp.where(here, 1.0, 0.0).astype(F32)
+        chosen.append((jnp.clip(slot, 0, held - 1), keep, lax.rem(quarter, 2)))
+    return chosen
+
+
+def bring(sources, targets, sems):
+    copies = [pltpu.make_async_copy(a, b, sems.at[i]) for i, (a, b) in enumerate(zip(sources, targets))]
     for copy in copies:
         copy.start()
     for copy in copies:
         copy.wait()
+
+
+def pack_kernel(adapters, down_far, up_q_far, up_kv_far, *refs):
+    quarters, (down, up_q, up_kv, sems) = refs[:4], refs[4:]
+    bring((down_far, up_q_far, up_kv_far), (down, up_q, up_kv), sems)
+    rep = lax.axis_index("rep").astype(jnp.int32)
     half = up_kv.shape[3] // 2
     cols = up_q.shape[2]
     width = down.shape[2]
-    for step, out in enumerate(quarters):
-        slot, keep, part = picked(meta, down.shape[0], jnp.bitwise_xor(meta[0], step))
+    for (slot, keep, part), out in zip(picked(adapters, down.shape[0]), quarters):
         rows = pl.ds(pl.multiple_of(part * 48, 16), 48)
         ranks = pl.ds(pl.multiple_of(part * 16, 16), 16)
         out[0:48, :] = (down[slot, rows, :].astype(F32) * keep).astype(BF16)
         out[48:64, 0:cols] = (up_q[slot, ranks, :].astype(F32) * keep).astype(BF16)
         for which in range(2):
             both = up_kv[slot, which, ranks, :].astype(F32) * keep
-            mine = jnp.where(meta[1] == 0, both[:, :half], both[:, half:])
+            mine = jnp.where(rep == 0, both[:, :half], both[:, half:])
             out[48:64, cols + which * half : cols + (which + 1) * half] = mine.astype(BF16)
         out[48:64, 1024:width] = jnp.zeros((16, width - 1024), BF16)
 
 
-def pack_out_kernel(meta, down, up, *quarters):
-    width = up.shape[2]
-    for step, out in enumerate(quarters):
-        slot, keep, part = picked(meta, down.shape[0], jnp.bitwise_xor(meta[0], step))
-        ranks = pl.ds(pl.multiple_of(part * 16, 16), 16)
-        out[:, 0:width] = (up[slot, ranks, :].astype(F32) * keep).astype(BF16)
-        out[:, width:1408] = jnp.zeros((16, 1408 - width), BF16)
-        out[:, 1408:1920] = (down[slot, ranks, :].astype(F32) * keep).astype(BF16)
+def pack_out_kernel(adapters, out_down_far, out_up_far, out, out_down, out_up, sems):
+    bring((out_down_far, out_up_far), (out_down, out_up), sems)
+    width = out_up.shape[2]
+    held = out_up.shape[0]
+    for request in range(2):
+        slot = adapters[request] - lax.axis_index("seq").astype(jnp.int32) * held
+        here = jnp.logical_and(slot >= 0, slot < held)
+        keep = jnp.where(here, 1.0, 0.0).astype(F32)
+        slot = jnp.clip(slot, 0, held - 1)
+        rows = slice(request * 32, (request + 1) * 32)
+        out[rows, 0:width] = (out_up[slot].astype(F32) * keep).astype(BF16)
+        out[rows, width:1408] = jnp.zeros((32, 1408 - width), BF16)
+        out[rows, 1408:1920] = (out_down[slot].astype(F32) * keep).astype(BF16)
+
+
+def add_kernel(a, b, out):
+    out[...] = a[...] + b[...]
 
 
 def sum_kernel(a, b, c, d, out):
@@ -378,10 +393,10 @@
         panel[index] = quarter[...]
 
 
-def low_kernel(meta, tok0, tok1, p0, p1, p2, p3, low_t, ups, panel):
+def low_kernel(meta, tokens, p0, p1, p2, p3, low_t, ups, panel):
     place_quarters(meta, (p0, p1, p2, p3), panel)
     down = jnp.concatenate([panel[j, 0:48, :] for j in range(4)], axis=0)
-    both = jnp.concatenate([dot(down, tok0[...]), dot(down, tok1[...])], axis=1)
+    both = dot(down, tokens[...])
     for b in range(SHARD_BLOCKS):
         request = meta[META_REQUEST + meta[0] * SHARD_BLOCKS + b]
         at = slice(b * BLOCK, (b + 1) * BLOCK)
@@ -396,38 +411,38 @@
     copies = []
     for i, (w, buf) in enumerate(zip(weights, buffers)):
         lanes = lane if i < 2 else slice(None)
-        pair = []
         for n, part in enumerate((chip + meta[1], chip + 1 - meta[1])):
             rows = pl.ds(pl.multiple_of(part * width, 16), width)
-            pair.append(pltpu.make_async_copy(w.at[rows, lanes], buf.at[n], sems.at[i, n]))
-        copies.append(pair)
-    for pair in copies:
-        for copy in pair:
-            copy.start()
+            copies.append(pltpu.make_async_copy(w.at[rows, lanes], buf.at[n], sems.at[i, n]))
     return copies
 
 
 WEIGHT_AT = (slice(0, 256), slice(256, 512), slice(512, 1024))
 
 
-def near_kernel(meta, own0, own1, other, wq, wk, wv, *refs):
-    outs, buffers, sems = refs[:-4], refs[-4:-1], refs[-1]
-    copies = weight_copies(meta, (wk, wv, wq), buffers, sems, meta[2] * 2, other.shape[0])
-    for at, pair, buf in zip(WEIGHT_AT, copies, buffers):
-        pair[0].wait()
-        pair[1].wait()
-        for c, out in enumerate(outs):
+def near_kernel(meta, own, other, wq, wk, wv, out0, out1, fk, fv, fq, bk, bv, bq, sems, far_sems):
+    weights = (wk, wv, wq)
+    width = other.shape[0]
+    copies = weight_copies(meta, weights, (bk, bv, bq), sems, meta[2] * 2, width)
+    later = weight_copies(meta, weights, (fk, fv, fq), far_sems, (1 - meta[2]) * 2, width)
+    for copy in copies:
+        copy.start()
+    for i, (at, buf) in enumerate(zip(WEIGHT_AT, (bk, bv, bq))):
+        copies[2 * i].wait()
+        copies[2 * i + 1].wait()
+        if i == 1:
+            for copy in later:
+                copy.start()
+        for c, out in enumerate((out0, out1)):
             tok = slice(c * CHUNK, (c + 1) * CHUNK)
-            out[:, at] = dot_t((own0, own1)[c][...], buf[0]) + dot_t(other[:, tok], buf[1])
-
-
-def far_kernel(meta, part, own, other, wq, wk, wv, q_out, kv_out, *refs):
-    buffers, sems = refs[:-1], refs[-1]
-    copies = weight_copies(meta, (wk, wv, wq), buffers, sems, (1 - meta[2]) * 2, own.shape[0])
-    for i, (at, pair, buf) in enumerate(zip(WEIGHT_AT, copies, buffers)):
-        pair[0].wait()
-        pair[1].wait()
-        turned = jnp.transpose(part[:, at] + dot_t(own[...], buf[0]) + dot_t(other[...], buf[1]))
+            out[:, at] = dot_t(own[:, tok], buf[0]) + dot_t(other[:, tok], buf[1])
+    for copy in later:
+        copy.wait()
+
+
+def far_kernel(part, own, other, wk, wv, wq, q_out, kv_out):
+    for i, (at, w) in enumerate(zip(WEIGHT_AT, (wk, wv, wq))):
+        turned = jnp.transpose(part[:, at] + dot_t(own[...], w[0]) + dot_t(other[...], w[1]))
         if i == 2:
             q_out[...] = turned
         else:
@@ -456,11 +471,15 @@
     return jnp.concatenate([a * cosine - b * sine, b * cosine + a * sine], axis=0)
 
 
-def finish_keys(meta, chunks, low_k, low_v, ups, gain, cosine, sine, keys, values, first):
+def gain_rows(gain):
+    return jnp.transpose(jnp.broadcast_to(gain[...], (HEAD_SIZE, HEAD_SIZE)))
+
+
+def finish_keys(meta, chunks, low_k, low_v, ups, gain, cosine, sine, keys, values, first, blocks):
     base = (meta[0] - 2) * SHARD_BLOCKS + first
     k_term = dot_t(ups[:, 512:768], by_request(meta, low_k, base))
     v_term = dot_t(ups[:, 768:1024], by_request(meta, low_v, base))
-    for b in range(SHARD_BLOCKS):
+    for b in blocks:
         at = slice((first + b) * BLOCK, (first + b + 1) * BLOCK)
         here = slice(b * BLOCK, (b + 1) * BLOCK)
         chunk = chunks[b // CHUNK_BLOCKS]
@@ -470,11 +489,14 @@
             k = chunk[head, lanes].astype(F32) + adapter_scale * k_term[head, here]
             k = k.astype(BF16).astype(F32)
             turned = norm_rotate(k, gain, cosine[:, at], sine[:, at])
-            keys[at, head] = jnp.transpose(turned).astype(BF16)
-        values[:, at] = (chunk[256:512, lanes].astype(F32) + adapter_scale * v_term[:, here]).astype(BF16)
-
-
-def attend(meta, q, keys, values, c, g, low_block, high_block):
+            keys[here, head] = jnp.transpose(turned).astype(BF16)
+        values[:, here] = (chunk[256:512, lanes].astype(F32) + adapter_scale * v_term[:, here]).astype(BF16)
+
+
+def attend(meta, q_rot, keys, values, c, g, first, low_block, high_block):
+    rows = slice(c * BLOCK, (c + 1) * BLOCK)
+    heads = [slice((2 * g + h) * HEAD_SIZE, (2 * g + h + 1) * HEAD_SIZE) for h in range(2)]
+    q = jnp.concatenate([q_rot[head, rows] for head in heads], axis=1)
     base = (meta[0] - 2) * SHARD_BLOCKS
     mine = block_request(meta, base + 8 + c)
     head = slice(g * HEAD_SIZE, (g + 1) * HEAD_SIZE)
@@ -485,13 +507,13 @@
     den = jnp.zeros((BLOCK, 2 * BLOCK), F32)
     pieces = []
     for j in range(low_block, high_block + 1):
-        block = base + j
+        block = base + first + j
         ok = jnp.logical_and(block >= 0, block_request(meta, block) == mine)
         piece = jnp.exp(scores[(j - low_block) * BLOCK : (j - low_block + 1) * BLOCK])
         piece = piece * jnp.where(ok, 1.0, 0.0).astype(F32)
-        if j == c + 8:
+        if first + j == c + 8:
             piece = jnp.where(query >= key, piece, 0.0)
-        if j == c:
+        if first + j == c:
             piece = jnp.where(query < key, piece, 0.0)
         den = den + piece
         pieces.append(piece.astype(BF16))
@@ -499,13 +521,16 @@
     return num, jnp.sum(den, axis=0, keepdims=True)
 
 
-def attend_near_kernel(
-    meta, q0, q1, o0, o1, h0, h1, low, low_h, ups, q_gain, k_gain, cosine, sine,
-    q_rot, num_out, den_out, keys, values,
+def attend_own_kernel(
+    meta, q0, q1, o0, o1, low, ups, q_gain, k_gain, cosine, sine, weights,
+    q_rot, num_out, den_out, weights_out, keys, values, sem,
 ):
-    gain = k_gain[...]
-    finish_keys(meta, (o0, o1), low[32:64, :], low[64:96, :], ups, gain, cosine, sine, keys, values, 8)
-    finish_keys(meta, (h0, h1), low_h[0:32, :], low_h[32:64, :], ups, gain, cosine, sine, keys, values, 4)
+    fetch = pltpu.make_async_copy(weights, weights_out, sem)
+    fetch.start()
+    finish_keys(
+        meta, (o0, o1), low[32:64, :], low[64:96, :], ups, gain_rows(k_gain), cosine, sine, keys, values, 8, range(4)
+    )
+    gain = gain_rows(q_gain)
     q_term = dot_t(ups[:, 0:512], by_request(meta, low[0:32, :], meta[0] * SHARD_BLOCKS))
     for c in range(SHARD_BLOCKS):
         q = (q0, q1)[c // CHUNK_BLOCKS]
@@ -515,86 +540,92 @@
         for h in range(4):
             head = slice(h * HEAD_SIZE, (h + 1) * HEAD_SIZE)
             x = q[head, lanes] + adapter_scale * q_term[head, rows]
-            q_rot[head, rows] = (norm_rotate(x, q_gain[...], cosine[:, at], sine[:, at]) * score_scale).astype(BF16)
+            q_rot[head, rows] = (norm_rotate(x, gain, cosine[:, at], sine[:, at]) * score_scale).astype(BF16)
     for g in range(2):
         for c in range(SHARD_BLOCKS):
             rows = slice(c * BLOCK, (c + 1) * BLOCK)
-            heads = [slice((2 * g + h) * HEAD_SIZE, (2 * g + h + 1) * HEAD_SIZE) for h in range(2)]
-            q = jnp.concatenate([q_rot[head, rows] for head in heads], axis=1)
-            num, den = attend(meta, q, keys, values, c, g, max(4, c + 1), c + 8)
+            num, den = attend(meta, q_rot, keys, values, c, g, 8, 0, c)
             for h in range(2):
+                n = 2 * g + h
                 part = slice(h * BLOCK, (h + 1) * BLOCK)
-                num_out[heads[h], rows] = num[:, part]
-                den_out[2 * g + h : 2 * g + h + 1, rows] = den[:, part]
-
-
-def attend_far_kernel(
-    meta, q_rot, num_in, den_in, h0, h1, low_h, ups, k_gain, cosine, sine, p0, p1, p2, p3, out, keys, values, panel
+                num_out[n * HEAD_SIZE : (n + 1) * HEAD_SIZE, rows] = num[:, part]
+                den_out[n : n + 1, rows] = den[:, part]
+    fetch.wait()
+
+
+def attend_prev_kernel(
+    meta, q_rot, num_in, den_in, h0, h1, low_h, ups, k_gain, cosine, sine, num_out, den_out, keys, values
 ):
-    place_quarters(meta, (p0, p1, p2, p3), panel)
-    cols = q_rot.shape[0]
-    out[cols : cols + 64, :] = jnp.concatenate([panel[j, :, 1408:1920] for j in range(4)], axis=0)
     finish_keys(
-        meta, (h0, h1), low_h[0:32, :], low_h[32:64, :], ups, k_gain[...], cosine, sine, keys, values, 0
+        meta, (h0, h1), low_h[0:32, :], low_h[32:64, :], ups, gain_rows(k_gain), cosine, sine, keys, values, 4, range(4)
     )
     for g in range(2):
         for c in range(SHARD_BLOCKS):
             rows = slice(c * BLOCK, (c + 1) * BLOCK)
-            heads = [slice((2 * g + h) * HEAD_SIZE, (2 * g + h + 1) * HEAD_SIZE) for h in range(2)]
-            q = jnp.concatenate([q_rot[head, rows] for head in heads], axis=1)
-            num, den = attend(meta, q, keys, values, c, g, c, 3)
+            num, den = attend(meta, q_rot, keys, values, c, g, 4, 0, 3)
             for h in range(2):
+                n = 2 * g + h
                 part = slice(h * BLOCK, (h + 1) * BLOCK)
-                total = den_in[2 * g + h : 2 * g + h + 1, rows] + den[:, part]
-                out[heads[h], rows] = ((num_in[heads[h], rows] + num[:, part]) / total).astype(BF16)
-
-
-def out_copies(meta, w, buf, sems, chip, depth):
-    rows = w.shape[0] // 2
-    copies = []
-    for half in range(2):
-        at = slice(half * rows, (half + 1) * rows)
-        pair = []
-        for n, p in enumerate((chip + meta[1], chip + 1 - meta[1])):
-            lanes = pl.ds(pl.multiple_of(p * depth, BLOCK), depth)
-            pair.append(pltpu.make_async_copy(w.at[at, lanes], buf.at[n, at, :], sems.at[half, n]))
-            pair[-1].start()
-        copies.append((at, pair))
-    return copies
-
-
-def out_near_kernel(meta, own, other, w, part, low, buf, sems):
-    cols = own.shape[1]
-    copies = out_copies(meta, w, buf, sems, meta[2] * 2, cols)
-    mine = own[0:cols, :]
-    theirs = other[0:cols, :]
-    low[...] = dot(own[cols : cols + 64, :], mine) + dot(other[cols : cols + 64, :], theirs)
-    for at, pair in copies:
-        pair[0].wait()
-        pair[1].wait()
-        part[at, :] = dot(buf[0, at, :], mine) + dot(buf[1, at, :], theirs)
-
-
-def out_far_kernel(meta, own, other, w, part, low, p0, p1, p2, p3, out, panel, buf, sems):
-    copies = out_copies(meta, w, buf, sems, (1 - meta[2]) * 2, own.shape[1])
-    place_quarters(meta, (p0, p1, p2, p3), panel)
-    cols = own.shape[1]
-    mine = own[0:cols, :]
-    theirs = other[0:cols, :]
-    lows = low[...] + dot(own[cols : cols + 64, :], mine) + dot(other[cols : cols + 64, :], theirs)
-    lows = lows.astype(BF16).astype(F32)
+                head = slice(n * HEAD_SIZE, (n + 1) * HEAD_SIZE)
+                num_out[head, rows] = num_in[head, rows] + num[:, part]
+                den_out[n : n + 1, rows] = den_in[n : n + 1, rows] + den[:, part]
+
+
+def attend_far_kernel(chunk, meta, q_rot, num_in, den_in, *refs):
+    count = CHUNK_BLOCKS - chunk
+    kept, (low_h, ups, k_gain, cosine, sine, out, keys, values) = refs[:count], refs[count:]
+    blocks = range(chunk * CHUNK_BLOCKS, SHARD_BLOCKS)
+    finish_keys(
+        meta, (None,) * chunk + tuple(kept), low_h[0:32, :], low_h[32:64, :], ups, gain_rows(k_gain), cosine, sine,
+        keys, values, 0, blocks,
+    )
+    for g in range(2):
+        for c in range(chunk * CHUNK_BLOCKS, (chunk + 1) * CHUNK_BLOCKS):
+            rows = slice(c * BLOCK, (c + 1) * BLOCK)
+            here = slice(c % CHUNK_BLOCKS * BLOCK, (c % CHUNK_BLOCKS + 1) * BLOCK)
+            num, den = attend(meta, q_rot, keys, values, c, g, 0, c, 3)
+            for h in range(2):
+                n = 2 * g + h
+                part = slice(h * BLOCK, (h + 1) * BLOCK)
+                head = slice(n * HEAD_SIZE, (n + 1) * HEAD_SIZE)
+                total = den_in[n : n + 1, rows] + den[:, part]
+                out[head, here] = ((num_in[head, rows] + num[:, part]) / total).astype(BF16)
+
+
+def request_flag(meta):
     flags = []
     for b in range(SHARD_BLOCKS):
         request = block_request(meta, meta[0] * SHARD_BLOCKS + b)
         flags.append(jnp.full((1, BLOCK), jnp.where(request == 0, 1.0, 0.0).astype(F32)))
-    flag = jnp.concatenate(flags, axis=1)
-    chosen = jnp.concatenate([lows[0:32] * flag, lows[32:64] * (1.0 - flag)], axis=0).astype(BF16)
-    up = jnp.concatenate([panel[j, :, 0 : w.shape[0]] for j in range(4)], axis=0)
-    for at, pair in copies:
-        total = part[at, :] + adapter_scale * dot_t(up[:, at], chosen)
-        pair[0].wait()
-        pair[1].wait()
-        out[at, :] = (total + dot(buf[0, at, :], mine) + dot(buf[1, at, :], theirs)).astype(BF16)
+    return jnp.concatenate(flags, axis=1)
+
+
+def out_low_kernel(meta, att0, att1, panel_a, panel_b, low):
+    down = panel_a[:, 1408:1920] + panel_b[:, 1408:1920]
+    both = jnp.concatenate([dot(down, att0[...]), dot(down, att1[...])], axis=1)
+    flag = request_flag(meta)
+    low[...] = both[0:32] * flag + both[32:64] * (1.0 - flag)
+
+
+def part_lanes(meta, chip, cols):
+    return [pl.ds(pl.multiple_of(p * cols, BLOCK), cols) for p in (chip + meta[1], chip + 1 - meta[1])]
+
+
+def out_near_kernel(meta, own, other, w, part):
+    first, second = part_lanes(meta, meta[2] * 2, own.shape[0])
+    part[...] = dot(w[:, first], own[...]) + dot(w[:, second], other[...])
+
+
+def out_far_kernel(chunk, meta, own, other, w, part, low, panel_a, panel_b, *refs):
+    out = refs[-1]
+    tok = slice(chunk * CHUNK, (chunk + 1) * CHUNK)
+    lows = low[:, tok].astype(BF16).astype(F32)
+    flag = request_flag(meta)[:, tok]
+    chosen = jnp.concatenate([lows * flag, lows * (1.0 - flag)], axis=0).astype(BF16)
+    up = panel_a[:, 0 : w.shape[0]] + panel_b[:, 0 : w.shape[0]]
+    first, second = part_lanes(meta, (1 - meta[2]) * 2, own.shape[0])
+    total = part[...] + adapter_scale * dot_t(up, chosen)
+    out[...] = (total + dot(w[:, first], own[...]) + dot(w[:, second], other[...])).astype(BF16)
 
 
 def exchange_quarters(quarters):
@@ -602,8 +633,9 @@
 
 
 def share_quarter(total):
-    pairs = ([(0, 1), (1, 0), (2, 3), (3, 2)], [(1, 2), (2, 1)], [(0, 2), (3, 1)])
-    return [total] + [lax.ppermute(total, "seq", pair) for pair in pairs]
+    beside = lax.ppermute(total, "seq", [(j, j ^ 1) for j in range(4)])
+    middle = [(1, 2), (2, 1)]
+    return [total, beside, lax.ppermute(total, "seq", middle), lax.ppermute(beside, "seq", middle)]
 
 
 def per_device(
@@ -640,25 +672,31 @@
     def after(value, *others):
         return lax.optimization_barrier((value, *others))[0]
 
-    down_pool = jnp.swapaxes(adapter_down, 1, 2)
-    quarters = call(
-        pack_kernel,
-        "pack",
-        (shape((64, width)),) * 4,
-        [SM, FAR, FAR, FAR],
-        [meta, down_pool, adapter_up_query, key_value_up_panels],
-        [pltpu.VMEM(a.shape, BF16) for a in (down_pool, adapter_up_query, key_value_up_panels)]
-        + [pltpu.SemaphoreType.DMA((3,))],
-    )
+    far_own = across(tokens)
+    near_other = core(tokens)
+
+    def swapped(value, by):
+        return lax.ppermute(value, "seq", [(j, j ^ by) for j in range(4)])
+
+    def pack(kernel, name, result, pools, order):
+        return call(
+            kernel,
+            name,
+            result,
+            [SM] + [FAR] * len(pools),
+            [adapter_of_request, *pools],
+            [pltpu.VMEM(pool.shape, BF16) for pool in pools] + [pltpu.SemaphoreType.DMA((len(pools),))],
+            after=order,
+        )
+
+    pools = [jnp.swapaxes(adapter_down, 1, 2), adapter_up_query, key_value_up_panels]
+    quarters = pack(pack_kernel, "pack", (shape((64, width)),) * 4, pools, [])
     received = exchange_quarters(quarters)
+    out_pools = [jnp.swapaxes(adapter_out_down, 1, 2), adapter_out_up]
+    out_panel = pack(pack_out_kernel, "pack_out", shape((64, 1920)), out_pools, [quarters[0]])
+    out_beside = swapped(out_panel, 1)
 
     chunks = rows // CHUNK
-    token_chunks = call(
-        split_kernel, "split", (shape((width, CHUNK)),) * chunks, [VM], [tokens], after=[quarters[0]]
-    )
-    far_own = [across(chunk) for chunk in token_chunks]
-    near_other = core(tokens)
-
     weights = [query_matrix, key_matrix, value_matrix]
     weight_scratch = [
         pltpu.VMEM((2, width, 256), BF16),
@@ -666,31 +704,29 @@
         pltpu.VMEM((2, width, cols), BF16),
         pltpu.SemaphoreType.DMA((3, 2)),
     ]
-    near = call(
+    weight_shapes = [(2, width, 256), (2, width, 256), (2, width, cols)]
+    near0, near1, *far_weights = call(
         near_kernel,
         "near",
-        (shape((CHUNK, 1024), F32),) * chunks,
-        [SM, VM, VM, VM, FAR, FAR, FAR],
-        [meta, *token_chunks, near_other, *weights],
-        weight_scratch,
-        after=[quarters[0]],
-    )
+        (shape((CHUNK, 1024), F32),) * chunks + tuple(shape(dims) for dims in weight_shapes),
+        [SM, VM, VM, FAR, FAR, FAR],
+        [meta, tokens, near_other, *weights],
+        [pltpu.VMEM(dims, BF16) for dims in weight_shapes] + [pltpu.SemaphoreType.DMA((3, 2))] * 2,
+        after=[out_panel],
+    )
+    near = [near0, near1]
 
     def project(c, prior):
+        mine = pl.BlockSpec((width, CHUNK), lambda i: (0, c))
         return call(
             far_kernel,
             "far",
             (shape((cols, CHUNK), F32), shape((512, CHUNK))),
-            [SM, VM, VM, VM, FAR, FAR, FAR],
-            [meta, near[c], far_own[c], core(after(far_own[c], prior)), *weights],
-            weight_scratch,
+            [VM, mine, mine, VM, VM, VM],
+            [near[c], far_own, far_other, *far_weights],
+            grid=(1,),
             after=[prior],
         )
-
-    quarter = call(sum_kernel, "sum", shape((64, width)), [VM] * 4, received, after=[near[0]])
-    pieces = share_quarter(quarter)
-
-    first_q, first_kv = project(0, quarter)
 
     all_blocks = request_of_block.shape[0]
     window = jnp.arange(3 * rows, dtype=jnp.int32) + (seq - 2) * rows
@@ -701,80 +737,102 @@
     frequency = jnp.power(rope_base, -jnp.arange(half_dim, dtype=F32) * 2.0 / HEAD_SIZE)
     angles = frequency[:, None] * position.astype(F32)[None, :]
     cosine, sine = jnp.cos(angles), jnp.sin(angles)
-    q_gain = query_gain.reshape(HEAD_SIZE, 1)
-    k_gain = key_norm_gain.reshape(HEAD_SIZE, 1)
-
-    out_quarters = call(
-        pack_out_kernel,
-        "pack_out",
-        (shape((16, 1920)),) * 4,
-        [SM, VM, VM],
-        [meta, jnp.swapaxes(adapter_out_down, 1, 2), adapter_out_up],
-        after=[first_kv],
-    )
-    out_received = exchange_quarters(out_quarters)
-
+    q_gain = query_gain.reshape(1, HEAD_SIZE)
+    k_gain = key_norm_gain.reshape(1, HEAD_SIZE)
+
+    quarter = call(sum_kernel, "sum", shape((64, width)), [VM] * 4, received, after=[near[0], cosine, sine])
+    pieces = share_quarter(quarter)
+    far_other = core(after(far_own, pieces[1], pieces[2]))
+    late_q, late_kv = project(1, pieces[1])
     partial_low, ups = call(
         low_kernel,
         "low",
         (shape((96, rows), F32), shape((64, 1024))),
-        [SM] + [VM] * 6,
-        [meta, *token_chunks, *pieces],
+        [SM] + [VM] * 5,
+        [meta, tokens, *pieces],
         [pltpu.VMEM((4, 64, width), BF16)],
-        after=[first_kv],
+        after=[late_kv],
     )
     chip_low = partial_low + core(partial_low)
     low = chip_low + across(chip_low)
-    second_q, second_kv = project(1, chip_low)
-    own_kv = [first_kv, second_kv]
-    kv_prev = [up(kv) for kv in own_kv]
-    kv_prev2 = [up(after(kv_prev[0], chip_low)), up(kv_prev[1])]
+    early_q, early_kv = project(0, chip_low)
+
+    prev_late, prev_early = up(late_kv), up(early_kv)
     low_kv = low[32:96].astype(BF16)
     low_prev = up(low_kv)
     low_prev2 = up(low_kv, 2)
-
-    out_quarter = call(sum_kernel, "out_sum", shape((16, 1920)), [VM] * 4, out_received, after=[second_kv])
-    out_pieces = share_quarter(out_quarter)
-
-    window_scratch = [pltpu.VMEM((3 * rows, 256), BF16), pltpu.VMEM((256, 3 * rows), BF16)]
-    q_rot, num, den = call(
-        attend_near_kernel,
-        "attend_near",
-        (shape((cols, rows)), shape((cols, rows), F32), shape((8, rows), F32)),
-        [SM] + [VM] * 13,
-        [meta, first_q, second_q, *own_kv, *kv_prev, low, low_prev, ups, q_gain, k_gain, cosine, sine],
-        window_scratch,
-    )
-    attended = call(
-        attend_far_kernel,
-        "attend_far",
-        shape((cols + 64, rows)),
-        [SM] + [VM] * 14,
-        [meta, q_rot, num, den, *kv_prev2, low_prev2, ups, k_gain, cosine, sine, *out_pieces],
-        window_scratch + [pltpu.VMEM((4, 16, 1920), BF16)],
-    )
-
-    att_far = across(attended)
-    att_core = core(attended)
-    att_far_core = core(att_far)
-    out_weights = output_matrix.T
-    out_scratch = [pltpu.VMEM((2, width, cols), BF16), pltpu.SemaphoreType.DMA((2, 2))]
-    out_part, out_low = call(
-        out_near_kernel,
-        "out_near",
-        (shape((width, rows), F32), shape((64, rows), F32)),
-        [SM, VM, VM, FAR],
-        [meta, attended, att_core, out_weights],
-        out_scratch,
-    )
-    return call(
-        out_far_kernel,
-        "out_far",
-        shape((width, rows)),
-        [SM, VM, VM, FAR] + [VM] * 6,
-        [meta, att_far, att_far_core, out_weights, out_part, out_low, *out_pieces],
-        [pltpu.VMEM((4, 16, 1920), BF16)] + out_scratch,
-    ).T
+    prev2_late = up(after(prev_late, early_kv))
+
+    shard_scratch = [pltpu.VMEM((rows, 256), BF16), pltpu.VMEM((256, rows), BF16)]
+    sums = (shape((cols, rows), F32), shape((8, rows), F32))
+    q_rot, num, den, out_weights = call(
+        attend_own_kernel,
+        "attend_own",
+        (shape((cols, rows)), *sums, shape(output_matrix.T.shape)),
+        [SM] + [VM] * 10 + [FAR],
+        [meta, early_q, late_q, early_kv, late_kv, low, ups, q_gain, k_gain, cosine, sine, output_matrix.T],
+        shard_scratch + [pltpu.SemaphoreType.DMA],
+    )
+    prev2_early = up(after(prev_early, low_prev, low_prev2, num))
+    num, den = call(
+        attend_prev_kernel,
+        "attend_prev",
+        sums,
+        [SM] + [VM] * 10,
+        [meta, q_rot, num, den, prev_early, prev_late, low_prev, ups, k_gain, cosine, sine],
+        shard_scratch,
+    )
+
+    def attend_far(chunk, kept, order):
+        return call(
+            functools.partial(attend_far_kernel, chunk),
+            "attend_far",
+            shape((cols, CHUNK)),
+            [SM] + [VM] * (8 + len(kept)),
+            [meta, q_rot, num, den, *kept, low_prev2, ups, k_gain, cosine, sine],
+            shard_scratch,
+            after=order,
+        )
+
+    att_late = attend_far(1, [prev2_late], [])
+    att_early = attend_far(0, [prev2_early, prev2_late], [att_late])
+
+    out_pair = call(add_kernel, "out_add", shape((64, 1920)), [VM] * 2, [out_panel, out_beside], after=[early_kv])
+    out_rest = swapped(out_pair, 2)
+    out_low = call(
+        out_low_kernel,
+        "out_low",
+        shape((32, rows), F32),
+        [SM] + [VM] * 4,
+        [meta, att_early, att_late, out_pair, out_rest],
+    )
+    out_low = out_low + core(out_low)
+    out_low = out_low + across(out_low)
+
+    result = []
+    for chunk, att in ((1, att_late), (0, att_early)):
+        att_far = across(att)
+        part = call(
+            out_near_kernel,
+            "out_near",
+            shape((width, CHUNK), F32),
+            [SM] + [VM] * 3,
+            [meta, att, core(att), out_weights],
+            after=[att_early],
+        )
+        result = [
+            call(
+                functools.partial(out_far_kernel, chunk),
+                "out_far",
+                shape((width, rows)),
+                [SM] + [VM] * 7 + [HB] * len(result),
+                [meta, att_far, core(att_far), out_weights, part, out_low, out_pair, out_rest, *result],
+                out_specs=pl.BlockSpec((width, CHUNK), lambda i, chunk=chunk: (0, chunk)),
+                grid=(1,),
+                aliases={8: 0} if result else {},
+            )
+        ]
+    return result[0].T
 
 
 def plain_sizes(mesh):

time: 129 us -> 110 us (0.85)
  Pallas kernels: 48.6 us -> 38 us
  local copies, waits for them, and re-layouts: 14.2 us -> 3.98 us
  waiting for transfers between devices: 28.6 us -> 31.9 us
    pallas_call x13 -> x17, Pallas kernels: 48.6 us -> 38 us  [call(): pl.pallas_call(body, out_shape=out_shape, in_specs=list(in_specs) + [HB]...]
    ppermute x6 -> x3, waiting for transfers between devices: 9.33 us -> 0.01 us  [exchange_quarters(): lax.ppermute(quarters[s], 'seq', [(j, j ^ s) for j in range(4)])]
    unnamed x66 -> x24, local copies, waits for them, and re-layouts: 12.6 us -> 3.89 us
    ppermute x6, starting transfers between devices: 4.93 us -> 13 us  [up(): return lax.ppermute(value, 'seq', [(i, (i + by) % 4) for i in range(4)])]
    ppermute x6 -> x5, waiting for transfers between devices: 0.02 us -> 7.24 us  [the longest x2 7.24 us: swapped(): return lax.ppermute(value, 'seq', [(j, j ^ by) for j in range(4)])]
    ppermute x6 -> x3, starting transfers between devices: 9.81 us -> 4.39 us  [exchange_quarters(): lax.ppermute(quarters[s], 'seq', [(j, j ^ s) for j in range(4)])]
    ppermute x6 -> x5, starting transfers between devices: 10.7 us -> 5.35 us  [the longest x1 2.6 us: share_quarter(): beside = lax.ppermute(total, 'seq', [(j, j ^ 1) for j in range(4)])]
    ppermute x4 -> x5, waiting for transfers between devices: 8.76 us -> 11 us  [across(): return lax.ppermute(value, 'head', SWAP)]
  transfers between devices with their start and end apart: 28 -> 27, of which waited for: 7 -> 9; matrix products, arithmetic and copies ran while one was open for 4% -> 3% of each run, Pallas kernels for 30% -> 31%
where the time goes in v2:
time: 110 us
  Pallas kernels  38 us (35%)
  waiting for transfers between devices  31.9 us (29%)
  starting transfers between devices  31.8 us (29%)
  local copies, waits for them, and re-layouts  3.98 us (4%)
  other arithmetic  2.82 us (3%)
    pallas_call x17, Pallas kernels, call(): pl.pallas_call(body, out_shape=out_shape, in_specs=list(in_specs) + [HB]...  38 us
    ppermute x6, starting transfers between devices, up(): return lax.ppermute(value, 'seq', [(i, (i + by) % 4) for i in range(4)])  13 us
    ppermute x5, waiting for transfers between devices, across(): return lax.ppermute(value, 'head', SWAP)  11 us
    ppermute x6, waiting for transfers between devices, up(): return lax.ppermute(value, 'seq', [(i, (i + by) % 4) for i in range(4)])  9.94 us
    ppermute x5, starting transfers between devices, across(): return lax.ppermute(value, 'head', SWAP)  7.81 us
    ppermute x2, waiting for transfers between devices, swapped(): return lax.ppermute(value, 'seq', [(j, j ^ by) for j in range(4)])  7.24 us
    ppermute x3, starting transfers between devices, exchange_quarters(): lax.ppermute(quarters[s], 'seq', [(j, j ^ s) for j in range(4)])  4.39 us
    unnamed x24, local copies, waits for them, and re-layouts  3.89 us
  transfers between devices with their start and end apart: 27, of which 9 were waited for; matrix products, arithmetic and copies ran while one was open for 3% of the time, Pallas kernels for 31%

profile of v2, /device:TPU:0, one launch (start us, length us, event | category | flops | bytes accessed | tf_op | source)
XLA Modules:
  0.0 109.6 jit_solution(6063709818570193774)
XLA Ops:
  0.5 2.5 %collective-permute-start.1 = (bf16[1344,512]{1,0:T(8,128)(2,1)}, bf16[1344,512]{1,0:T(8,128)(2,1)S(1)}, u32[]{:S(2)}, u32[]{:S(2)}) collective-permute-start(bf16[1344,512]{1,0:T(8,128)(2,1)} %bitcast.11), channel_id=1, source_target_pairs={{0,2},{2,0},{1,3},{3,1},{4,6},{6,4},{5,7},{7,5},{8,10},{10,8},{9,1... | collective-permute-start | bytes 4128776 | tf_op jit(solution)/shard_map/ppermute | solution.py:664
  3.7 2.5 %pack.1 = (bf16[64,1344]{1,0:T(8,128)(2,1)S(1)}, bf16[64,1344]{1,0:T(8,128)(2,1)}, bf16[64,1344]{1,0:T(8,128)(2,1)}, bf16[64,1344]{1,0:T(8,128)(2,1)}) custom-call(s32[2]{0:T(128)S(1)} %copy-done.8, bf16[2,96,1344]{2,1,0:T(8,128)(2,1)} %bitcast.20, bf16[2,32,512]{2,1,0:T(8,128)(2,1)} %refs_2_.2, bf16[2,2,32,512]{3,2,1,0:T(8,128)(2,1)} %refs_3_.2), custom_call_target="tpu_custom_call" | custom-call | flops 1000 | bytes 1000 | tf_op jit(solution)/shard_map/pack/pallas_call | solution.py:312
  6.8 1.6 %collective-permute-start.2 = (bf16[64,1344]{1,0:T(8,128)(2,1)}, bf16[64,1344]{1,0:T(8,128)(2,1)}, u32[]{:S(2)}, u32[]{:S(2)}) collective-permute-start(bf16[64,1344]{1,0:T(8,128)(2,1)} %get-tuple-element.31), channel_id=1, source_target_pairs={{0,4},{4,0},{8,12},{12,8},{1,5},{5,1},{9,13},{13,9},{2,6},{6,2},{1... | collective-permute-start | bytes 516104 | tf_op jit(solution)/shard_map/ppermute | solution.py:632
  8.4 2.6 %collective-permute-start.3 = (bf16[64,1344]{1,0:T(8,128)(2,1)}, bf16[64,1344]{1,0:T(8,128)(2,1)}, u32[]{:S(2)}, u32[]{:S(2)}) collective-permute-start(bf16[64,1344]{1,0:T(8,128)(2,1)} %get-tuple-element.32), channel_id=1, source_target_pairs={{0,8},{4,12},{8,0},{12,4},{1,9},{5,13},{9,1},{13,5},{2,10},{6,14},... | collective-permute-start | bytes 516104 | tf_op jit(solution)/shard_map/ppermute | solution.py:632
  13.2 1.4 %multiply_sine_fusion = (f32[64,1536]{1,0:T(8,128)S(1)}, f32[64,1536]{1,0:T(8,128)S(1)}) fusion(f32[1536]{0:T(1024)S(1)} %fusion, f32[64]{0:T(128)S(1)} %multiply_power_fusion), kind=kLoop, calls=%fused_computation | loop fusion | flops 98304 | bytes 792832 | tf_op jit(solution)/shard_map/sin | solution.py:739
  15.6 1.6 %pack_out.1.refs_6_.refs_0_ = bf16[64,1920]{1,0:T(8,128)(2,1)S(1)} custom-call(s32[2]{0:T(128)S(1)} %copy-done.9, bf16[2,32,512]{2,1,0:T(8,128)(2,1)} %bitcast.21, bf16[2,32,1344]{2,1,0:T(8,128)(2,1)} %refs_2_.3, bf16[64,1344]{1,0:T(8,128)(2,1)S(1)} %copy-done.5), custom_call_target="tpu_custom_call" | custom-call | flops 1000 | bytes 1000 | tf_op jit(solution)/shard_map/pack_out/pallas_call | solution.py:312
  18.9 6.7 %near.1 = (f32[256,1024]{1,0:T(8,128)S(1)}, f32[256,1024]{1,0:T(8,128)S(1)}, bf16[2,1344,256]{2,1,0:T(8,128)(2,1)S(1)}, bf16[2,1344,256]{2,1,0:T(8,128)(2,1)S(1)}, bf16[2,1344,512]{2,1,0:T(8,128)(2,1)S(1)}) custom-call(s32[21]{0:T(128)S(1)} %concatenate.3.refs_0_, bf16[1344,512]{1,0:T(8,128)(2,1)S(1)} %bitcast.12, ...), custom_call_target="tpu_custom_call" | custom-call | flops 1000 | bytes 1000 | tf_op jit(solution)/shard_map/near/pallas_call | solution.py:312
  26.8 2.6 %collective-permute-start.5 = (bf16[64,1344]{1,0:T(8,128)(2,1)S(1)}, bf16[64,1344]{1,0:T(8,128)(2,1)S(1)}, u32[]{:S(2)}, u32[]{:S(2)}) collective-permute-start(bf16[64,1344]{1,0:T(8,128)(2,1)S(1)} %sum.1.refs_2_), channel_id=1, source_target_pairs={{0,4},{4,0},{8,12},{12,8},{1,5},{5,1},{9,13},{13,9},{2,6},{6,2},{1... | collective-permute-start | bytes 516104 | tf_op jit(solution)/shard_map/ppermute | solution.py:636
  30.0 4.0 %collective-permute-done.1.refs_1_ = bf16[1344,512]{1,0:T(8,128)(2,1)S(1)} collective-permute-done((bf16[1344,512]{1,0:T(8,128)(2,1)}, bf16[1344,512]{1,0:T(8,128)(2,1)S(1)}, u32[]{:S(2)}, u32[]{:S(2)}) %collective-permute-start.1) | collective-permute-done | bytes 1376288 | tf_op jit(solution)/shard_map/ppermute | solution.py:664
  34.7 2.4 %collective-permute-done.7.refs_2_ = bf16[1344,512]{1,0:T(8,128)(2,1)S(1)} collective-permute-done((bf16[1344,512]{1,0:T(8,128)(2,1)S(1)}, bf16[1344,512]{1,0:T(8,128)(2,1)S(1)}, u32[]{:S(2)}, u32[]{:S(2)}) %collective-permute-start.7) | collective-permute-done | bytes 1376288 | tf_op jit(solution)/shard_map/ppermute | solution.py:667
  37.1 2.0 %far.2 = (f32[512,256]{1,0:T(8,128)S(1)}, bf16[512,256]{1,0:T(8,128)(2,1)S(1)}) custom-call(f32[256,1024]{1,0:T(8,128)S(1)} %get-tuple-element.38.refs_0_, bf16[1344,512]{1,0:T(8,128)(2,1)S(1)} %collective-permute-done.1.refs_1_, bf16[1344,512]{1,0:T(8,128)(2,1)S(1)} %collective-permute-done.7.refs_2_, bf16[2,1344,256]{2,1,0:T(8,128)(2,1)S(1)} %get-tuple-element.35.refs_3_, ...), custom_call_target="tpu_custom_call" | custom-call | flops 1000 | bytes 1000 | tf_op jit(solution)/shard_map/far/pallas_call | solution.py:312
  40.5 6.8 %collective-permute-start.12 = (bf16[512,256]{1,0:T(8,128)(2,1)S(1)}, bf16[512,256]{1,0:T(8,128)(2,1)S(1)}, u32[]{:S(2)}, u32[]{:S(2)}) collective-permute-start(bf16[512,256]{1,0:T(8,128)(2,1)S(1)} %get-tuple-element.39.refs_6_.refs_4_), channel_id=1, source_target_pairs={{0,4},{4,8},{8,12},{12,0},{1,5},{5,9},{9,13},{13,1},{2,6},{6,10},{... | collective-permute-start | bytes 786440 | tf_op jit(solution)/shard_map/ppermute | solution.py:670
  47.9 2.0 %far.3 = (f32[512,256]{1,0:T(8,128)S(1)}, bf16[512,256]{1,0:T(8,128)(2,1)S(1)}) custom-call(f32[256,1024]{1,0:T(8,128)S(1)} %get-tuple-element.30.refs_4_.refs_0_, bf16[1344,512]{1,0:T(8,128)(2,1)S(1)} %collective-permute-done.1.refs_1_, bf16[1344,512]{1,0:T(8,128)(2,1)S(1)} %collective-permute-done.7.refs_2_, ...), custom_call_target="tpu_custom_call" | custom-call | flops 1000 | bytes 1000 | tf_op jit(solution)/shard_map/far/pallas_call | solution.py:312
  50.0 1.8 %collective-permute-start.11 = (bf16[512,256]{1,0:T(8,128)(2,1)S(1)}, bf16[512,256]{1,0:T(8,128)(2,1)S(1)}, u32[]{:S(2)}, u32[]{:S(2)}) collective-permute-start(bf16[512,256]{1,0:T(8,128)(2,1)S(1)} %get-tuple-element.43.refs_3_.refs_2_), channel_id=1, source_target_pairs={{0,4},{4,8},{8,12},{12,0},{1,5},{5,9},{9,13},{13,1},{2,6},{6,10},{... | collective-permute-start | bytes 786440 | tf_op jit(solution)/shard_map/ppermute | solution.py:670
  51.7 2.6 %collective-permute-done.10 = f32[96,512]{1,0:T(8,128)S(1)} collective-permute-done((f32[96,512]{1,0:T(8,128)S(1)}, f32[96,512]{1,0:T(8,128)S(1)}, u32[]{:S(2)}, u32[]{:S(2)}) %collective-permute-start.10) | collective-permute-done | bytes 196640 | tf_op jit(solution)/shard_map/ppermute | solution.py:664
  54.4 1.8 %collective-permute-start.13 = (bf16[64,512]{1,0:T(8,128)(2,1)S(1)}, bf16[64,512]{1,0:T(8,128)(2,1)S(1)}, u32[]{:S(2)}, u32[]{:S(2)}) collective-permute-start(bf16[64,512]{1,0:T(8,128)(2,1)S(1)} %slice.7), channel_id=1, source_target_pairs={{0,4},{4,8},{8,12},{12,0},{1,5},{5,9},{9,13},{13,1},{2,6},{6,10},{... | collective-permute-start | bytes 196616 | tf_op jit(solution)/shard_map/ppermute | solution.py:670
  57.1 1.8 %collective-permute-start.16 = (bf16[512,256]{1,0:T(8,128)(2,1)S(1)}, bf16[512,256]{1,0:T(8,128)(2,1)S(1)}, u32[]{:S(2)}, u32[]{:S(2)}) collective-permute-start(bf16[512,256]{1,0:T(8,128)(2,1)S(1)} %collective-permute-done.12.refs_5_), channel_id=1, source_target_pairs={{0,4},{4,8},{8,12},{12,0},{1,5},{5,9},{9,13},{13,1},{2,6},{6,10},{... | collective-permute-start | bytes 786440 | tf_op jit(solution)/shard_map/ppermute | solution.py:670
  58.9 5.0 %attend_own.1 = (bf16[512,512]{1,0:T(8,128)(2,1)S(1)}, f32[512,512]{1,0:T(8,128)S(1)}, f32[8,512]{1,0:T(8,128)S(1)}, bf16[1344,2048]{1,0:T(8,128)(2,1)S(1)}) custom-call(s32[21]{0:T(128)S(1)} %concatenate.3.refs_0_, f32[512,256]{1,0:T(8,128)S(1)} %get-tuple-element.41.refs_1_, f32[512,256]{1,0:T(8,128)S(1)} %get-tuple-element.42.refs_2_, ...), custom_call_target="tpu_custom_call" | custom-call | flops 1000 | bytes 1000 | tf_op jit(solution)/shard_map/attend_own/pallas_call | solution.py:312
  63.9 5.8 %collective-permute-done.14.refs_5_.refs_6_ = bf16[64,512]{1,0:T(8,128)(2,1)S(1)} collective-permute-done((bf16[64,512]{1,0:T(8,128)(2,1)S(1)}, bf16[64,512]{1,0:T(8,128)(2,1)S(1)}, u32[]{:S(2)}, u32[]{:S(2)}) %collective-permute-start.14) | collective-permute-done | bytes 65568 | tf_op jit(solution)/shard_map/ppermute | solution.py:670
  69.8 3.5 %attend_prev.1 = (f32[512,512]{1,0:T(8,128)S(1)}, f32[8,512]{1,0:T(8,128)S(1)}) custom-call(s32[21]{0:T(128)S(1)} %concatenate.3.refs_0_, bf16[512,512]{1,0:T(8,128)(2,1)S(1)} %get-tuple-element.45.refs_1_, f32[512,512]{1,0:T(8,128)S(1)} %get-tuple-element.46.refs_2_, f32[8,512]{1,0:T(8,128)S(1)} %get-tuple-element.47.refs_3_, ...), custom_call_target="tpu_custom_call" | custom-call | flops 1000 | bytes 1000 | tf_op jit(solution)/shard_map/attend_prev/pallas_call | solution.py:312
  73.4 1.7 %attend_far.2.refs_11_.refs_2_.refs_1_ = bf16[512,256]{1,0:T(8,128)(2,1)S(1)} custom-call(s32[21]{0:T(128)S(1)} %concatenate.3.refs_0_, bf16[512,512]{1,0:T(8,128)(2,1)S(1)} %get-tuple-element.45.refs_1_, f32[512,512]{1,0:T(8,128)S(1)} %get-tuple-element.48.refs_2_, f32[8,512]{1,0:T(8,128)S(1)} %get-tuple-element.49.refs_3_, ...), custom_call_target="tpu_custom_call" | custom-call | flops 1000 | bytes 1000 | tf_op jit(solution)/shard_map/attend_far/pallas_call | solution.py:312
  75.0 1.6 %collective-permute-start.24 = (bf16[512,256]{1,0:T(8,128)(2,1)S(1)}, bf16[512,256]{1,0:T(8,128)(2,1)S(1)}, u32[]{:S(2)}, u32[]{:S(2)}) collective-permute-start(bf16[512,256]{1,0:T(8,128)(2,1)S(1)} %attend_far.2.refs_11_.refs_2_.refs_1_), channel_id=1, source_target_pairs={{0,2},{2,0},{1,3},{3,1},{4,6},{6,4},{5,7},{7,5},{8,10},{10,8},{9,1... | collective-permute-start | bytes 786440 | tf_op jit(solution)/shard_map/ppermute | solution.py:664
  76.6 4.1 %collective-permute-done.15.refs_4_ = bf16[512,256]{1,0:T(8,128)(2,1)S(1)} collective-permute-done((bf16[512,256]{1,0:T(8,128)(2,1)S(1)}, bf16[512,256]{1,0:T(8,128)(2,1)S(1)}, u32[]{:S(2)}, u32[]{:S(2)}) %collective-permute-start.15) | collective-permute-done | bytes 262176 | tf_op jit(solution)/shard_map/ppermute | solution.py:670
  80.7 2.1 %attend_far.3.refs_1_.refs_4_ = bf16[512,256]{1,0:T(8,128)(2,1)S(1)} custom-call(s32[21]{0:T(128)S(1)} %concatenate.3.refs_0_, bf16[512,512]{1,0:T(8,128)(2,1)S(1)} %get-tuple-element.45.refs_1_, f32[512,512]{1,0:T(8,128)S(1)} %get-tuple-element.48.refs_2_, f32[8,512]{1,0:T(8,128)S(1)} %get-tuple-element.49.refs_3_, ...), custom_call_target="tpu_custom_call" | custom-call | flops 1000 | bytes 1000 | tf_op jit(solution)/shard_map/attend_far/pallas_call | solution.py:312
  82.8 1.6 %collective-permute-start.17 = (bf16[512,256]{1,0:T(8,128)(2,1)S(1)}, bf16[512,256]{1,0:T(8,128)(2,1)S(1)}, u32[]{:S(2)}, u32[]{:S(2)}) collective-permute-start(bf16[512,256]{1,0:T(8,128)(2,1)S(1)} %attend_far.3.refs_1_.refs_4_), channel_id=1, source_target_pairs={{0,2},{2,0},{1,3},{3,1},{4,6},{6,4},{5,7},{7,5},{8,10},{10,8},{9,1... | collective-permute-start | bytes 786440 | tf_op jit(solution)/shard_map/ppermute | solution.py:664
  86.2 3.1 %collective-permute-done.17.refs_1_ = bf16[512,256]{1,0:T(8,128)(2,1)S(1)} collective-permute-done((bf16[512,256]{1,0:T(8,128)(2,1)S(1)}, bf16[512,256]{1,0:T(8,128)(2,1)S(1)}, u32[]{:S(2)}, u32[]{:S(2)}) %collective-permute-start.17) | collective-permute-done | bytes 262176 | tf_op jit(solution)/shard_map/ppermute | solution.py:664
  89.3 7.2 %collective-permute-done.21.refs_4_.refs_7_ = bf16[64,1920]{1,0:T(8,128)(2,1)S(1)} collective-permute-done((bf16[64,1920]{1,0:T(8,128)(2,1)S(1)}, bf16[64,1920]{1,0:T(8,128)(2,1)S(1)}, u32[]{:S(2)}, u32[]{:S(2)}) %collective-permute-start.21) | collective-permute-done | bytes 245792 | tf_op jit(solution)/shard_map/ppermute | solution.py:679
  98.6 1.6 %collective-permute-start.23 = (f32[32,512]{1,0:T(8,128)S(1)}, f32[32,512]{1,0:T(8,128)S(1)}, u32[]{:S(2)}, u32[]{:S(2)}) collective-permute-start(f32[32,512]{1,0:T(8,128)S(1)} %add.27), channel_id=1, source_target_pairs={{0,2},{2,0},{1,3},{3,1},{4,6},{6,4},{5,7},{7,5},{8,10},{10,8},{9,1... | collective-permute-start | bytes 196616 | tf_op jit(solution)/shard_map/ppermute | solution.py:664
  100.2 1.4 %out_near.3.refs_4_ = f32[1344,256]{1,0:T(8,128)S(1)} custom-call(s32[21]{0:T(128)S(1)} %concatenate.3.refs_0_, bf16[512,256]{1,0:T(8,128)(2,1)S(1)} %attend_far.2.refs_11_.refs_2_.refs_1_, bf16[512,256]{1,0:T(8,128)(2,1)S(1)} %collective-permute-done.26.refs_2_, bf16[1344,2048]{1,0:T(8,128)(2,1)S(1)} %get-tuple-element.52.refs_3_, ...), custom_call_target="tpu_custom_call" | custom-call | flops 1000 | bytes 1000 | tf_op jit(solution)/shard_map/out_near/pallas_call | solution.py:312
  103.0 1.4 %out_near.2.refs_4_ = f32[1344,256]{1,0:T(8,128)S(1)} custom-call(s32[21]{0:T(128)S(1)} %concatenate.3.refs_0_, bf16[512,256]{1,0:T(8,128)(2,1)S(1)} %attend_far.3.refs_1_.refs_4_, bf16[512,256]{1,0:T(8,128)(2,1)S(1)} %collective-permute-done.19.refs_2_, bf16[1344,2048]{1,0:T(8,128)(2,1)S(1)} %get-tuple-element.52.refs_3_, ...), custom_call_target="tpu_custom_call" | custom-call | flops 1000 | bytes 1000 | tf_op jit(solution)/shard_map/out_near/pallas_call | solution.py:312
  104.4 2.6 %out_far.2.refs_8_ = bf16[1344,512]{1,0:T(8,128)(2,1)} custom-call(s32[21]{0:T(128)S(1)} %concatenate.3.refs_0_, bf16[512,256]{1,0:T(8,128)(2,1)S(1)} %collective-permute-done.24.refs_1_, bf16[512,256]{1,0:T(8,128)(2,1)S(1)} %collective-permute-done.25.refs_2_, bf16[1344,2048]{1,0:T(8,128)(2,1)S(1)} %get-tuple-element.52.refs_3_, ...), custom_call_target="tpu_custom_call" | custom-call | flops 1000 | bytes 1000 | tf_op jit(solution)/shard_map/out_far/pallas_call | solution.py:312
  107.0 2.6 %out_far.3 = bf16[1344,512]{1,0:T(8,128)(2,1)} custom-call(s32[21]{0:T(128)S(1)} %concatenate.3.refs_0_, bf16[512,256]{1,0:T(8,128)(2,1)S(1)} %collective-permute-done.17.refs_1_, bf16[512,256]{1,0:T(8,128)(2,1)S(1)} %collective-permute-done.18.refs_2_, bf16[1344,2048]{1,0:T(8,128)(2,1)S(1)} %get-tuple-element.52.refs_3_, ...), custom_call_target="tpu_custom_call", output_to_operand_aliasing={{}: (8, {})} | custom-call | flops 1000 | bytes 1000 | tf_op jit(solution)/shard_map/out_far/pallas_call | solution.py:312
  (73 shorter events, 16.7 us)
Async XLA Ops:
  0.0 17.9 %copy-start = (bf16[512,1344]{0,1:T(8,128)(2,1)S(1)}, bf16[512,1344]{0,1:T(8,128)(2,1)}, u32[]{:S(2)}) copy-start(bf16[512,1344]{0,1:T(8,128)(2,1)} %param.14) | copy-start | bytes 4128772
  0.0 17.9 %collective-permute-start = (bf16[1344,512]{1,0:T(8,128)(2,1)}, bf16[1344,512]{1,0:T(8,128)(2,1)}, u32[]{:S(2)}, u32[]{:S(2)}) collective-permute-start(bf16[1344,512]{1,0:T(8,128)(2,1)} %bitcast.10), channel_id=1, source_target_pairs={{0,1},{1,0},{2,3},{3,2},{4,5},{5,4},{6,7},{7,6},{8,9},{9,8},{10,11... | collective-permute-start | bytes 4128776 | tf_op jit(solution)/shard_map/ppermute | solution.py:667
  0.5 33.5 %collective-permute-start.1 = (bf16[1344,512]{1,0:T(8,128)(2,1)}, bf16[1344,512]{1,0:T(8,128)(2,1)S(1)}, u32[]{:S(2)}, u32[]{:S(2)}) collective-permute-start(bf16[1344,512]{1,0:T(8,128)(2,1)} %bitcast.11), channel_id=1, source_target_pairs={{0,2},{2,0},{1,3},{3,1},{4,6},{6,4},{5,7},{7,5},{8,10},{10,8},{9,1... | collective-permute-start | bytes 4128776 | tf_op jit(solution)/shard_map/ppermute | solution.py:664
  3.7 11.0 %copy-start.9 = (s32[2]{0:T(128)S(1)}, s32[2]{0:T(128)}, u32[]{:S(2)}) copy-start(s32[2]{0:T(128)} %refs_0_.3) | copy-start | bytes 28
  3.7 14.2 %copy-start.11 = (s32[16]{0:T(128)S(1)}, s32[16]{0:T(128)}, u32[]{:S(2)}) copy-start(s32[16]{0:T(128)} %param.26) | copy-start | bytes 196
  6.8 18.8 %collective-permute-start.2 = (bf16[64,1344]{1,0:T(8,128)(2,1)}, bf16[64,1344]{1,0:T(8,128)(2,1)}, u32[]{:S(2)}, u32[]{:S(2)}) collective-permute-start(bf16[64,1344]{1,0:T(8,128)(2,1)} %get-tuple-element.31), channel_id=1, source_target_pairs={{0,4},{4,0},{8,12},{12,8},{1,5},{5,1},{9,13},{13,9},{2,6},{6,2},{1... | collective-permute-start | bytes 516104 | tf_op jit(solution)/shard_map/ppermute | solution.py:632
  8.4 17.2 %collective-permute-start.3 = (bf16[64,1344]{1,0:T(8,128)(2,1)}, bf16[64,1344]{1,0:T(8,128)(2,1)}, u32[]{:S(2)}, u32[]{:S(2)}) collective-permute-start(bf16[64,1344]{1,0:T(8,128)(2,1)} %get-tuple-element.32), channel_id=1, source_target_pairs={{0,8},{4,12},{8,0},{12,4},{1,9},{5,13},{9,1},{13,5},{2,10},{6,14},... | collective-permute-start | bytes 516104 | tf_op jit(solution)/shard_map/ppermute | solution.py:632
  11.0 14.6 %collective-permute-start.4 = (bf16[64,1344]{1,0:T(8,128)(2,1)}, bf16[64,1344]{1,0:T(8,128)(2,1)}, u32[]{:S(2)}, u32[]{:S(2)}) collective-permute-start(bf16[64,1344]{1,0:T(8,128)(2,1)} %get-tuple-element.33), channel_id=1, source_target_pairs={{0,12},{4,8},{8,4},{12,0},{1,13},{5,9},{9,5},{13,1},{2,14},{6,10},... | collective-permute-start | bytes 516104 | tf_op jit(solution)/shard_map/ppermute | solution.py:632
  26.8 7.2 %collective-permute-start.5 = (bf16[64,1344]{1,0:T(8,128)(2,1)S(1)}, bf16[64,1344]{1,0:T(8,128)(2,1)S(1)}, u32[]{:S(2)}, u32[]{:S(2)}) collective-permute-start(bf16[64,1344]{1,0:T(8,128)(2,1)S(1)} %sum.1.refs_2_), channel_id=1, source_target_pairs={{0,4},{4,0},{8,12},{12,8},{1,5},{5,1},{9,13},{13,9},{2,6},{6,2},{1... | collective-permute-start | bytes 516104 | tf_op jit(solution)/shard_map/ppermute | solution.py:636
  29.4 4.6 %collective-permute-start.6 = (bf16[64,1344]{1,0:T(8,128)(2,1)S(1)}, bf16[64,1344]{1,0:T(8,128)(2,1)S(1)}, u32[]{:S(2)}, u32[]{:S(2)}) collective-permute-start(bf16[64,1344]{1,0:T(8,128)(2,1)S(1)} %sum.1.refs_2_), channel_id=1, source_target_pairs={{4,8},{8,4},{5,9},{9,5},{6,10},{10,6},{7,11},{11,7},{20,24},{24,20... | collective-permute-start | bytes 516104 | tf_op jit(solution)/shard_map/ppermute | solution.py:638
  34.0 3.1 %collective-permute-start.7 = (bf16[1344,512]{1,0:T(8,128)(2,1)S(1)}, bf16[1344,512]{1,0:T(8,128)(2,1)S(1)}, u32[]{:S(2)}, u32[]{:S(2)}) collective-permute-start(bf16[1344,512]{1,0:T(8,128)(2,1)S(1)} %collective-permute-done.1.refs_1_), channel_id=1, source_target_pairs={{0,1},{1,0},{2,3},{3,2},{4,5},{5,4},{6,7},{7,6},{8,9},{9,8},{10,11... | collective-permute-start | bytes 4128776 | tf_op jit(solution)/shard_map/ppermute | solution.py:667
  34.0 5.2 %collective-permute-start.8 = (bf16[64,1344]{1,0:T(8,128)(2,1)S(1)}, bf16[64,1344]{1,0:T(8,128)(2,1)S(1)}, u32[]{:S(2)}, u32[]{:S(2)}) collective-permute-start(bf16[64,1344]{1,0:T(8,128)(2,1)S(1)} %collective-permute-done.5.refs_6_.refs_3_), channel_id=1, source_target_pairs={{4,8},{8,4},{5,9},{9,5},{6,10},{10,6},{7,11},{11,7},{20,24},{24,20... | collective-permute-start | bytes 516104 | tf_op jit(solution)/shard_map/ppermute | solution.py:638
  40.3 7.0 %collective-permute-start.9 = (f32[96,512]{1,0:T(8,128)S(1)}, f32[96,512]{1,0:T(8,128)S(1)}, u32[]{:S(2)}, u32[]{:S(2)}) collective-permute-start(f32[96,512]{1,0:T(8,128)S(1)} %get-tuple-element.40), channel_id=1, source_target_pairs={{0,1},{1,0},{2,3},{3,2},{4,5},{5,4},{6,7},{7,6},{8,9},{9,8},{10,11... | collective-permute-start | bytes 589832 | tf_op jit(solution)/shard_map/ppermute | solution.py:667
  40.5 16.6 %collective-permute-start.12 = (bf16[512,256]{1,0:T(8,128)(2,1)S(1)}, bf16[512,256]{1,0:T(8,128)(2,1)S(1)}, u32[]{:S(2)}, u32[]{:S(2)}) collective-permute-start(bf16[512,256]{1,0:T(8,128)(2,1)S(1)} %get-tuple-element.39.refs_6_.refs_4_), channel_id=1, source_target_pairs={{0,4},{4,8},{8,12},{12,0},{1,5},{5,9},{9,13},{13,1},{2,6},{6,10},{... | collective-permute-start | bytes 786440 | tf_op jit(solution)/shard_map/ppermute | solution.py:670
  47.3 11.6 %copy-start.7 = (f32[128]{0:T(128)S(1)}, f32[128]{0:T(128)}, u32[]{:S(2)}) copy-start(f32[128]{0:T(128)} %param.20) | copy-start | bytes 1540
  47.3 11.5 %copy-start.10 = (f32[128]{0:T(128)S(1)}, f32[128]{0:T(128)}, u32[]{:S(2)}) copy-start(f32[128]{0:T(128)} %param.19) | copy-start | bytes 1540
  47.3 7.0 %collective-permute-start.10 = (f32[96,512]{1,0:T(8,128)S(1)}, f32[96,512]{1,0:T(8,128)S(1)}, u32[]{:S(2)}, u32[]{:S(2)}) collective-permute-start(f32[96,512]{1,0:T(8,128)S(1)} %add.25.refs_6_), channel_id=1, source_target_pairs={{0,2},{2,0},{1,3},{3,1},{4,6},{6,4},{5,7},{7,5},{8,10},{10,8},{9,1... | collective-permute-start | bytes 589832 | tf_op jit(solution)/shard_map/ppermute | solution.py:664
  50.0 13.9 %collective-permute-start.11 = (bf16[512,256]{1,0:T(8,128)(2,1)S(1)}, bf16[512,256]{1,0:T(8,128)(2,1)S(1)}, u32[]{:S(2)}, u32[]{:S(2)}) collective-permute-start(bf16[512,256]{1,0:T(8,128)(2,1)S(1)} %get-tuple-element.43.refs_3_.refs_2_), channel_id=1, source_target_pairs={{0,4},{4,8},{8,12},{12,0},{1,5},{5,9},{9,13},{13,1},{2,6},{6,10},{... | collective-permute-start | bytes 786440 | tf_op jit(solution)/shard_map/ppermute | solution.py:670
  54.4 9.5 %collective-permute-start.13 = (bf16[64,512]{1,0:T(8,128)(2,1)S(1)}, bf16[64,512]{1,0:T(8,128)(2,1)S(1)}, u32[]{:S(2)}, u32[]{:S(2)}) collective-permute-start(bf16[64,512]{1,0:T(8,128)(2,1)S(1)} %slice.7), channel_id=1, source_target_pairs={{0,4},{4,8},{8,12},{12,0},{1,5},{5,9},{9,13},{13,1},{2,6},{6,10},{... | collective-permute-start | bytes 196616 | tf_op jit(solution)/shard_map/ppermute | solution.py:670
  56.2 13.5 %collective-permute-start.14 = (bf16[64,512]{1,0:T(8,128)(2,1)S(1)}, bf16[64,512]{1,0:T(8,128)(2,1)S(1)}, u32[]{:S(2)}, u32[]{:S(2)}) collective-permute-start(bf16[64,512]{1,0:T(8,128)(2,1)S(1)} %slice.7), channel_id=1, source_target_pairs={{0,8},{4,12},{8,0},{12,4},{1,9},{5,13},{9,1},{13,5},{2,10},{6,14},... | collective-permute-start | bytes 196616 | tf_op jit(solution)/shard_map/ppermute | solution.py:670
  57.1 16.3 %collective-permute-start.16 = (bf16[512,256]{1,0:T(8,128)(2,1)S(1)}, bf16[512,256]{1,0:T(8,128)(2,1)S(1)}, u32[]{:S(2)}, u32[]{:S(2)}) collective-permute-start(bf16[512,256]{1,0:T(8,128)(2,1)S(1)} %collective-permute-done.12.refs_5_), channel_id=1, source_target_pairs={{0,4},{4,8},{8,12},{12,0},{1,5},{5,9},{9,13},{13,1},{2,6},{6,10},{... | collective-permute-start | bytes 786440 | tf_op jit(solution)/shard_map/ppermute | solution.py:670
  69.7 11.0 %collective-permute-start.15 = (bf16[512,256]{1,0:T(8,128)(2,1)S(1)}, bf16[512,256]{1,0:T(8,128)(2,1)S(1)}, u32[]{:S(2)}, u32[]{:S(2)}) collective-permute-start(bf16[512,256]{1,0:T(8,128)(2,1)S(1)} %collective-permute-done.11.refs_4_), channel_id=1, source_target_pairs={{0,4},{4,8},{8,12},{12,0},{1,5},{5,9},{9,13},{13,1},{2,6},{6,10},{... | collective-permute-start | bytes 786440 | tf_op jit(solution)/shard_map/ppermute | solution.py:670
  69.7 14.6 %collective-permute-start.20 = (bf16[64,1920]{1,0:T(8,128)(2,1)S(1)}, bf16[64,1920]{1,0:T(8,128)(2,1)S(1)}, u32[]{:S(2)}, u32[]{:S(2)}) collective-permute-start(bf16[64,1920]{1,0:T(8,128)(2,1)S(1)} %copy-done.3), channel_id=1, source_target_pairs={{0,4},{4,0},{8,12},{12,8},{1,5},{5,1},{9,13},{13,9},{2,6},{6,2},{1... | collective-permute-start | bytes 737288 | tf_op jit(solution)/shard_map/ppermute | solution.py:679
  75.0 11.2 %collective-permute-start.24 = (bf16[512,256]{1,0:T(8,128)(2,1)S(1)}, bf16[512,256]{1,0:T(8,128)(2,1)S(1)}, u32[]{:S(2)}, u32[]{:S(2)}) collective-permute-start(bf16[512,256]{1,0:T(8,128)(2,1)S(1)} %attend_far.2.refs_11_.refs_2_.refs_1_), channel_id=1, source_target_pairs={{0,2},{2,0},{1,3},{3,1},{4,6},{6,4},{5,7},{7,5},{8,10},{10,8},{9,1... | collective-permute-start | bytes 786440 | tf_op jit(solution)/shard_map/ppermute | solution.py:664
  82.8 6.5 %collective-permute-start.17 = (bf16[512,256]{1,0:T(8,128)(2,1)S(1)}, bf16[512,256]{1,0:T(8,128)(2,1)S(1)}, u32[]{:S(2)}, u32[]{:S(2)}) collective-permute-start(bf16[512,256]{1,0:T(8,128)(2,1)S(1)} %attend_far.3.refs_1_.refs_4_), channel_id=1, source_target_pairs={{0,2},{2,0},{1,3},{3,1},{4,6},{6,4},{5,7},{7,5},{8,10},{10,8},{9,1... | collective-permute-start | bytes 786440 | tf_op jit(solution)/shard_map/ppermute | solution.py:664
  84.4 12.2 %collective-permute-start.21 = (bf16[64,1920]{1,0:T(8,128)(2,1)S(1)}, bf16[64,1920]{1,0:T(8,128)(2,1)S(1)}, u32[]{:S(2)}, u32[]{:S(2)}) collective-permute-start(bf16[64,1920]{1,0:T(8,128)(2,1)S(1)} %out_add.1.refs_3_.refs_6_), channel_id=1, source_target_pairs={{0,8},{4,12},{8,0},{12,4},{1,9},{5,13},{9,1},{13,5},{2,10},{6,14},... | collective-permute-start | bytes 737288 | tf_op jit(solution)/shard_map/ppermute | solution.py:679
  85.7 14.5 %collective-permute-start.26 = (bf16[512,256]{1,0:T(8,128)(2,1)S(1)}, bf16[512,256]{1,0:T(8,128)(2,1)S(1)}, u32[]{:S(2)}, u32[]{:S(2)}) collective-permute-start(bf16[512,256]{1,0:T(8,128)(2,1)S(1)} %attend_far.2.refs_11_.refs_2_.refs_1_), channel_id=1, source_target_pairs={{0,1},{1,0},{2,3},{3,2},{4,5},{5,4},{6,7},{7,6},{8,9},{9,8},{10,11... | collective-permute-start | bytes 786440 | tf_op jit(solution)/shard_map/ppermute | solution.py:667
  85.7 17.3 %collective-permute-start.19 = (bf16[512,256]{1,0:T(8,128)(2,1)S(1)}, bf16[512,256]{1,0:T(8,128)(2,1)S(1)}, u32[]{:S(2)}, u32[]{:S(2)}) collective-permute-start(bf16[512,256]{1,0:T(8,128)(2,1)S(1)} %attend_far.3.refs_1_.refs_4_), channel_id=1, source_target_pairs={{0,1},{1,0},{2,3},{3,2},{4,5},{5,4},{6,7},{7,6},{8,9},{9,8},{10,11... | collective-permute-start | bytes 786440 | tf_op jit(solution)/shard_map/ppermute | solution.py:667
  86.2 18.2 %collective-permute-start.25 = (bf16[512,256]{1,0:T(8,128)(2,1)S(1)}, bf16[512,256]{1,0:T(8,128)(2,1)S(1)}, u32[]{:S(2)}, u32[]{:S(2)}) collective-permute-start(bf16[512,256]{1,0:T(8,128)(2,1)S(1)} %collective-permute-done.24.refs_1_), channel_id=1, source_target_pairs={{0,1},{1,0},{2,3},{3,2},{4,5},{5,4},{6,7},{7,6},{8,9},{9,8},{10,11... | collective-permute-start | bytes 786440 | tf_op jit(solution)/shard_map/ppermute | solution.py:667
  89.3 17.7 %collective-permute-start.18 = (bf16[512,256]{1,0:T(8,128)(2,1)S(1)}, bf16[512,256]{1,0:T(8,128)(2,1)S(1)}, u32[]{:S(2)}, u32[]{:S(2)}) collective-permute-start(bf16[512,256]{1,0:T(8,128)(2,1)S(1)} %collective-permute-done.17.refs_1_), channel_id=1, source_target_pairs={{0,1},{1,0},{2,3},{3,2},{4,5},{5,4},{6,7},{7,6},{8,9},{9,8},{10,11... | collective-permute-start | bytes 786440 | tf_op jit(solution)/shard_map/ppermute | solution.py:667
  97.3 1.3 %collective-permute-start.22 = (f32[32,512]{1,0:T(8,128)S(1)}, f32[32,512]{1,0:T(8,128)S(1)}, u32[]{:S(2)}, u32[]{:S(2)}) collective-permute-start(f32[32,512]{1,0:T(8,128)S(1)} %out_low.1), channel_id=1, source_target_pairs={{0,1},{1,0},{2,3},{3,2},{4,5},{5,4},{6,7},{7,6},{8,9},{9,8},{10,11... | collective-permute-start | bytes 196616 | tf_op jit(solution)/shard_map/ppermute | solution.py:667
  98.6 4.3 %collective-permute-start.23 = (f32[32,512]{1,0:T(8,128)S(1)}, f32[32,512]{1,0:T(8,128)S(1)}, u32[]{:S(2)}, u32[]{:S(2)}) collective-permute-start(f32[32,512]{1,0:T(8,128)S(1)} %add.27), channel_id=1, source_target_pairs={{0,2},{2,0},{1,3},{3,1},{4,6},{6,4},{5,7},{7,5},{8,10},{10,8},{9,1... | collective-permute-start | bytes 196616 | tf_op jit(solution)/shard_map/ppermute | solution.py:664
  (7 other events, 21.5 us)

commit v3 on v2

--- a/solution.py
+++ b/solution.py
@@ -742,8 +742,10 @@
 
     quarter = call(sum_kernel, "sum", shape((64, width)), [VM] * 4, received, after=[near[0], cosine, sine])
     pieces = share_quarter(quarter)
-    far_other = core(after(far_own, pieces[1], pieces[2]))
+    out_pair = call(add_kernel, "out_add", shape((64, 1920)), [VM] * 2, [out_panel, out_beside], after=[quarter])
+    far_other = core(after(far_own, pieces[1], pieces[2], out_pair))
     late_q, late_kv = project(1, pieces[1])
+    early_q, early_kv = project(0, late_kv)
     partial_low, ups = call(
         low_kernel,
         "low",
@@ -751,16 +753,15 @@
         [SM] + [VM] * 5,
         [meta, tokens, *pieces],
         [pltpu.VMEM((4, 64, width), BF16)],
-        after=[late_kv],
+        after=[early_kv],
     )
     chip_low = partial_low + core(partial_low)
     low = chip_low + across(chip_low)
-    early_q, early_kv = project(0, chip_low)
 
     prev_late, prev_early = up(late_kv), up(early_kv)
     low_kv = low[32:96].astype(BF16)
     low_prev = up(low_kv)
-    low_prev2 = up(low_kv, 2)
+    low_prev2 = up(low_prev)
     prev2_late = up(after(prev_late, early_kv))
 
     shard_scratch = [pltpu.VMEM((rows, 256), BF16), pltpu.VMEM((256, rows), BF16)]
@@ -773,7 +774,7 @@
         [meta, early_q, late_q, early_kv, late_kv, low, ups, q_gain, k_gain, cosine, sine, output_matrix.T],
         shard_scratch + [pltpu.SemaphoreType.DMA],
     )
-    prev2_early = up(after(prev_early, low_prev, low_prev2, num))
+    prev2_early = up(after(prev_early, low_prev, num))
     num, den = call(
         attend_prev_kernel,
         "attend_prev",
@@ -797,7 +798,6 @@
     att_late = attend_far(1, [prev2_late], [])
     att_early = attend_far(0, [prev2_early, prev2_late], [att_late])
 
-    out_pair = call(add_kernel, "out_add", shape((64, 1920)), [VM] * 2, [out_panel, out_beside], after=[early_kv])
     out_rest = swapped(out_pair, 2)
     out_low = call(
         out_low_kernel,

time: 110 us -> 105 us (0.955)
  waiting for transfers between devices: 31.9 us -> 28.9 us
  local copies, waits for them, and re-layouts: 3.98 us -> 1.45 us
  Pallas kernels: 38 us -> 39.8 us
    ppermute x6, waiting for transfers between devices: 9.94 us -> 5.4 us  [up(): return lax.ppermute(value, 'seq', [(i, (i + by) % 4) for i in range(4)])]
    ppermute x5, waiting for transfers between devices: 11 us -> 15 us  [across(): return lax.ppermute(value, 'head', SWAP)]
    ppermute x2, waiting for transfers between devices: 7.24 us -> 4.36 us  [swapped(): return lax.ppermute(value, 'seq', [(j, j ^ by) for j in range(4)])]
    unnamed x24 -> x16, local copies, waits for them, and re-layouts: 3.89 us -> 1.36 us
    ppermute x6, starting transfers between devices: 13 us -> 10.9 us  [up(): return lax.ppermute(value, 'seq', [(i, (i + by) % 4) for i in range(4)])]
    ppermute x2, starting transfers between devices: 1.42 us -> 3.47 us  [swapped(): return lax.ppermute(value, 'seq', [(j, j ^ by) for j in range(4)])]
    pallas_call x17, Pallas kernels: 38 us -> 39.8 us  [call(): pl.pallas_call(body, out_shape=out_shape, in_specs=list(in_specs) + [HB]...]
  transfers between devices with their start and end apart: 27 -> 27, of which waited for: 9 -> 10; matrix products, arithmetic and copies ran while one was open for 3% -> 2% of each run, Pallas kernels for 31% -> 34%
where the time goes in v3:
time: 105 us
  Pallas kernels  39.8 us (38%)
  starting transfers between devices  31.9 us (30%)
  waiting for transfers between devices  28.9 us (28%)
  other arithmetic  2.13 us (2%)
  local copies, waits for them, and re-layouts  1.45 us (1%)
    pallas_call x17, Pallas kernels, call(): pl.pallas_call(body, out_shape=out_shape, in_specs=list(in_specs) + [HB]...  39.8 us
    ppermute x5, waiting for transfers between devices, across(): return lax.ppermute(value, 'head', SWAP)  15 us
    ppermute x6, starting transfers between devices, up(): return lax.ppermute(value, 'seq', [(i, (i + by) % 4) for i in range(4)])  10.9 us
    ppermute x5, starting transfers between devices, across(): return lax.ppermute(value, 'head', SWAP)  7.12 us
    ppermute x6, waiting for transfers between devices, up(): return lax.ppermute(value, 'seq', [(i, (i + by) % 4) for i in range(4)])  5.4 us
    ppermute x3, starting transfers between devices, exchange_quarters(): lax.ppermute(quarters[s], 'seq', [(j, j ^ s) for j in range(4)])  4.45 us
    ppermute x2, waiting for transfers between devices, swapped(): return lax.ppermute(value, 'seq', [(j, j ^ by) for j in range(4)])  4.36 us
    ppermute x8, waiting for transfers between devices, core(): return lax.ppermute(value, 'rep', SWAP)  3.7 us
  transfers between devices with their start and end apart: 27, of which 10 were waited for; matrix products, arithmetic and copies ran while one was open for 2% of the time, Pallas kernels for 34%

profile of v3, /device:TPU:0, one launch (start us, length us, event | category | flops | bytes accessed | tf_op | source)
XLA Modules:
  0.0 105.1 jit_solution(17914653518564966220)
XLA Ops:
  0.5 2.5 %collective-permute-start.1 = (bf16[1344,512]{1,0:T(8,128)(2,1)}, bf16[1344,512]{1,0:T(8,128)(2,1)S(1)}, u32[]{:S(2)}, u32[]{:S(2)}) collective-permute-start(bf16[1344,512]{1,0:T(8,128)(2,1)} %bitcast.11), channel_id=1, source_target_pairs={{0,2},{2,0},{1,3},{3,1},{4,6},{6,4},{5,7},{7,5},{8,10},{10,8},{9,1... | collective-permute-start | bytes 4128776 | tf_op jit(solution)/shard_map/ppermute | solution.py:664
  3.7 2.5 %pack.1 = (bf16[64,1344]{1,0:T(8,128)(2,1)S(1)}, bf16[64,1344]{1,0:T(8,128)(2,1)}, bf16[64,1344]{1,0:T(8,128)(2,1)}, bf16[64,1344]{1,0:T(8,128)(2,1)}) custom-call(s32[2]{0:T(128)S(1)} %copy-done.4, bf16[2,96,1344]{2,1,0:T(8,128)(2,1)} %bitcast.20, bf16[2,32,512]{2,1,0:T(8,128)(2,1)} %refs_2_.2, bf16[2,2,32,512]{3,2,1,0:T(8,128)(2,1)} %refs_3_.2), custom_call_target="tpu_custom_call" | custom-call | flops 1000 | bytes 1000 | tf_op jit(solution)/shard_map/pack/pallas_call | solution.py:312
  6.2 1.6 %collective-permute-start.2 = (bf16[64,1344]{1,0:T(8,128)(2,1)}, bf16[64,1344]{1,0:T(8,128)(2,1)}, u32[]{:S(2)}, u32[]{:S(2)}) collective-permute-start(bf16[64,1344]{1,0:T(8,128)(2,1)} %get-tuple-element.31), channel_id=1, source_target_pairs={{0,4},{4,0},{8,12},{12,8},{1,5},{5,1},{9,13},{13,9},{2,6},{6,2},{1... | collective-permute-start | bytes 516104 | tf_op jit(solution)/shard_map/ppermute | solution.py:632
  7.8 2.6 %collective-permute-start.3 = (bf16[64,1344]{1,0:T(8,128)(2,1)}, bf16[64,1344]{1,0:T(8,128)(2,1)}, u32[]{:S(2)}, u32[]{:S(2)}) collective-permute-start(bf16[64,1344]{1,0:T(8,128)(2,1)} %get-tuple-element.32), channel_id=1, source_target_pairs={{0,8},{4,12},{8,0},{12,4},{1,9},{5,13},{9,1},{13,5},{2,10},{6,14},... | collective-permute-start | bytes 516104 | tf_op jit(solution)/shard_map/ppermute | solution.py:632
  10.6 2.3 %pack_out.1.refs_6_.refs_0_ = bf16[64,1920]{1,0:T(8,128)(2,1)} custom-call(s32[2]{0:T(128)S(1)} %copy-done.4, bf16[2,32,512]{2,1,0:T(8,128)(2,1)} %bitcast.21, bf16[2,32,1344]{2,1,0:T(8,128)(2,1)} %refs_2_.3, bf16[64,1344]{1,0:T(8,128)(2,1)S(1)} %get-tuple-element.29.refs_3_.refs_0_), custom_call_target="tpu_custom_call" | custom-call | flops 1000 | bytes 1000 | tf_op jit(solution)/shard_map/pack_out/pallas_call | solution.py:312
  15.5 1.4 %multiply_sine_fusion = (f32[64,1536]{1,0:T(8,128)S(1)}, f32[64,1536]{1,0:T(8,128)S(1)}) fusion(f32[1536]{0:T(1024)S(1)} %fusion, f32[64]{0:T(128)S(1)} %multiply_power_fusion), kind=kLoop, calls=%fused_computation | loop fusion | flops 98304 | bytes 792832 | tf_op jit(solution)/shard_map/sin | solution.py:739
  17.0 6.7 %near.1 = (f32[256,1024]{1,0:T(8,128)S(1)}, f32[256,1024]{1,0:T(8,128)S(1)}, bf16[2,1344,256]{2,1,0:T(8,128)(2,1)S(1)}, bf16[2,1344,256]{2,1,0:T(8,128)(2,1)S(1)}, bf16[2,1344,512]{2,1,0:T(8,128)(2,1)S(1)}) custom-call(s32[21]{0:T(128)S(1)} %concatenate.3.refs_0_, bf16[1344,512]{1,0:T(8,128)(2,1)S(1)} %bitcast.12, ...), custom_call_target="tpu_custom_call" | custom-call | flops 1000 | bytes 1000 | tf_op jit(solution)/shard_map/near/pallas_call | solution.py:312
  25.4 3.4 %collective-permute-start.5 = (bf16[64,1344]{1,0:T(8,128)(2,1)S(1)}, bf16[64,1344]{1,0:T(8,128)(2,1)S(1)}, u32[]{:S(2)}, u32[]{:S(2)}) collective-permute-start(bf16[64,1344]{1,0:T(8,128)(2,1)S(1)} %sum.1.refs_2_), channel_id=1, source_target_pairs={{0,4},{4,0},{8,12},{12,8},{1,5},{5,1},{9,13},{13,9},{2,6},{6,2},{1... | collective-permute-start | bytes 516104 | tf_op jit(solution)/shard_map/ppermute | solution.py:636
  30.6 3.4 %collective-permute-done.1.refs_1_ = bf16[1344,512]{1,0:T(8,128)(2,1)S(1)} collective-permute-done((bf16[1344,512]{1,0:T(8,128)(2,1)}, bf16[1344,512]{1,0:T(8,128)(2,1)S(1)}, u32[]{:S(2)}, u32[]{:S(2)}) %collective-permute-start.1) | collective-permute-done | bytes 1376288 | tf_op jit(solution)/shard_map/ppermute | solution.py:664
  34.7 2.4 %collective-permute-done.8.refs_2_ = bf16[1344,512]{1,0:T(8,128)(2,1)S(1)} collective-permute-done((bf16[1344,512]{1,0:T(8,128)(2,1)S(1)}, bf16[1344,512]{1,0:T(8,128)(2,1)S(1)}, u32[]{:S(2)}, u32[]{:S(2)}) %collective-permute-start.8) | collective-permute-done | bytes 1376288 | tf_op jit(solution)/shard_map/ppermute | solution.py:667
  37.1 2.0 %far.2 = (f32[512,256]{1,0:T(8,128)S(1)}, bf16[512,256]{1,0:T(8,128)(2,1)S(1)}) custom-call(f32[256,1024]{1,0:T(8,128)S(1)} %get-tuple-element.38.refs_0_, bf16[1344,512]{1,0:T(8,128)(2,1)S(1)} %collective-permute-done.1.refs_1_, bf16[1344,512]{1,0:T(8,128)(2,1)S(1)} %collective-permute-done.8.refs_2_, bf16[2,1344,256]{2,1,0:T(8,128)(2,1)S(1)} %get-tuple-element.35.refs_3_, ...), custom_call_target="tpu_custom_call" | custom-call | flops 1000 | bytes 1000 | tf_op jit(solution)/shard_map/far/pallas_call | solution.py:312
  39.2 2.0 %far.3 = (f32[512,256]{1,0:T(8,128)S(1)}, bf16[512,256]{1,0:T(8,128)(2,1)S(1)}) custom-call(f32[256,1024]{1,0:T(8,128)S(1)} %get-tuple-element.30.refs_4_.refs_0_, bf16[1344,512]{1,0:T(8,128)(2,1)S(1)} %collective-permute-done.1.refs_1_, bf16[1344,512]{1,0:T(8,128)(2,1)S(1)} %collective-permute-done.8.refs_2_, ...), custom_call_target="tpu_custom_call" | custom-call | flops 1000 | bytes 1000 | tf_op jit(solution)/shard_map/far/pallas_call | solution.py:312
  42.5 3.8 %collective-permute-start.13 = (bf16[512,256]{1,0:T(8,128)(2,1)S(1)}, bf16[512,256]{1,0:T(8,128)(2,1)S(1)}, u32[]{:S(2)}, u32[]{:S(2)}) collective-permute-start(bf16[512,256]{1,0:T(8,128)(2,1)S(1)} %get-tuple-element.39.refs_6_.refs_4_), channel_id=1, source_target_pairs={{0,4},{4,8},{8,12},{12,0},{1,5},{5,9},{9,13},{13,1},{2,6},{6,10},{... | collective-permute-start | bytes 786440 | tf_op jit(solution)/shard_map/ppermute | solution.py:670
  47.5 1.6 %collective-permute-start.12 = (bf16[512,256]{1,0:T(8,128)(2,1)S(1)}, bf16[512,256]{1,0:T(8,128)(2,1)S(1)}, u32[]{:S(2)}, u32[]{:S(2)}) collective-permute-start(bf16[512,256]{1,0:T(8,128)(2,1)S(1)} %get-tuple-element.42.refs_6_.refs_3_), channel_id=1, source_target_pairs={{0,4},{4,8},{8,12},{12,0},{1,5},{5,9},{9,13},{13,1},{2,6},{6,10},{... | collective-permute-start | bytes 786440 | tf_op jit(solution)/shard_map/ppermute | solution.py:670
  49.1 4.3 %collective-permute-done.11 = f32[96,512]{1,0:T(8,128)S(1)} collective-permute-done((f32[96,512]{1,0:T(8,128)S(1)}, f32[96,512]{1,0:T(8,128)S(1)}, u32[]{:S(2)}, u32[]{:S(2)}) %collective-permute-start.11) | collective-permute-done | bytes 196640 | tf_op jit(solution)/shard_map/ppermute | solution.py:664
  53.4 1.6 %collective-permute-start.14 = (bf16[64,512]{1,0:T(8,128)(2,1)S(1)}, bf16[64,512]{1,0:T(8,128)(2,1)S(1)}, u32[]{:S(2)}, u32[]{:S(2)}) collective-permute-start(bf16[64,512]{1,0:T(8,128)(2,1)S(1)} %slice.7), channel_id=1, source_target_pairs={{0,4},{4,8},{8,12},{12,0},{1,5},{5,9},{9,13},{13,1},{2,6},{6,10},{... | collective-permute-start | bytes 196616 | tf_op jit(solution)/shard_map/ppermute | solution.py:670
  56.4 5.0 %attend_own.1 = (bf16[512,512]{1,0:T(8,128)(2,1)S(1)}, f32[512,512]{1,0:T(8,128)S(1)}, f32[8,512]{1,0:T(8,128)S(1)}, bf16[1344,2048]{1,0:T(8,128)(2,1)S(1)}) custom-call(s32[21]{0:T(128)S(1)} %concatenate.3.refs_0_, f32[512,256]{1,0:T(8,128)S(1)} %get-tuple-element.40.refs_1_, f32[512,256]{1,0:T(8,128)S(1)} %get-tuple-element.41.refs_2_, ...), custom_call_target="tpu_custom_call" | custom-call | flops 1000 | bytes 1000 | tf_op jit(solution)/shard_map/attend_own/pallas_call | solution.py:312
  62.4 1.6 %collective-permute-start.17 = (bf16[64,512]{1,0:T(8,128)(2,1)S(1)}, bf16[64,512]{1,0:T(8,128)(2,1)S(1)}, u32[]{:S(2)}, u32[]{:S(2)}) collective-permute-start(bf16[64,512]{1,0:T(8,128)(2,1)S(1)} %collective-permute-done.14.refs_6_), channel_id=1, source_target_pairs={{0,4},{4,8},{8,12},{12,0},{1,5},{5,9},{9,13},{13,1},{2,6},{6,10},{... | collective-permute-start | bytes 196616 | tf_op jit(solution)/shard_map/ppermute | solution.py:670
  64.0 3.5 %attend_prev.1 = (f32[512,512]{1,0:T(8,128)S(1)}, f32[8,512]{1,0:T(8,128)S(1)}) custom-call(s32[21]{0:T(128)S(1)} %concatenate.3.refs_0_, bf16[512,512]{1,0:T(8,128)(2,1)S(1)} %get-tuple-element.45.refs_1_, f32[512,512]{1,0:T(8,128)S(1)} %get-tuple-element.46.refs_2_, f32[8,512]{1,0:T(8,128)S(1)} %get-tuple-element.47.refs_3_, ...), custom_call_target="tpu_custom_call" | custom-call | flops 1000 | bytes 1000 | tf_op jit(solution)/shard_map/attend_prev/pallas_call | solution.py:312
  67.5 5.4 %collective-permute-done.17.refs_5_.refs_6_ = bf16[64,512]{1,0:T(8,128)(2,1)S(1)} collective-permute-done((bf16[64,512]{1,0:T(8,128)(2,1)S(1)}, bf16[64,512]{1,0:T(8,128)(2,1)S(1)}, u32[]{:S(2)}, u32[]{:S(2)}) %collective-permute-start.17) | collective-permute-done | bytes 65568 | tf_op jit(solution)/shard_map/ppermute | solution.py:670
  72.9 1.7 %attend_far.2.refs_11_.refs_2_.refs_1_ = bf16[512,256]{1,0:T(8,128)(2,1)S(1)} custom-call(s32[21]{0:T(128)S(1)} %concatenate.3.refs_0_, bf16[512,512]{1,0:T(8,128)(2,1)S(1)} %get-tuple-element.45.refs_1_, f32[512,512]{1,0:T(8,128)S(1)} %get-tuple-element.48.refs_2_, f32[8,512]{1,0:T(8,128)S(1)} %get-tuple-element.49.refs_3_, ...), custom_call_target="tpu_custom_call" | custom-call | flops 1000 | bytes 1000 | tf_op jit(solution)/shard_map/attend_far/pallas_call | solution.py:312
  74.6 1.6 %collective-permute-start.24 = (bf16[512,256]{1,0:T(8,128)(2,1)S(1)}, bf16[512,256]{1,0:T(8,128)(2,1)S(1)}, u32[]{:S(2)}, u32[]{:S(2)}) collective-permute-start(bf16[512,256]{1,0:T(8,128)(2,1)S(1)} %attend_far.2.refs_11_.refs_2_.refs_1_), channel_id=1, source_target_pairs={{0,2},{2,0},{1,3},{3,1},{4,6},{6,4},{5,7},{7,5},{8,10},{10,8},{9,1... | collective-permute-start | bytes 786440 | tf_op jit(solution)/shard_map/ppermute | solution.py:664
  76.1 2.1 %attend_far.3.refs_1_.refs_4_ = bf16[512,256]{1,0:T(8,128)(2,1)S(1)} custom-call(s32[21]{0:T(128)S(1)} %concatenate.3.refs_0_, bf16[512,512]{1,0:T(8,128)(2,1)S(1)} %get-tuple-element.45.refs_1_, f32[512,512]{1,0:T(8,128)S(1)} %get-tuple-element.48.refs_2_, f32[8,512]{1,0:T(8,128)S(1)} %get-tuple-element.49.refs_3_, ...), custom_call_target="tpu_custom_call" | custom-call | flops 1000 | bytes 1000 | tf_op jit(solution)/shard_map/attend_far/pallas_call | solution.py:312
  78.8 2.7 %collective-permute-start.21 = (bf16[64,1920]{1,0:T(8,128)(2,1)S(1)}, bf16[64,1920]{1,0:T(8,128)(2,1)S(1)}, u32[]{:S(2)}, u32[]{:S(2)}) collective-permute-start(bf16[64,1920]{1,0:T(8,128)(2,1)S(1)} %out_add.1.refs_3_.refs_6_), channel_id=1, source_target_pairs={{0,8},{4,12},{8,0},{12,4},{1,9},{5,13},{9,1},{13,5},{2,10},{6,14},... | collective-permute-start | bytes 737288 | tf_op jit(solution)/shard_map/ppermute | solution.py:679
  82.1 1.8 %collective-permute-done.24.refs_1_ = bf16[512,256]{1,0:T(8,128)(2,1)S(1)} collective-permute-done((bf16[512,256]{1,0:T(8,128)(2,1)S(1)}, bf16[512,256]{1,0:T(8,128)(2,1)S(1)}, u32[]{:S(2)}, u32[]{:S(2)}) %collective-permute-start.24) | collective-permute-done | bytes 262176 | tf_op jit(solution)/shard_map/ppermute | solution.py:664
  83.9 3.8 %collective-permute-done.18.refs_1_ = bf16[512,256]{1,0:T(8,128)(2,1)S(1)} collective-permute-done((bf16[512,256]{1,0:T(8,128)(2,1)S(1)}, bf16[512,256]{1,0:T(8,128)(2,1)S(1)}, u32[]{:S(2)}, u32[]{:S(2)}) %collective-permute-start.18) | collective-permute-done | bytes 262176 | tf_op jit(solution)/shard_map/ppermute | solution.py:664
  87.7 4.4 %collective-permute-done.21.refs_4_.refs_7_ = bf16[64,1920]{1,0:T(8,128)(2,1)S(1)} collective-permute-done((bf16[64,1920]{1,0:T(8,128)(2,1)S(1)}, bf16[64,1920]{1,0:T(8,128)(2,1)S(1)}, u32[]{:S(2)}, u32[]{:S(2)}) %collective-permute-start.21) | collective-permute-done | bytes 245792 | tf_op jit(solution)/shard_map/ppermute | solution.py:679
  95.4 1.4 %out_near.3.refs_4_ = f32[1344,256]{1,0:T(8,128)S(1)} custom-call(s32[21]{0:T(128)S(1)} %concatenate.3.refs_0_, bf16[512,256]{1,0:T(8,128)(2,1)S(1)} %attend_far.2.refs_11_.refs_2_.refs_1_, bf16[512,256]{1,0:T(8,128)(2,1)S(1)} %collective-permute-done.26.refs_2_, bf16[1344,2048]{1,0:T(8,128)(2,1)S(1)} %get-tuple-element.52.refs_3_, ...), custom_call_target="tpu_custom_call" | custom-call | flops 1000 | bytes 1000 | tf_op jit(solution)/shard_map/out_near/pallas_call | solution.py:312
  96.8 1.6 %collective-permute-done.23 = f32[32,512]{1,0:T(8,128)S(1)} collective-permute-done((f32[32,512]{1,0:T(8,128)S(1)}, f32[32,512]{1,0:T(8,128)S(1)}, u32[]{:S(2)}, u32[]{:S(2)}) %collective-permute-start.23) | collective-permute-done | bytes 65568 | tf_op jit(solution)/shard_map/ppermute | solution.py:664
  98.5 1.4 %out_near.2.refs_4_ = f32[1344,256]{1,0:T(8,128)S(1)} custom-call(s32[21]{0:T(128)S(1)} %concatenate.3.refs_0_, bf16[512,256]{1,0:T(8,128)(2,1)S(1)} %attend_far.3.refs_1_.refs_4_, bf16[512,256]{1,0:T(8,128)(2,1)S(1)} %collective-permute-done.20.refs_2_, bf16[1344,2048]{1,0:T(8,128)(2,1)S(1)} %get-tuple-element.52.refs_3_, ...), custom_call_target="tpu_custom_call" | custom-call | flops 1000 | bytes 1000 | tf_op jit(solution)/shard_map/out_near/pallas_call | solution.py:312
  99.9 2.6 %out_far.2.refs_8_ = bf16[1344,512]{1,0:T(8,128)(2,1)} custom-call(s32[21]{0:T(128)S(1)} %concatenate.3.refs_0_, bf16[512,256]{1,0:T(8,128)(2,1)S(1)} %collective-permute-done.24.refs_1_, bf16[512,256]{1,0:T(8,128)(2,1)S(1)} %collective-permute-done.25.refs_2_, bf16[1344,2048]{1,0:T(8,128)(2,1)S(1)} %get-tuple-element.52.refs_3_, ...), custom_call_target="tpu_custom_call" | custom-call | flops 1000 | bytes 1000 | tf_op jit(solution)/shard_map/out_far/pallas_call | solution.py:312
  102.5 2.6 %out_far.3 = bf16[1344,512]{1,0:T(8,128)(2,1)} custom-call(s32[21]{0:T(128)S(1)} %concatenate.3.refs_0_, bf16[512,256]{1,0:T(8,128)(2,1)S(1)} %collective-permute-done.18.refs_1_, bf16[512,256]{1,0:T(8,128)(2,1)S(1)} %collective-permute-done.19.refs_2_, bf16[1344,2048]{1,0:T(8,128)(2,1)S(1)} %get-tuple-element.52.refs_3_, ...), custom_call_target="tpu_custom_call", output_to_operand_aliasing={{}: (8, {})} | custom-call | flops 1000 | bytes 1000 | tf_op jit(solution)/shard_map/out_far/pallas_call | solution.py:312
  (65 shorter events, 16.8 us)
Async XLA Ops:
  0.0 17.0 %copy-start = (bf16[512,1344]{0,1:T(8,128)(2,1)S(1)}, bf16[512,1344]{0,1:T(8,128)(2,1)}, u32[]{:S(2)}) copy-start(bf16[512,1344]{0,1:T(8,128)(2,1)} %param.14) | copy-start | bytes 4128772
  0.0 14.8 %collective-permute-start = (bf16[1344,512]{1,0:T(8,128)(2,1)}, bf16[1344,512]{1,0:T(8,128)(2,1)}, u32[]{:S(2)}, u32[]{:S(2)}) collective-permute-start(bf16[1344,512]{1,0:T(8,128)(2,1)} %bitcast.10), channel_id=1, source_target_pairs={{0,1},{1,0},{2,3},{3,2},{4,5},{5,4},{6,7},{7,6},{8,9},{9,8},{10,11... | collective-permute-start | bytes 4128776 | tf_op jit(solution)/shard_map/ppermute | solution.py:667
  0.5 33.5 %collective-permute-start.1 = (bf16[1344,512]{1,0:T(8,128)(2,1)}, bf16[1344,512]{1,0:T(8,128)(2,1)S(1)}, u32[]{:S(2)}, u32[]{:S(2)}) collective-permute-start(bf16[1344,512]{1,0:T(8,128)(2,1)} %bitcast.11), channel_id=1, source_target_pairs={{0,2},{2,0},{1,3},{3,1},{4,6},{6,4},{5,7},{7,5},{8,10},{10,8},{9,1... | collective-permute-start | bytes 4128776 | tf_op jit(solution)/shard_map/ppermute | solution.py:664
  3.7 9.9 %copy-start.7 = (s32[16]{0:T(128)S(1)}, s32[16]{0:T(128)}, u32[]{:S(2)}) copy-start(s32[16]{0:T(128)} %param.26) | copy-start | bytes 196
  3.7 13.3 %copy-start.5 = (s32[2]{0:T(128)S(1)}, s32[2]{0:T(128)}, u32[]{:S(2)}) copy-start(s32[2]{0:T(128)} %refs_0_.3) | copy-start | bytes 28
  6.2 17.6 %collective-permute-start.2 = (bf16[64,1344]{1,0:T(8,128)(2,1)}, bf16[64,1344]{1,0:T(8,128)(2,1)}, u32[]{:S(2)}, u32[]{:S(2)}) collective-permute-start(bf16[64,1344]{1,0:T(8,128)(2,1)} %get-tuple-element.31), channel_id=1, source_target_pairs={{0,4},{4,0},{8,12},{12,8},{1,5},{5,1},{9,13},{13,9},{2,6},{6,2},{1... | collective-permute-start | bytes 516104 | tf_op jit(solution)/shard_map/ppermute | solution.py:632
  7.8 16.4 %collective-permute-start.3 = (bf16[64,1344]{1,0:T(8,128)(2,1)}, bf16[64,1344]{1,0:T(8,128)(2,1)}, u32[]{:S(2)}, u32[]{:S(2)}) collective-permute-start(bf16[64,1344]{1,0:T(8,128)(2,1)} %get-tuple-element.32), channel_id=1, source_target_pairs={{0,8},{4,12},{8,0},{12,4},{1,9},{5,13},{9,1},{13,5},{2,10},{6,14},... | collective-permute-start | bytes 516104 | tf_op jit(solution)/shard_map/ppermute | solution.py:632
  10.4 13.8 %collective-permute-start.4 = (bf16[64,1344]{1,0:T(8,128)(2,1)}, bf16[64,1344]{1,0:T(8,128)(2,1)}, u32[]{:S(2)}, u32[]{:S(2)}) collective-permute-start(bf16[64,1344]{1,0:T(8,128)(2,1)} %get-tuple-element.33), channel_id=1, source_target_pairs={{0,12},{4,8},{8,4},{12,0},{1,13},{5,9},{9,5},{13,1},{2,14},{6,10},... | collective-permute-start | bytes 516104 | tf_op jit(solution)/shard_map/ppermute | solution.py:632
  14.8 14.7 %collective-permute-start.7 = (bf16[64,1920]{1,0:T(8,128)(2,1)}, bf16[64,1920]{1,0:T(8,128)(2,1)}, u32[]{:S(2)}, u32[]{:S(2)}) collective-permute-start(bf16[64,1920]{1,0:T(8,128)(2,1)} %pack_out.1.refs_6_.refs_0_), channel_id=1, source_target_pairs={{0,4},{4,0},{8,12},{12,8},{1,5},{5,1},{9,13},{13,9},{2,6},{6,2},{1... | collective-permute-start | bytes 737288 | tf_op jit(solution)/shard_map/ppermute | solution.py:679
  25.4 8.6 %collective-permute-start.5 = (bf16[64,1344]{1,0:T(8,128)(2,1)S(1)}, bf16[64,1344]{1,0:T(8,128)(2,1)S(1)}, u32[]{:S(2)}, u32[]{:S(2)}) collective-permute-start(bf16[64,1344]{1,0:T(8,128)(2,1)S(1)} %sum.1.refs_2_), channel_id=1, source_target_pairs={{0,4},{4,0},{8,12},{12,8},{1,5},{5,1},{9,13},{13,9},{2,6},{6,2},{1... | collective-permute-start | bytes 516104 | tf_op jit(solution)/shard_map/ppermute | solution.py:636
  28.8 5.2 %collective-permute-start.6 = (bf16[64,1344]{1,0:T(8,128)(2,1)S(1)}, bf16[64,1344]{1,0:T(8,128)(2,1)S(1)}, u32[]{:S(2)}, u32[]{:S(2)}) collective-permute-start(bf16[64,1344]{1,0:T(8,128)(2,1)S(1)} %sum.1.refs_2_), channel_id=1, source_target_pairs={{4,8},{8,4},{5,9},{9,5},{6,10},{10,6},{7,11},{11,7},{20,24},{24,20... | collective-permute-start | bytes 516104 | tf_op jit(solution)/shard_map/ppermute | solution.py:638
  34.0 3.1 %collective-permute-start.8 = (bf16[1344,512]{1,0:T(8,128)(2,1)S(1)}, bf16[1344,512]{1,0:T(8,128)(2,1)S(1)}, u32[]{:S(2)}, u32[]{:S(2)}) collective-permute-start(bf16[1344,512]{1,0:T(8,128)(2,1)S(1)} %collective-permute-done.1.refs_1_), channel_id=1, source_target_pairs={{0,1},{1,0},{2,3},{3,2},{4,5},{5,4},{6,7},{7,6},{8,9},{9,8},{10,11... | collective-permute-start | bytes 4128776 | tf_op jit(solution)/shard_map/ppermute | solution.py:667
  34.0 7.2 %collective-permute-start.9 = (bf16[64,1344]{1,0:T(8,128)(2,1)S(1)}, bf16[64,1344]{1,0:T(8,128)(2,1)S(1)}, u32[]{:S(2)}, u32[]{:S(2)}) collective-permute-start(bf16[64,1344]{1,0:T(8,128)(2,1)S(1)} %collective-permute-done.5.refs_6_.refs_3_), channel_id=1, source_target_pairs={{4,8},{8,4},{5,9},{9,5},{6,10},{10,6},{7,11},{11,7},{20,24},{24,20... | collective-permute-start | bytes 516104 | tf_op jit(solution)/shard_map/ppermute | solution.py:638
  41.2 15.2 %copy-start.3 = (f32[128]{0:T(128)S(1)}, f32[128]{0:T(128)}, u32[]{:S(2)}) copy-start(f32[128]{0:T(128)} %param.20) | copy-start | bytes 1540
  41.2 15.1 %copy-start.6 = (f32[128]{0:T(128)S(1)}, f32[128]{0:T(128)}, u32[]{:S(2)}) copy-start(f32[128]{0:T(128)} %param.19) | copy-start | bytes 1540
  42.3 4.0 %collective-permute-start.10 = (f32[96,512]{1,0:T(8,128)S(1)}, f32[96,512]{1,0:T(8,128)S(1)}, u32[]{:S(2)}, u32[]{:S(2)}) collective-permute-start(f32[96,512]{1,0:T(8,128)S(1)} %get-tuple-element.43), channel_id=1, source_target_pairs={{0,1},{1,0},{2,3},{3,2},{4,5},{5,4},{6,7},{7,6},{8,9},{9,8},{10,11... | collective-permute-start | bytes 589832 | tf_op jit(solution)/shard_map/ppermute | solution.py:667
  42.5 12.5 %collective-permute-start.13 = (bf16[512,256]{1,0:T(8,128)(2,1)S(1)}, bf16[512,256]{1,0:T(8,128)(2,1)S(1)}, u32[]{:S(2)}, u32[]{:S(2)}) collective-permute-start(bf16[512,256]{1,0:T(8,128)(2,1)S(1)} %get-tuple-element.39.refs_6_.refs_4_), channel_id=1, source_target_pairs={{0,4},{4,8},{8,12},{12,0},{1,5},{5,9},{9,13},{13,1},{2,6},{6,10},{... | collective-permute-start | bytes 786440 | tf_op jit(solution)/shard_map/ppermute | solution.py:670
  46.3 7.0 %collective-permute-start.11 = (f32[96,512]{1,0:T(8,128)S(1)}, f32[96,512]{1,0:T(8,128)S(1)}, u32[]{:S(2)}, u32[]{:S(2)}) collective-permute-start(f32[96,512]{1,0:T(8,128)S(1)} %add.25), channel_id=1, source_target_pairs={{0,2},{2,0},{1,3},{3,1},{4,6},{6,4},{5,7},{7,5},{8,10},{10,8},{9,1... | collective-permute-start | bytes 589832 | tf_op jit(solution)/shard_map/ppermute | solution.py:664
  47.5 13.9 %collective-permute-start.12 = (bf16[512,256]{1,0:T(8,128)(2,1)S(1)}, bf16[512,256]{1,0:T(8,128)(2,1)S(1)}, u32[]{:S(2)}, u32[]{:S(2)}) collective-permute-start(bf16[512,256]{1,0:T(8,128)(2,1)S(1)} %get-tuple-element.42.refs_6_.refs_3_), channel_id=1, source_target_pairs={{0,4},{4,8},{8,12},{12,0},{1,5},{5,9},{9,13},{13,1},{2,6},{6,10},{... | collective-permute-start | bytes 786440 | tf_op jit(solution)/shard_map/ppermute | solution.py:670
  53.4 8.0 %collective-permute-start.14 = (bf16[64,512]{1,0:T(8,128)(2,1)S(1)}, bf16[64,512]{1,0:T(8,128)(2,1)S(1)}, u32[]{:S(2)}, u32[]{:S(2)}) collective-permute-start(bf16[64,512]{1,0:T(8,128)(2,1)S(1)} %slice.7), channel_id=1, source_target_pairs={{0,4},{4,8},{8,12},{12,0},{1,5},{5,9},{9,13},{13,1},{2,6},{6,10},{... | collective-permute-start | bytes 196616 | tf_op jit(solution)/shard_map/ppermute | solution.py:670
  55.1 12.4 %collective-permute-start.16 = (bf16[512,256]{1,0:T(8,128)(2,1)S(1)}, bf16[512,256]{1,0:T(8,128)(2,1)S(1)}, u32[]{:S(2)}, u32[]{:S(2)}) collective-permute-start(bf16[512,256]{1,0:T(8,128)(2,1)S(1)} %collective-permute-done.13.refs_5_), channel_id=1, source_target_pairs={{0,4},{4,8},{8,12},{12,0},{1,5},{5,9},{9,13},{13,1},{2,6},{6,10},{... | collective-permute-start | bytes 786440 | tf_op jit(solution)/shard_map/ppermute | solution.py:670
  61.4 14.7 %collective-permute-start.15 = (bf16[512,256]{1,0:T(8,128)(2,1)S(1)}, bf16[512,256]{1,0:T(8,128)(2,1)S(1)}, u32[]{:S(2)}, u32[]{:S(2)}) collective-permute-start(bf16[512,256]{1,0:T(8,128)(2,1)S(1)} %collective-permute-done.12.refs_4_), channel_id=1, source_target_pairs={{0,4},{4,8},{8,12},{12,0},{1,5},{5,9},{9,13},{13,1},{2,6},{6,10},{... | collective-permute-start | bytes 786440 | tf_op jit(solution)/shard_map/ppermute | solution.py:670
  62.4 10.5 %collective-permute-start.17 = (bf16[64,512]{1,0:T(8,128)(2,1)S(1)}, bf16[64,512]{1,0:T(8,128)(2,1)S(1)}, u32[]{:S(2)}, u32[]{:S(2)}) collective-permute-start(bf16[64,512]{1,0:T(8,128)(2,1)S(1)} %collective-permute-done.14.refs_6_), channel_id=1, source_target_pairs={{0,4},{4,8},{8,12},{12,0},{1,5},{5,9},{9,13},{13,1},{2,6},{6,10},{... | collective-permute-start | bytes 196616 | tf_op jit(solution)/shard_map/ppermute | solution.py:670
  74.6 9.3 %collective-permute-start.24 = (bf16[512,256]{1,0:T(8,128)(2,1)S(1)}, bf16[512,256]{1,0:T(8,128)(2,1)S(1)}, u32[]{:S(2)}, u32[]{:S(2)}) collective-permute-start(bf16[512,256]{1,0:T(8,128)(2,1)S(1)} %attend_far.2.refs_11_.refs_2_.refs_1_), channel_id=1, source_target_pairs={{0,2},{2,0},{1,3},{3,1},{4,6},{6,4},{5,7},{7,5},{8,10},{10,8},{9,1... | collective-permute-start | bytes 786440 | tf_op jit(solution)/shard_map/ppermute | solution.py:664
  78.2 9.5 %collective-permute-start.18 = (bf16[512,256]{1,0:T(8,128)(2,1)S(1)}, bf16[512,256]{1,0:T(8,128)(2,1)S(1)}, u32[]{:S(2)}, u32[]{:S(2)}) collective-permute-start(bf16[512,256]{1,0:T(8,128)(2,1)S(1)} %attend_far.3.refs_1_.refs_4_), channel_id=1, source_target_pairs={{0,2},{2,0},{1,3},{3,1},{4,6},{6,4},{5,7},{7,5},{8,10},{10,8},{9,1... | collective-permute-start | bytes 786440 | tf_op jit(solution)/shard_map/ppermute | solution.py:664
  78.8 13.2 %collective-permute-start.21 = (bf16[64,1920]{1,0:T(8,128)(2,1)S(1)}, bf16[64,1920]{1,0:T(8,128)(2,1)S(1)}, u32[]{:S(2)}, u32[]{:S(2)}) collective-permute-start(bf16[64,1920]{1,0:T(8,128)(2,1)S(1)} %out_add.1.refs_3_.refs_6_), channel_id=1, source_target_pairs={{0,8},{4,12},{8,0},{12,4},{1,9},{5,13},{9,1},{13,5},{2,10},{6,14},... | collective-permute-start | bytes 737288 | tf_op jit(solution)/shard_map/ppermute | solution.py:679
  81.6 13.8 %collective-permute-start.26 = (bf16[512,256]{1,0:T(8,128)(2,1)S(1)}, bf16[512,256]{1,0:T(8,128)(2,1)S(1)}, u32[]{:S(2)}, u32[]{:S(2)}) collective-permute-start(bf16[512,256]{1,0:T(8,128)(2,1)S(1)} %attend_far.2.refs_11_.refs_2_.refs_1_), channel_id=1, source_target_pairs={{0,1},{1,0},{2,3},{3,2},{4,5},{5,4},{6,7},{7,6},{8,9},{9,8},{10,11... | collective-permute-start | bytes 786440 | tf_op jit(solution)/shard_map/ppermute | solution.py:667
  81.6 16.9 %collective-permute-start.20 = (bf16[512,256]{1,0:T(8,128)(2,1)S(1)}, bf16[512,256]{1,0:T(8,128)(2,1)S(1)}, u32[]{:S(2)}, u32[]{:S(2)}) collective-permute-start(bf16[512,256]{1,0:T(8,128)(2,1)S(1)} %attend_far.3.refs_1_.refs_4_), channel_id=1, source_target_pairs={{0,1},{1,0},{2,3},{3,2},{4,5},{5,4},{6,7},{7,6},{8,9},{9,8},{10,11... | collective-permute-start | bytes 786440 | tf_op jit(solution)/shard_map/ppermute | solution.py:667
  83.9 16.0 %collective-permute-start.25 = (bf16[512,256]{1,0:T(8,128)(2,1)S(1)}, bf16[512,256]{1,0:T(8,128)(2,1)S(1)}, u32[]{:S(2)}, u32[]{:S(2)}) collective-permute-start(bf16[512,256]{1,0:T(8,128)(2,1)S(1)} %collective-permute-done.24.refs_1_), channel_id=1, source_target_pairs={{0,1},{1,0},{2,3},{3,2},{4,5},{5,4},{6,7},{7,6},{8,9},{9,8},{10,11... | collective-permute-start | bytes 786440 | tf_op jit(solution)/shard_map/ppermute | solution.py:667
  87.7 14.8 %collective-permute-start.19 = (bf16[512,256]{1,0:T(8,128)(2,1)S(1)}, bf16[512,256]{1,0:T(8,128)(2,1)S(1)}, u32[]{:S(2)}, u32[]{:S(2)}) collective-permute-start(bf16[512,256]{1,0:T(8,128)(2,1)S(1)} %collective-permute-done.18.refs_1_), channel_id=1, source_target_pairs={{0,1},{1,0},{2,3},{3,2},{4,5},{5,4},{6,7},{7,6},{8,9},{9,8},{10,11... | collective-permute-start | bytes 786440 | tf_op jit(solution)/shard_map/ppermute | solution.py:667
  92.8 1.3 %collective-permute-start.22 = (f32[32,512]{1,0:T(8,128)S(1)}, f32[32,512]{1,0:T(8,128)S(1)}, u32[]{:S(2)}, u32[]{:S(2)}) collective-permute-start(f32[32,512]{1,0:T(8,128)S(1)} %out_low.1), channel_id=1, source_target_pairs={{0,1},{1,0},{2,3},{3,2},{4,5},{5,4},{6,7},{7,6},{8,9},{9,8},{10,11... | collective-permute-start | bytes 196616 | tf_op jit(solution)/shard_map/ppermute | solution.py:667
  94.1 4.3 %collective-permute-start.23 = (f32[32,512]{1,0:T(8,128)S(1)}, f32[32,512]{1,0:T(8,128)S(1)}, u32[]{:S(2)}, u32[]{:S(2)}) collective-permute-start(f32[32,512]{1,0:T(8,128)S(1)} %add.27), channel_id=1, source_target_pairs={{0,2},{2,0},{1,3},{3,1},{4,6},{6,4},{5,7},{7,5},{8,10},{10,8},{9,1... | collective-permute-start | bytes 196616 | tf_op jit(solution)/shard_map/ppermute | solution.py:664
  (3 other events, 8.5 us)

commit v4 on v3

--- a/solution.py
+++ b/solution.py
@@ -377,8 +377,10 @@
         out[rows, 1408:1920] = (out_down[slot].astype(F32) * keep).astype(BF16)
 
 
-def add_kernel(a, b, out):
-    out[...] = a[...] + b[...]
+def add_kernel(a, b, up, down):
+    width = up.shape[1]
+    up[...] = a[:, 0:width] + b[:, 0:width]
+    down[...] = a[:, 1408:1920] + b[:, 1408:1920]
 
 
 def sum_kernel(a, b, c, d, out):
@@ -601,7 +603,7 @@
 
 
 def out_low_kernel(meta, att0, att1, panel_a, panel_b, low):
-    down = panel_a[:, 1408:1920] + panel_b[:, 1408:1920]
+    down = panel_a[...] + panel_b[...]
     both = jnp.concatenate([dot(down, att0[...]), dot(down, att1[...])], axis=1)
     flag = request_flag(meta)
     low[...] = both[0:32] * flag + both[32:64] * (1.0 - flag)
@@ -622,7 +624,7 @@
     lows = low[:, tok].astype(BF16).astype(F32)
     flag = request_flag(meta)[:, tok]
     chosen = jnp.concatenate([lows * flag, lows * (1.0 - flag)], axis=0).astype(BF16)
-    up = panel_a[:, 0 : w.shape[0]] + panel_b[:, 0 : w.shape[0]]
+    up = panel_a[...] + panel_b[...]
     first, second = part_lanes(meta, (1 - meta[2]) * 2, own.shape[0])
     total = part[...] + adapter_scale * dot_t(up, chosen)
     out[...] = (total + dot(w[:, first], own[...]) + dot(w[:, second], other[...])).astype(BF16)
@@ -742,8 +744,16 @@
 
     quarter = call(sum_kernel, "sum", shape((64, width)), [VM] * 4, received, after=[near[0], cosine, sine])
     pieces = share_quarter(quarter)
-    out_pair = call(add_kernel, "out_add", shape((64, 1920)), [VM] * 2, [out_panel, out_beside], after=[quarter])
-    far_other = core(after(far_own, pieces[1], pieces[2], out_pair))
+    up_pair, down_pair = call(
+        add_kernel,
+        "out_add",
+        (shape((64, width)), shape((64, cols))),
+        [VM] * 2,
+        [out_panel, out_beside],
+        after=[quarter],
+    )
+    down_rest = swapped(down_pair, 2)
+    far_other = core(after(far_own, pieces[1], pieces[2], down_pair))
     late_q, late_kv = project(1, pieces[1])
     early_q, early_kv = project(0, late_kv)
     partial_low, ups = call(
@@ -795,38 +805,43 @@
             after=order,
         )
 
-    att_late = attend_far(1, [prev2_late], [])
+    att_late = attend_far(1, [prev2_late], [down_rest])
     att_early = attend_far(0, [prev2_early, prev2_late], [att_late])
 
-    out_rest = swapped(out_pair, 2)
+    up_rest = swapped(up_pair, 2)
+    crossed = [(chunk, across(att)) for chunk, att in ((1, att_late), (0, att_early))]
+    parts = []
+    for att in (att_late, att_early):
+        parts.append(
+            call(
+                out_near_kernel,
+                "out_near",
+                shape((width, CHUNK), F32),
+                [SM] + [VM] * 3,
+                [meta, att, core(att), out_weights],
+                after=[att_early] + parts,
+            )
+        )
     out_low = call(
         out_low_kernel,
         "out_low",
         shape((32, rows), F32),
         [SM] + [VM] * 4,
-        [meta, att_early, att_late, out_pair, out_rest],
+        [meta, att_early, att_late, down_pair, down_rest],
+        after=[parts[1]],
     )
     out_low = out_low + core(out_low)
     out_low = out_low + across(out_low)
 
     result = []
-    for chunk, att in ((1, att_late), (0, att_early)):
-        att_far = across(att)
-        part = call(
-            out_near_kernel,
-            "out_near",
-            shape((width, CHUNK), F32),
-            [SM] + [VM] * 3,
-            [meta, att, core(att), out_weights],
-            after=[att_early],
-        )
+    for (chunk, att_far), part in zip(crossed, parts):
         result = [
             call(
                 functools.partial(out_far_kernel, chunk),
                 "out_far",
                 shape((width, rows)),
                 [SM] + [VM] * 7 + [HB] * len(result),
-                [meta, att_far, core(att_far), out_weights, part, out_low, out_pair, out_rest, *result],
+                [meta, att_far, core(after(att_far, out_low, up_rest)), out_weights, part, out_low, up_pair, up_rest, *result],
                 out_specs=pl.BlockSpec((width, CHUNK), lambda i, chunk=chunk: (0, chunk)),
                 grid=(1,),
                 aliases={8: 0} if result else {},

time: 105 us -> 103 us (0.981)
  waiting for transfers between devices: 28.9 us -> 23.7 us
  starting transfers between devices: 31.9 us -> 34.2 us
    ppermute x6, waiting for transfers between devices: 5.4 us -> 0.02 us  [up(): return lax.ppermute(value, 'seq', [(i, (i + by) % 4) for i in range(4)])]
    ppermute x5, waiting for transfers between devices: 15 us -> 12.2 us  [across(): return lax.ppermute(value, 'head', SWAP)]
    ppermute x2 -> x3, starting transfers between devices: 3.47 us -> 5.56 us  [swapped(): return lax.ppermute(value, 'seq', [(j, j ^ by) for j in range(4)])]
    ppermute x2 -> x3, waiting for transfers between devices: 4.36 us -> 6.35 us  [swapped(): return lax.ppermute(value, 'seq', [(j, j ^ by) for j in range(4)])]
  transfers between devices with their start and end apart: 27 -> 28, of which waited for: 10 -> 8; matrix products, arithmetic and copies ran while one was open for 2% -> 2% of each run, Pallas kernels for 34% -> 35%
where the time goes in v4:
time: 103 us; the launch traced here: 102 us
  Pallas kernels  39.8 us (39%)
  starting transfers between devices  34.2 us (33%)
  waiting for transfers between devices  23.7 us (23%)
  other arithmetic  2.16 us (2%)
  local copies, waits for them, and re-layouts  1.44 us (1%)
    pallas_call x17, Pallas kernels, call(): pl.pallas_call(body, out_shape=out_shape, in_specs=list(in_specs) + [HB]...  39.8 us
    ppermute x5, waiting for transfers between devices, across(): return lax.ppermute(value, 'head', SWAP)  12.2 us
    ppermute x6, starting transfers between devices, up(): return lax.ppermute(value, 'seq', [(i, (i + by) % 4) for i in range(4)])  10.6 us
    ppermute x5, starting transfers between devices, across(): return lax.ppermute(value, 'head', SWAP)  6.91 us
    ppermute x3, waiting for transfers between devices, swapped(): return lax.ppermute(value, 'seq', [(j, j ^ by) for j in range(4)])  6.35 us
    ppermute x3, starting transfers between devices, swapped(): return lax.ppermute(value, 'seq', [(j, j ^ by) for j in range(4)])  5.56 us
    ppermute x8, waiting for transfers between devices, core(): return lax.ppermute(value, 'rep', SWAP)  4.72 us
    ppermute x3, starting transfers between devices, exchange_quarters(): lax.ppermute(quarters[s], 'seq', [(j, j ^ s) for j in range(4)])  4.45 us
  transfers between devices with their start and end apart: 28, of which 8 were waited for; matrix products, arithmetic and copies ran while one was open for 2% of the time, Pallas kernels for 35%

profile of v4, /device:TPU:0, one launch (start us, length us, event | category | flops | bytes accessed | tf_op | source)
XLA Modules:
  0.0 102.2 jit_solution(1036314907095355733)
XLA Ops:
  0.5 2.5 %collective-permute-start.1 = (bf16[1344,512]{1,0:T(8,128)(2,1)}, bf16[1344,512]{1,0:T(8,128)(2,1)S(1)}, u32[]{:S(2)}, u32[]{:S(2)}) collective-permute-start(bf16[1344,512]{1,0:T(8,128)(2,1)} %bitcast.11), channel_id=1, source_target_pairs={{0,2},{2,0},{1,3},{3,1},{4,6},{6,4},{5,7},{7,5},{8,10},{10,8},{9,1... | collective-permute-start | bytes 4128776 | tf_op jit(solution)/shard_map/ppermute | solution.py:666
  3.7 2.5 %pack.1 = (bf16[64,1344]{1,0:T(8,128)(2,1)S(1)}, bf16[64,1344]{1,0:T(8,128)(2,1)}, bf16[64,1344]{1,0:T(8,128)(2,1)}, bf16[64,1344]{1,0:T(8,128)(2,1)}) custom-call(s32[2]{0:T(128)S(1)} %copy-done.4, bf16[2,96,1344]{2,1,0:T(8,128)(2,1)} %bitcast.20, bf16[2,32,512]{2,1,0:T(8,128)(2,1)} %refs_2_.2, bf16[2,2,32,512]{3,2,1,0:T(8,128)(2,1)} %refs_3_.2), custom_call_target="tpu_custom_call" | custom-call | flops 1000 | bytes 1000 | tf_op jit(solution)/shard_map/pack/pallas_call | solution.py:312
  6.2 1.6 %collective-permute-start.2 = (bf16[64,1344]{1,0:T(8,128)(2,1)}, bf16[64,1344]{1,0:T(8,128)(2,1)}, u32[]{:S(2)}, u32[]{:S(2)}) collective-permute-start(bf16[64,1344]{1,0:T(8,128)(2,1)} %get-tuple-element.35), channel_id=1, source_target_pairs={{0,4},{4,0},{8,12},{12,8},{1,5},{5,1},{9,13},{13,9},{2,6},{6,2},{1... | collective-permute-start | bytes 516104 | tf_op jit(solution)/shard_map/ppermute | solution.py:634
  7.8 2.6 %collective-permute-start.3 = (bf16[64,1344]{1,0:T(8,128)(2,1)}, bf16[64,1344]{1,0:T(8,128)(2,1)}, u32[]{:S(2)}, u32[]{:S(2)}) collective-permute-start(bf16[64,1344]{1,0:T(8,128)(2,1)} %get-tuple-element.36), channel_id=1, source_target_pairs={{0,8},{4,12},{8,0},{12,4},{1,9},{5,13},{9,1},{13,5},{2,10},{6,14},... | collective-permute-start | bytes 516104 | tf_op jit(solution)/shard_map/ppermute | solution.py:634
  10.6 2.3 %pack_out.1.refs_6_.refs_0_ = bf16[64,1920]{1,0:T(8,128)(2,1)} custom-call(s32[2]{0:T(128)S(1)} %copy-done.4, bf16[2,32,512]{2,1,0:T(8,128)(2,1)} %bitcast.21, bf16[2,32,1344]{2,1,0:T(8,128)(2,1)} %refs_2_.3, bf16[64,1344]{1,0:T(8,128)(2,1)S(1)} %get-tuple-element.33.refs_3_.refs_0_), custom_call_target="tpu_custom_call" | custom-call | flops 1000 | bytes 1000 | tf_op jit(solution)/shard_map/pack_out/pallas_call | solution.py:312
  15.5 1.4 %multiply_sine_fusion = (f32[64,1536]{1,0:T(8,128)S(1)}, f32[64,1536]{1,0:T(8,128)S(1)}) fusion(f32[1536]{0:T(1024)S(1)} %fusion, f32[64]{0:T(128)S(1)} %multiply_power_fusion), kind=kLoop, calls=%fused_computation | loop fusion | flops 98304 | bytes 792832 | tf_op jit(solution)/shard_map/sin | solution.py:741
  17.1 6.7 %near.1 = (f32[256,1024]{1,0:T(8,128)S(1)}, f32[256,1024]{1,0:T(8,128)S(1)}, bf16[2,1344,256]{2,1,0:T(8,128)(2,1)S(1)}, bf16[2,1344,256]{2,1,0:T(8,128)(2,1)S(1)}, bf16[2,1344,512]{2,1,0:T(8,128)(2,1)S(1)}) custom-call(s32[21]{0:T(128)S(1)} %concatenate.3.refs_0_, bf16[1344,512]{1,0:T(8,128)(2,1)S(1)} %bitcast.12, ...), custom_call_target="tpu_custom_call" | custom-call | flops 1000 | bytes 1000 | tf_op jit(solution)/shard_map/near/pallas_call | solution.py:312
  25.4 3.4 %collective-permute-start.5 = (bf16[64,1344]{1,0:T(8,128)(2,1)S(1)}, bf16[64,1344]{1,0:T(8,128)(2,1)S(1)}, u32[]{:S(2)}, u32[]{:S(2)}) collective-permute-start(bf16[64,1344]{1,0:T(8,128)(2,1)S(1)} %sum.1.refs_2_), channel_id=1, source_target_pairs={{0,4},{4,0},{8,12},{12,8},{1,5},{5,1},{9,13},{13,9},{2,6},{6,2},{1... | collective-permute-start | bytes 516104 | tf_op jit(solution)/shard_map/ppermute | solution.py:638
  30.6 3.4 %collective-permute-done.1.refs_1_ = bf16[1344,512]{1,0:T(8,128)(2,1)S(1)} collective-permute-done((bf16[1344,512]{1,0:T(8,128)(2,1)}, bf16[1344,512]{1,0:T(8,128)(2,1)S(1)}, u32[]{:S(2)}, u32[]{:S(2)}) %collective-permute-start.1) | collective-permute-done | bytes 1376288 | tf_op jit(solution)/shard_map/ppermute | solution.py:666
  34.7 2.4 %collective-permute-done.8.refs_2_ = bf16[1344,512]{1,0:T(8,128)(2,1)S(1)} collective-permute-done((bf16[1344,512]{1,0:T(8,128)(2,1)S(1)}, bf16[1344,512]{1,0:T(8,128)(2,1)S(1)}, u32[]{:S(2)}, u32[]{:S(2)}) %collective-permute-start.8) | collective-permute-done | bytes 1376288 | tf_op jit(solution)/shard_map/ppermute | solution.py:669
  37.1 2.0 %far.2 = (f32[512,256]{1,0:T(8,128)S(1)}, bf16[512,256]{1,0:T(8,128)(2,1)S(1)}) custom-call(f32[256,1024]{1,0:T(8,128)S(1)} %get-tuple-element.43.refs_0_, bf16[1344,512]{1,0:T(8,128)(2,1)S(1)} %collective-permute-done.1.refs_1_, bf16[1344,512]{1,0:T(8,128)(2,1)S(1)} %collective-permute-done.8.refs_2_, bf16[2,1344,256]{2,1,0:T(8,128)(2,1)S(1)} %get-tuple-element.40.refs_3_, ...), custom_call_target="tpu_custom_call" | custom-call | flops 1000 | bytes 1000 | tf_op jit(solution)/shard_map/far/pallas_call | solution.py:312
  39.2 2.0 %far.3 = (f32[512,256]{1,0:T(8,128)S(1)}, bf16[512,256]{1,0:T(8,128)(2,1)S(1)}) custom-call(f32[256,1024]{1,0:T(8,128)S(1)} %get-tuple-element.34.refs_4_.refs_0_, bf16[1344,512]{1,0:T(8,128)(2,1)S(1)} %collective-permute-done.1.refs_1_, bf16[1344,512]{1,0:T(8,128)(2,1)S(1)} %collective-permute-done.8.refs_2_, ...), custom_call_target="tpu_custom_call" | custom-call | flops 1000 | bytes 1000 | tf_op jit(solution)/shard_map/far/pallas_call | solution.py:312
  42.5 3.8 %collective-permute-start.13 = (bf16[512,256]{1,0:T(8,128)(2,1)S(1)}, bf16[512,256]{1,0:T(8,128)(2,1)S(1)}, u32[]{:S(2)}, u32[]{:S(2)}) collective-permute-start(bf16[512,256]{1,0:T(8,128)(2,1)S(1)} %get-tuple-element.44.refs_6_.refs_4_), channel_id=1, source_target_pairs={{0,4},{4,8},{8,12},{12,0},{1,5},{5,9},{9,13},{13,1},{2,6},{6,10},{... | collective-permute-start | bytes 786440 | tf_op jit(solution)/shard_map/ppermute | solution.py:672
  47.5 1.6 %collective-permute-start.12 = (bf16[512,256]{1,0:T(8,128)(2,1)S(1)}, bf16[512,256]{1,0:T(8,128)(2,1)S(1)}, u32[]{:S(2)}, u32[]{:S(2)}) collective-permute-start(bf16[512,256]{1,0:T(8,128)(2,1)S(1)} %get-tuple-element.47.refs_6_.refs_3_), channel_id=1, source_target_pairs={{0,4},{4,8},{8,12},{12,0},{1,5},{5,9},{9,13},{13,1},{2,6},{6,10},{... | collective-permute-start | bytes 786440 | tf_op jit(solution)/shard_map/ppermute | solution.py:672
  49.1 4.3 %collective-permute-done.11 = f32[96,512]{1,0:T(8,128)S(1)} collective-permute-done((f32[96,512]{1,0:T(8,128)S(1)}, f32[96,512]{1,0:T(8,128)S(1)}, u32[]{:S(2)}, u32[]{:S(2)}) %collective-permute-start.11) | collective-permute-done | bytes 196640 | tf_op jit(solution)/shard_map/ppermute | solution.py:666
  53.4 1.6 %collective-permute-start.14 = (bf16[64,512]{1,0:T(8,128)(2,1)S(1)}, bf16[64,512]{1,0:T(8,128)(2,1)S(1)}, u32[]{:S(2)}, u32[]{:S(2)}) collective-permute-start(bf16[64,512]{1,0:T(8,128)(2,1)S(1)} %slice.7), channel_id=1, source_target_pairs={{0,4},{4,8},{8,12},{12,0},{1,5},{5,9},{9,13},{13,1},{2,6},{6,10},{... | collective-permute-start | bytes 196616 | tf_op jit(solution)/shard_map/ppermute | solution.py:672
  55.0 1.3 %collective-permute-start.16 = (bf16[512,256]{1,0:T(8,128)(2,1)S(1)}, bf16[512,256]{1,0:T(8,128)(2,1)S(1)}, u32[]{:S(2)}, u32[]{:S(2)}) collective-permute-start(bf16[512,256]{1,0:T(8,128)(2,1)S(1)} %collective-permute-done.13.refs_5_), channel_id=1, source_target_pairs={{0,4},{4,8},{8,12},{12,0},{1,5},{5,9},{9,13},{13,1},{2,6},{6,10},{... | collective-permute-start | bytes 786440 | tf_op jit(solution)/shard_map/ppermute | solution.py:672
  56.4 5.0 %attend_own.1 = (bf16[512,512]{1,0:T(8,128)(2,1)S(1)}, f32[512,512]{1,0:T(8,128)S(1)}, f32[8,512]{1,0:T(8,128)S(1)}, bf16[1344,2048]{1,0:T(8,128)(2,1)S(1)}) custom-call(s32[21]{0:T(128)S(1)} %concatenate.3.refs_0_, f32[512,256]{1,0:T(8,128)S(1)} %get-tuple-element.45.refs_1_, f32[512,256]{1,0:T(8,128)S(1)} %get-tuple-element.46.refs_2_, ...), custom_call_target="tpu_custom_call" | custom-call | flops 1000 | bytes 1000 | tf_op jit(solution)/shard_map/attend_own/pallas_call | solution.py:312
  62.4 2.1 %collective-permute-start.18 = (bf16[64,512]{1,0:T(8,128)(2,1)S(1)}, bf16[64,512]{1,0:T(8,128)(2,1)S(1)}, u32[]{:S(2)}, u32[]{:S(2)}) collective-permute-start(bf16[64,512]{1,0:T(8,128)(2,1)S(1)} %get-tuple-element.38.refs_3_), channel_id=1, source_target_pairs={{0,8},{4,12},{8,0},{12,4},{1,9},{5,13},{9,1},{13,5},{2,10},{6,14},... | collective-permute-start | bytes 196616 | tf_op jit(solution)/shard_map/ppermute | solution.py:681
  64.5 1.3 %collective-permute-start.17 = (bf16[64,512]{1,0:T(8,128)(2,1)S(1)}, bf16[64,512]{1,0:T(8,128)(2,1)S(1)}, u32[]{:S(2)}, u32[]{:S(2)}) collective-permute-start(bf16[64,512]{1,0:T(8,128)(2,1)S(1)} %collective-permute-done.14.refs_6_), channel_id=1, source_target_pairs={{0,4},{4,8},{8,12},{12,0},{1,5},{5,9},{9,13},{13,1},{2,6},{6,10},{... | collective-permute-start | bytes 196616 | tf_op jit(solution)/shard_map/ppermute | solution.py:672
  65.9 3.5 %attend_prev.1 = (f32[512,512]{1,0:T(8,128)S(1)}, f32[8,512]{1,0:T(8,128)S(1)}) custom-call(s32[21]{0:T(128)S(1)} %concatenate.3.refs_0_, bf16[512,512]{1,0:T(8,128)(2,1)S(1)} %get-tuple-element.50.refs_1_, f32[512,512]{1,0:T(8,128)S(1)} %get-tuple-element.51.refs_2_, f32[8,512]{1,0:T(8,128)S(1)} %get-tuple-element.52.refs_3_, ...), custom_call_target="tpu_custom_call" | custom-call | flops 1000 | bytes 1000 | tf_op jit(solution)/shard_map/attend_prev/pallas_call | solution.py:312
  69.4 6.3 %collective-permute-done.18.refs_10_.refs_4_ = bf16[64,512]{1,0:T(8,128)(2,1)S(1)} collective-permute-done((bf16[64,512]{1,0:T(8,128)(2,1)S(1)}, bf16[64,512]{1,0:T(8,128)(2,1)S(1)}, u32[]{:S(2)}, u32[]{:S(2)}) %collective-permute-start.18) | collective-permute-done | bytes 65568 | tf_op jit(solution)/shard_map/ppermute | solution.py:681
  75.7 1.7 %attend_far.2.refs_11_.refs_1_.refs_2_ = bf16[512,256]{1,0:T(8,128)(2,1)S(1)} custom-call(s32[21]{0:T(128)S(1)} %concatenate.3.refs_0_, bf16[512,512]{1,0:T(8,128)(2,1)S(1)} %get-tuple-element.50.refs_1_, f32[512,512]{1,0:T(8,128)S(1)} %get-tuple-element.53.refs_2_, f32[8,512]{1,0:T(8,128)S(1)} %get-tuple-element.54.refs_3_, ...), custom_call_target="tpu_custom_call" | custom-call | flops 1000 | bytes 1000 | tf_op jit(solution)/shard_map/attend_far/pallas_call | solution.py:312
  77.5 2.1 %attend_far.3.refs_4_.refs_1_ = bf16[512,256]{1,0:T(8,128)(2,1)S(1)} custom-call(s32[21]{0:T(128)S(1)} %concatenate.3.refs_0_, bf16[512,512]{1,0:T(8,128)(2,1)S(1)} %get-tuple-element.50.refs_1_, f32[512,512]{1,0:T(8,128)S(1)} %get-tuple-element.53.refs_2_, f32[8,512]{1,0:T(8,128)S(1)} %get-tuple-element.54.refs_3_, ...), custom_call_target="tpu_custom_call" | custom-call | flops 1000 | bytes 1000 | tf_op jit(solution)/shard_map/attend_far/pallas_call | solution.py:312
  80.1 1.5 %collective-permute-start.26 = (bf16[512,256]{1,0:T(8,128)(2,1)S(1)}, bf16[512,256]{1,0:T(8,128)(2,1)S(1)}, u32[]{:S(2)}, u32[]{:S(2)}) collective-permute-start(bf16[512,256]{1,0:T(8,128)(2,1)S(1)} %attend_far.2.refs_11_.refs_1_.refs_2_), channel_id=1, source_target_pairs={{0,2},{2,0},{1,3},{3,1},{4,6},{6,4},{5,7},{7,5},{8,10},{10,8},{9,1... | collective-permute-start | bytes 786440 | tf_op jit(solution)/shard_map/ppermute | solution.py:666
  82.2 2.7 %collective-permute-start.24 = (bf16[64,1344]{1,0:T(8,128)(2,1)S(1)}, bf16[64,1344]{1,0:T(8,128)(2,1)S(1)}, u32[]{:S(2)}, u32[]{:S(2)}) collective-permute-start(bf16[64,1344]{1,0:T(8,128)(2,1)S(1)} %get-tuple-element.58.refs_6_), channel_id=1, source_target_pairs={{0,8},{4,12},{8,0},{12,4},{1,9},{5,13},{9,1},{13,5},{2,10},{6,14},... | collective-permute-start | bytes 516104 | tf_op jit(solution)/shard_map/ppermute | solution.py:681
  84.9 1.4 %out_near.2.refs_5_.refs_4_ = f32[1344,256]{1,0:T(8,128)S(1)} custom-call(s32[21]{0:T(128)S(1)} %concatenate.3.refs_0_, bf16[512,256]{1,0:T(8,128)(2,1)S(1)} %attend_far.2.refs_11_.refs_1_.refs_2_, bf16[512,256]{1,0:T(8,128)(2,1)S(1)} %collective-permute-done.21.refs_2_, bf16[1344,2048]{1,0:T(8,128)(2,1)S(1)} %get-tuple-element.57.refs_3_, ...), custom_call_target="tpu_custom_call" | custom-call | flops 1000 | bytes 1000 | tf_op jit(solution)/shard_map/out_near/pallas_call | solution.py:312
  86.3 1.4 %out_near.3.refs_5_.refs_4_ = f32[1344,256]{1,0:T(8,128)S(1)} custom-call(s32[21]{0:T(128)S(1)} %concatenate.3.refs_0_, bf16[512,256]{1,0:T(8,128)(2,1)S(1)} %attend_far.3.refs_4_.refs_1_, bf16[512,256]{1,0:T(8,128)(2,1)S(1)} %collective-permute-done.20.refs_2_, bf16[1344,2048]{1,0:T(8,128)(2,1)S(1)} %get-tuple-element.57.refs_3_, ...), custom_call_target="tpu_custom_call" | custom-call | flops 1000 | bytes 1000 | tf_op jit(solution)/shard_map/out_near/pallas_call | solution.py:312
  88.6 1.2 %collective-permute-done.22 = f32[32,512]{1,0:T(8,128)S(1)} collective-permute-done((f32[32,512]{1,0:T(8,128)S(1)}, f32[32,512]{1,0:T(8,128)S(1)}, u32[]{:S(2)}, u32[]{:S(2)}) %collective-permute-start.22) | collective-permute-done | bytes 65568 | tf_op jit(solution)/shard_map/ppermute | solution.py:669
  91.0 4.4 %collective-permute-done.23 = f32[32,512]{1,0:T(8,128)S(1)} collective-permute-done((f32[32,512]{1,0:T(8,128)S(1)}, f32[32,512]{1,0:T(8,128)S(1)}, u32[]{:S(2)}, u32[]{:S(2)}) %collective-permute-start.23) | collective-permute-done | bytes 65568 | tf_op jit(solution)/shard_map/ppermute | solution.py:666
  97.1 2.6 %out_far.2.refs_8_ = bf16[1344,512]{1,0:T(8,128)(2,1)} custom-call(s32[21]{0:T(128)S(1)} %concatenate.3.refs_0_, bf16[512,256]{1,0:T(8,128)(2,1)S(1)} %collective-permute-done.26.refs_1_, bf16[512,256]{1,0:T(8,128)(2,1)S(1)} %collective-permute-done.27.refs_2_, bf16[1344,2048]{1,0:T(8,128)(2,1)S(1)} %get-tuple-element.57.refs_3_, ...), custom_call_target="tpu_custom_call" | custom-call | flops 1000 | bytes 1000 | tf_op jit(solution)/shard_map/out_far/pallas_call | solution.py:312
  99.7 2.6 %out_far.3 = bf16[1344,512]{1,0:T(8,128)(2,1)} custom-call(s32[21]{0:T(128)S(1)} %concatenate.3.refs_0_, bf16[512,256]{1,0:T(8,128)(2,1)S(1)} %collective-permute-done.19.refs_1_, bf16[512,256]{1,0:T(8,128)(2,1)S(1)} %collective-permute-done.25.refs_2_, bf16[1344,2048]{1,0:T(8,128)(2,1)S(1)} %get-tuple-element.57.refs_3_, ...), custom_call_target="tpu_custom_call", output_to_operand_aliasing={{}: (8, {})} | custom-call | flops 1000 | bytes 1000 | tf_op jit(solution)/shard_map/out_far/pallas_call | solution.py:312
  (67 shorter events, 15.8 us)
Async XLA Ops:
  0.0 17.1 %copy-start = (bf16[512,1344]{0,1:T(8,128)(2,1)S(1)}, bf16[512,1344]{0,1:T(8,128)(2,1)}, u32[]{:S(2)}) copy-start(bf16[512,1344]{0,1:T(8,128)(2,1)} %param.14) | copy-start | bytes 4128772
  0.0 14.8 %collective-permute-start = (bf16[1344,512]{1,0:T(8,128)(2,1)}, bf16[1344,512]{1,0:T(8,128)(2,1)}, u32[]{:S(2)}, u32[]{:S(2)}) collective-permute-start(bf16[1344,512]{1,0:T(8,128)(2,1)} %bitcast.10), channel_id=1, source_target_pairs={{0,1},{1,0},{2,3},{3,2},{4,5},{5,4},{6,7},{7,6},{8,9},{9,8},{10,11... | collective-permute-start | bytes 4128776 | tf_op jit(solution)/shard_map/ppermute | solution.py:669
  0.5 33.5 %collective-permute-start.1 = (bf16[1344,512]{1,0:T(8,128)(2,1)}, bf16[1344,512]{1,0:T(8,128)(2,1)S(1)}, u32[]{:S(2)}, u32[]{:S(2)}) collective-permute-start(bf16[1344,512]{1,0:T(8,128)(2,1)} %bitcast.11), channel_id=1, source_target_pairs={{0,2},{2,0},{1,3},{3,1},{4,6},{6,4},{5,7},{7,5},{8,10},{10,8},{9,1... | collective-permute-start | bytes 4128776 | tf_op jit(solution)/shard_map/ppermute | solution.py:666
  3.7 13.3 %copy-start.5 = (s32[2]{0:T(128)S(1)}, s32[2]{0:T(128)}, u32[]{:S(2)}) copy-start(s32[2]{0:T(128)} %refs_0_.3) | copy-start | bytes 28
  6.2 17.6 %collective-permute-start.2 = (bf16[64,1344]{1,0:T(8,128)(2,1)}, bf16[64,1344]{1,0:T(8,128)(2,1)}, u32[]{:S(2)}, u32[]{:S(2)}) collective-permute-start(bf16[64,1344]{1,0:T(8,128)(2,1)} %get-tuple-element.35), channel_id=1, source_target_pairs={{0,4},{4,0},{8,12},{12,8},{1,5},{5,1},{9,13},{13,9},{2,6},{6,2},{1... | collective-permute-start | bytes 516104 | tf_op jit(solution)/shard_map/ppermute | solution.py:634
  7.8 16.4 %collective-permute-start.3 = (bf16[64,1344]{1,0:T(8,128)(2,1)}, bf16[64,1344]{1,0:T(8,128)(2,1)}, u32[]{:S(2)}, u32[]{:S(2)}) collective-permute-start(bf16[64,1344]{1,0:T(8,128)(2,1)} %get-tuple-element.36), channel_id=1, source_target_pairs={{0,8},{4,12},{8,0},{12,4},{1,9},{5,13},{9,1},{13,5},{2,10},{6,14},... | collective-permute-start | bytes 516104 | tf_op jit(solution)/shard_map/ppermute | solution.py:634
  10.4 13.8 %collective-permute-start.4 = (bf16[64,1344]{1,0:T(8,128)(2,1)}, bf16[64,1344]{1,0:T(8,128)(2,1)}, u32[]{:S(2)}, u32[]{:S(2)}) collective-permute-start(bf16[64,1344]{1,0:T(8,128)(2,1)} %get-tuple-element.37), channel_id=1, source_target_pairs={{0,12},{4,8},{8,4},{12,0},{1,13},{5,9},{9,5},{13,1},{2,14},{6,10},... | collective-permute-start | bytes 516104 | tf_op jit(solution)/shard_map/ppermute | solution.py:634
  14.8 14.7 %collective-permute-start.7 = (bf16[64,1920]{1,0:T(8,128)(2,1)}, bf16[64,1920]{1,0:T(8,128)(2,1)}, u32[]{:S(2)}, u32[]{:S(2)}) collective-permute-start(bf16[64,1920]{1,0:T(8,128)(2,1)} %pack_out.1.refs_6_.refs_0_), channel_id=1, source_target_pairs={{0,4},{4,0},{8,12},{12,8},{1,5},{5,1},{9,13},{13,9},{2,6},{6,2},{1... | collective-permute-start | bytes 737288 | tf_op jit(solution)/shard_map/ppermute | solution.py:681
  25.4 8.6 %collective-permute-start.5 = (bf16[64,1344]{1,0:T(8,128)(2,1)S(1)}, bf16[64,1344]{1,0:T(8,128)(2,1)S(1)}, u32[]{:S(2)}, u32[]{:S(2)}) collective-permute-start(bf16[64,1344]{1,0:T(8,128)(2,1)S(1)} %sum.1.refs_2_), channel_id=1, source_target_pairs={{0,4},{4,0},{8,12},{12,8},{1,5},{5,1},{9,13},{13,9},{2,6},{6,2},{1... | collective-permute-start | bytes 516104 | tf_op jit(solution)/shard_map/ppermute | solution.py:638
  28.8 5.2 %collective-permute-start.6 = (bf16[64,1344]{1,0:T(8,128)(2,1)S(1)}, bf16[64,1344]{1,0:T(8,128)(2,1)S(1)}, u32[]{:S(2)}, u32[]{:S(2)}) collective-permute-start(bf16[64,1344]{1,0:T(8,128)(2,1)S(1)} %sum.1.refs_2_), channel_id=1, source_target_pairs={{4,8},{8,4},{5,9},{9,5},{6,10},{10,6},{7,11},{11,7},{20,24},{24,20... | collective-permute-start | bytes 516104 | tf_op jit(solution)/shard_map/ppermute | solution.py:640
  34.0 3.1 %collective-permute-start.8 = (bf16[1344,512]{1,0:T(8,128)(2,1)S(1)}, bf16[1344,512]{1,0:T(8,128)(2,1)S(1)}, u32[]{:S(2)}, u32[]{:S(2)}) collective-permute-start(bf16[1344,512]{1,0:T(8,128)(2,1)S(1)} %collective-permute-done.1.refs_1_), channel_id=1, source_target_pairs={{0,1},{1,0},{2,3},{3,2},{4,5},{5,4},{6,7},{7,6},{8,9},{9,8},{10,11... | collective-permute-start | bytes 4128776 | tf_op jit(solution)/shard_map/ppermute | solution.py:669
  34.0 7.2 %collective-permute-start.9 = (bf16[64,1344]{1,0:T(8,128)(2,1)S(1)}, bf16[64,1344]{1,0:T(8,128)(2,1)S(1)}, u32[]{:S(2)}, u32[]{:S(2)}) collective-permute-start(bf16[64,1344]{1,0:T(8,128)(2,1)S(1)} %collective-permute-done.5.refs_6_.refs_3_), channel_id=1, source_target_pairs={{4,8},{8,4},{5,9},{9,5},{6,10},{10,6},{7,11},{11,7},{20,24},{24,20... | collective-permute-start | bytes 516104 | tf_op jit(solution)/shard_map/ppermute | solution.py:640
  41.2 15.1 %copy-start.3 = (f32[128]{0:T(128)S(1)}, f32[128]{0:T(128)}, u32[]{:S(2)}) copy-start(f32[128]{0:T(128)} %param.20) | copy-start | bytes 1540
  41.2 15.1 %copy-start.6 = (f32[128]{0:T(128)S(1)}, f32[128]{0:T(128)}, u32[]{:S(2)}) copy-start(f32[128]{0:T(128)} %param.19) | copy-start | bytes 1540
  42.3 4.0 %collective-permute-start.10 = (f32[96,512]{1,0:T(8,128)S(1)}, f32[96,512]{1,0:T(8,128)S(1)}, u32[]{:S(2)}, u32[]{:S(2)}) collective-permute-start(f32[96,512]{1,0:T(8,128)S(1)} %get-tuple-element.48), channel_id=1, source_target_pairs={{0,1},{1,0},{2,3},{3,2},{4,5},{5,4},{6,7},{7,6},{8,9},{9,8},{10,11... | collective-permute-start | bytes 589832 | tf_op jit(solution)/shard_map/ppermute | solution.py:669
  42.5 12.5 %collective-permute-start.13 = (bf16[512,256]{1,0:T(8,128)(2,1)S(1)}, bf16[512,256]{1,0:T(8,128)(2,1)S(1)}, u32[]{:S(2)}, u32[]{:S(2)}) collective-permute-start(bf16[512,256]{1,0:T(8,128)(2,1)S(1)} %get-tuple-element.44.refs_6_.refs_4_), channel_id=1, source_target_pairs={{0,4},{4,8},{8,12},{12,0},{1,5},{5,9},{9,13},{13,1},{2,6},{6,10},{... | collective-permute-start | bytes 786440 | tf_op jit(solution)/shard_map/ppermute | solution.py:672
  46.3 7.0 %collective-permute-start.11 = (f32[96,512]{1,0:T(8,128)S(1)}, f32[96,512]{1,0:T(8,128)S(1)}, u32[]{:S(2)}, u32[]{:S(2)}) collective-permute-start(f32[96,512]{1,0:T(8,128)S(1)} %add.25), channel_id=1, source_target_pairs={{0,2},{2,0},{1,3},{3,1},{4,6},{6,4},{5,7},{7,5},{8,10},{10,8},{9,1... | collective-permute-start | bytes 589832 | tf_op jit(solution)/shard_map/ppermute | solution.py:666
  47.5 13.9 %collective-permute-start.12 = (bf16[512,256]{1,0:T(8,128)(2,1)S(1)}, bf16[512,256]{1,0:T(8,128)(2,1)S(1)}, u32[]{:S(2)}, u32[]{:S(2)}) collective-permute-start(bf16[512,256]{1,0:T(8,128)(2,1)S(1)} %get-tuple-element.47.refs_6_.refs_3_), channel_id=1, source_target_pairs={{0,4},{4,8},{8,12},{12,0},{1,5},{5,9},{9,13},{13,1},{2,6},{6,10},{... | collective-permute-start | bytes 786440 | tf_op jit(solution)/shard_map/ppermute | solution.py:672
  53.4 8.0 %collective-permute-start.14 = (bf16[64,512]{1,0:T(8,128)(2,1)S(1)}, bf16[64,512]{1,0:T(8,128)(2,1)S(1)}, u32[]{:S(2)}, u32[]{:S(2)}) collective-permute-start(bf16[64,512]{1,0:T(8,128)(2,1)S(1)} %slice.7), channel_id=1, source_target_pairs={{0,4},{4,8},{8,12},{12,0},{1,5},{5,9},{9,13},{13,1},{2,6},{6,10},{... | collective-permute-start | bytes 196616 | tf_op jit(solution)/shard_map/ppermute | solution.py:672
  55.0 20.7 %collective-permute-start.16 = (bf16[512,256]{1,0:T(8,128)(2,1)S(1)}, bf16[512,256]{1,0:T(8,128)(2,1)S(1)}, u32[]{:S(2)}, u32[]{:S(2)}) collective-permute-start(bf16[512,256]{1,0:T(8,128)(2,1)S(1)} %collective-permute-done.13.refs_5_), channel_id=1, source_target_pairs={{0,4},{4,8},{8,12},{12,0},{1,5},{5,9},{9,13},{13,1},{2,6},{6,10},{... | collective-permute-start | bytes 786440 | tf_op jit(solution)/shard_map/ppermute | solution.py:672
  61.4 16.1 %collective-permute-start.15 = (bf16[512,256]{1,0:T(8,128)(2,1)S(1)}, bf16[512,256]{1,0:T(8,128)(2,1)S(1)}, u32[]{:S(2)}, u32[]{:S(2)}) collective-permute-start(bf16[512,256]{1,0:T(8,128)(2,1)S(1)} %collective-permute-done.12.refs_4_), channel_id=1, source_target_pairs={{0,4},{4,8},{8,12},{12,0},{1,5},{5,9},{9,13},{13,1},{2,6},{6,10},{... | collective-permute-start | bytes 786440 | tf_op jit(solution)/shard_map/ppermute | solution.py:672
  62.4 13.3 %collective-permute-start.18 = (bf16[64,512]{1,0:T(8,128)(2,1)S(1)}, bf16[64,512]{1,0:T(8,128)(2,1)S(1)}, u32[]{:S(2)}, u32[]{:S(2)}) collective-permute-start(bf16[64,512]{1,0:T(8,128)(2,1)S(1)} %get-tuple-element.38.refs_3_), channel_id=1, source_target_pairs={{0,8},{4,12},{8,0},{12,4},{1,9},{5,13},{9,1},{13,5},{2,10},{6,14},... | collective-permute-start | bytes 196616 | tf_op jit(solution)/shard_map/ppermute | solution.py:681
  64.5 11.2 %collective-permute-start.17 = (bf16[64,512]{1,0:T(8,128)(2,1)S(1)}, bf16[64,512]{1,0:T(8,128)(2,1)S(1)}, u32[]{:S(2)}, u32[]{:S(2)}) collective-permute-start(bf16[64,512]{1,0:T(8,128)(2,1)S(1)} %collective-permute-done.14.refs_6_), channel_id=1, source_target_pairs={{0,4},{4,8},{8,12},{12,0},{1,5},{5,9},{9,13},{13,1},{2,6},{6,10},{... | collective-permute-start | bytes 196616 | tf_op jit(solution)/shard_map/ppermute | solution.py:672
  77.4 7.5 %collective-permute-start.21 = (bf16[512,256]{1,0:T(8,128)(2,1)S(1)}, bf16[512,256]{1,0:T(8,128)(2,1)S(1)}, u32[]{:S(2)}, u32[]{:S(2)}) collective-permute-start(bf16[512,256]{1,0:T(8,128)(2,1)S(1)} %attend_far.2.refs_11_.refs_1_.refs_2_), channel_id=1, source_target_pairs={{0,1},{1,0},{2,3},{3,2},{4,5},{5,4},{6,7},{7,6},{8,9},{9,8},{10,11... | collective-permute-start | bytes 786440 | tf_op jit(solution)/shard_map/ppermute | solution.py:669
  79.6 6.7 %collective-permute-start.20 = (bf16[512,256]{1,0:T(8,128)(2,1)S(1)}, bf16[512,256]{1,0:T(8,128)(2,1)S(1)}, u32[]{:S(2)}, u32[]{:S(2)}) collective-permute-start(bf16[512,256]{1,0:T(8,128)(2,1)S(1)} %attend_far.3.refs_4_.refs_1_), channel_id=1, source_target_pairs={{0,1},{1,0},{2,3},{3,2},{4,5},{5,4},{6,7},{7,6},{8,9},{9,8},{10,11... | collective-permute-start | bytes 786440 | tf_op jit(solution)/shard_map/ppermute | solution.py:669
  80.1 15.3 %collective-permute-start.26 = (bf16[512,256]{1,0:T(8,128)(2,1)S(1)}, bf16[512,256]{1,0:T(8,128)(2,1)S(1)}, u32[]{:S(2)}, u32[]{:S(2)}) collective-permute-start(bf16[512,256]{1,0:T(8,128)(2,1)S(1)} %attend_far.2.refs_11_.refs_1_.refs_2_), channel_id=1, source_target_pairs={{0,2},{2,0},{1,3},{3,1},{4,6},{6,4},{5,7},{7,5},{8,10},{10,8},{9,1... | collective-permute-start | bytes 786440 | tf_op jit(solution)/shard_map/ppermute | solution.py:666
  81.6 13.9 %collective-permute-start.19 = (bf16[512,256]{1,0:T(8,128)(2,1)S(1)}, bf16[512,256]{1,0:T(8,128)(2,1)S(1)}, u32[]{:S(2)}, u32[]{:S(2)}) collective-permute-start(bf16[512,256]{1,0:T(8,128)(2,1)S(1)} %attend_far.3.refs_4_.refs_1_), channel_id=1, source_target_pairs={{0,2},{2,0},{1,3},{3,1},{4,6},{6,4},{5,7},{7,5},{8,10},{10,8},{9,1... | collective-permute-start | bytes 786440 | tf_op jit(solution)/shard_map/ppermute | solution.py:666
  82.2 13.3 %collective-permute-start.24 = (bf16[64,1344]{1,0:T(8,128)(2,1)S(1)}, bf16[64,1344]{1,0:T(8,128)(2,1)S(1)}, u32[]{:S(2)}, u32[]{:S(2)}) collective-permute-start(bf16[64,1344]{1,0:T(8,128)(2,1)S(1)} %get-tuple-element.58.refs_6_), channel_id=1, source_target_pairs={{0,8},{4,12},{8,0},{12,4},{1,9},{5,13},{9,1},{13,5},{2,10},{6,14},... | collective-permute-start | bytes 516104 | tf_op jit(solution)/shard_map/ppermute | solution.py:681
  88.5 1.3 %collective-permute-start.22 = (f32[32,512]{1,0:T(8,128)S(1)}, f32[32,512]{1,0:T(8,128)S(1)}, u32[]{:S(2)}, u32[]{:S(2)}) collective-permute-start(f32[32,512]{1,0:T(8,128)S(1)} %out_low.1), channel_id=1, source_target_pairs={{0,1},{1,0},{2,3},{3,2},{4,5},{5,4},{6,7},{7,6},{8,9},{9,8},{10,11... | collective-permute-start | bytes 196616 | tf_op jit(solution)/shard_map/ppermute | solution.py:669
  89.8 5.6 %collective-permute-start.23 = (f32[32,512]{1,0:T(8,128)S(1)}, f32[32,512]{1,0:T(8,128)S(1)}, u32[]{:S(2)}, u32[]{:S(2)}) collective-permute-start(f32[32,512]{1,0:T(8,128)S(1)} %add.27), channel_id=1, source_target_pairs={{0,2},{2,0},{1,3},{3,1},{4,6},{6,4},{5,7},{7,5},{8,10},{10,8},{9,1... | collective-permute-start | bytes 196616 | tf_op jit(solution)/shard_map/ppermute | solution.py:666
  95.5 1.6 %collective-permute-start.27 = (bf16[512,256]{1,0:T(8,128)(2,1)S(1)}, bf16[512,256]{1,0:T(8,128)(2,1)S(1)}, u32[]{:S(2)}, u32[]{:S(2)}) collective-permute-start(bf16[512,256]{1,0:T(8,128)(2,1)S(1)} %collective-permute-done.26.refs_1_), channel_id=1, source_target_pairs={{0,1},{1,0},{2,3},{3,2},{4,5},{5,4},{6,7},{7,6},{8,9},{9,8},{10,11... | collective-permute-start | bytes 786440 | tf_op jit(solution)/shard_map/ppermute | solution.py:669
  95.6 4.1 %collective-permute-start.25 = (bf16[512,256]{1,0:T(8,128)(2,1)S(1)}, bf16[512,256]{1,0:T(8,128)(2,1)S(1)}, u32[]{:S(2)}, u32[]{:S(2)}) collective-permute-start(bf16[512,256]{1,0:T(8,128)(2,1)S(1)} %collective-permute-done.19.refs_1_), channel_id=1, source_target_pairs={{0,1},{1,0},{2,3},{3,2},{4,5},{5,4},{6,7},{7,6},{8,9},{9,8},{10,11... | collective-permute-start | bytes 786440 | tf_op jit(solution)/shard_map/ppermute | solution.py:669
  (4 other events, 18.4 us)

commit v5 on v4

--- a/solution.py
+++ b/solution.py
@@ -805,8 +805,8 @@
             after=order,
         )
 
-    att_late = attend_far(1, [prev2_late], [down_rest])
-    att_early = attend_far(0, [prev2_early, prev2_late], [att_late])
+    att_late = attend_far(1, [prev2_late], [])
+    att_early = attend_far(0, [prev2_early, prev2_late], [att_late, down_rest])
 
     up_rest = swapped(up_pair, 2)
     crossed = [(chunk, across(att)) for chunk, att in ((1, att_late), (0, att_early))]

time: 103 us -> 101 us (0.981)
  waiting for transfers between devices: 23.7 us -> 21 us
    ppermute x3, waiting for transfers between devices: 6.35 us -> 0.24 us  [swapped(): return lax.ppermute(value, 'seq', [(j, j ^ by) for j in range(4)])]
    ppermute x6, waiting for transfers between devices: 0.02 us -> 4.34 us  [up(): return lax.ppermute(value, 'seq', [(i, (i + by) % 4) for i in range(4)])]
  transfers between devices with their start and end apart: 28 -> 28, of which waited for: 8 -> 9; matrix products, arithmetic and copies ran while one was open for 2% -> 2% of each run, Pallas kernels for 35% -> 36%
where the time goes in v5:
time: 101 us; the launch traced here: 100 us
  Pallas kernels  39.8 us (39%)
  starting transfers between devices  35.1 us (35%)
  waiting for transfers between devices  21 us (21%)
  other arithmetic  2.16 us (2%)
  local copies, waits for them, and re-layouts  1.44 us (1%)
    pallas_call x17, Pallas kernels, call(): pl.pallas_call(body, out_shape=out_shape, in_specs=list(in_specs) + [HB]...  39.8 us
    ppermute x5, waiting for transfers between devices, across(): return lax.ppermute(value, 'head', SWAP)  11.3 us
    ppermute x6, starting transfers between devices, up(): return lax.ppermute(value, 'seq', [(i, (i + by) % 4) for i in range(4)])  10.9 us
    ppermute x5, starting transfers between devices, across(): return lax.ppermute(value, 'head', SWAP)  6.91 us
    ppermute x3, starting transfers between devices, swapped(): return lax.ppermute(value, 'seq', [(j, j ^ by) for j in range(4)])  6.39 us
    ppermute x8, waiting for transfers between devices, core(): return lax.ppermute(value, 'rep', SWAP)  4.72 us
    ppermute x3, starting transfers between devices, exchange_quarters(): lax.ppermute(quarters[s], 'seq', [(j, j ^ s) for j in range(4)])  4.45 us
    ppermute x6, waiting for transfers between devices, up(): return lax.ppermute(value, 'seq', [(i, (i + by) % 4) for i in range(4)])  4.34 us
  transfers between devices with their start and end apart: 28, of which 9 were waited for; matrix products, arithmetic and copies ran while one was open for 2% of the time, Pallas kernels for 36%

profile of v5, /device:TPU:0, one launch (start us, length us, event | category | flops | bytes accessed | tf_op | source)
XLA Modules:
  0.0 100.4 jit_solution(11990804508175354866)
XLA Ops:
  0.5 2.5 %collective-permute-start.1 = (bf16[1344,512]{1,0:T(8,128)(2,1)}, bf16[1344,512]{1,0:T(8,128)(2,1)S(1)}, u32[]{:S(2)}, u32[]{:S(2)}) collective-permute-start(bf16[1344,512]{1,0:T(8,128)(2,1)} %bitcast.11), channel_id=1, source_target_pairs={{0,2},{2,0},{1,3},{3,1},{4,6},{6,4},{5,7},{7,5},{8,10},{10,8},{9,1... | collective-permute-start | bytes 4128776 | tf_op jit(solution)/shard_map/ppermute | solution.py:666
  3.7 2.5 %pack.1 = (bf16[64,1344]{1,0:T(8,128)(2,1)S(1)}, bf16[64,1344]{1,0:T(8,128)(2,1)}, bf16[64,1344]{1,0:T(8,128)(2,1)}, bf16[64,1344]{1,0:T(8,128)(2,1)}) custom-call(s32[2]{0:T(128)S(1)} %copy-done.4, bf16[2,96,1344]{2,1,0:T(8,128)(2,1)} %bitcast.20, bf16[2,32,512]{2,1,0:T(8,128)(2,1)} %refs_2_.2, bf16[2,2,32,512]{3,2,1,0:T(8,128)(2,1)} %refs_3_.2), custom_call_target="tpu_custom_call" | custom-call | flops 1000 | bytes 1000 | tf_op jit(solution)/shard_map/pack/pallas_call | solution.py:312
  6.2 1.6 %collective-permute-start.2 = (bf16[64,1344]{1,0:T(8,128)(2,1)}, bf16[64,1344]{1,0:T(8,128)(2,1)}, u32[]{:S(2)}, u32[]{:S(2)}) collective-permute-start(bf16[64,1344]{1,0:T(8,128)(2,1)} %get-tuple-element.35), channel_id=1, source_target_pairs={{0,4},{4,0},{8,12},{12,8},{1,5},{5,1},{9,13},{13,9},{2,6},{6,2},{1... | collective-permute-start | bytes 516104 | tf_op jit(solution)/shard_map/ppermute | solution.py:634
  7.8 2.6 %collective-permute-start.3 = (bf16[64,1344]{1,0:T(8,128)(2,1)}, bf16[64,1344]{1,0:T(8,128)(2,1)}, u32[]{:S(2)}, u32[]{:S(2)}) collective-permute-start(bf16[64,1344]{1,0:T(8,128)(2,1)} %get-tuple-element.36), channel_id=1, source_target_pairs={{0,8},{4,12},{8,0},{12,4},{1,9},{5,13},{9,1},{13,5},{2,10},{6,14},... | collective-permute-start | bytes 516104 | tf_op jit(solution)/shard_map/ppermute | solution.py:634
  10.6 2.3 %pack_out.1.refs_6_.refs_0_ = bf16[64,1920]{1,0:T(8,128)(2,1)} custom-call(s32[2]{0:T(128)S(1)} %copy-done.4, bf16[2,32,512]{2,1,0:T(8,128)(2,1)} %bitcast.21, bf16[2,32,1344]{2,1,0:T(8,128)(2,1)} %refs_2_.3, bf16[64,1344]{1,0:T(8,128)(2,1)S(1)} %get-tuple-element.33.refs_3_.refs_0_), custom_call_target="tpu_custom_call" | custom-call | flops 1000 | bytes 1000 | tf_op jit(solution)/shard_map/pack_out/pallas_call | solution.py:312
  15.5 1.4 %multiply_sine_fusion = (f32[64,1536]{1,0:T(8,128)S(1)}, f32[64,1536]{1,0:T(8,128)S(1)}) fusion(f32[1536]{0:T(1024)S(1)} %fusion, f32[64]{0:T(128)S(1)} %multiply_power_fusion), kind=kLoop, calls=%fused_computation | loop fusion | flops 98304 | bytes 792832 | tf_op jit(solution)/shard_map/sin | solution.py:741
  17.1 6.7 %near.1 = (f32[256,1024]{1,0:T(8,128)S(1)}, f32[256,1024]{1,0:T(8,128)S(1)}, bf16[2,1344,256]{2,1,0:T(8,128)(2,1)S(1)}, bf16[2,1344,256]{2,1,0:T(8,128)(2,1)S(1)}, bf16[2,1344,512]{2,1,0:T(8,128)(2,1)S(1)}) custom-call(s32[21]{0:T(128)S(1)} %concatenate.3.refs_0_, bf16[1344,512]{1,0:T(8,128)(2,1)S(1)} %bitcast.12, ...), custom_call_target="tpu_custom_call" | custom-call | flops 1000 | bytes 1000 | tf_op jit(solution)/shard_map/near/pallas_call | solution.py:312
  25.4 3.4 %collective-permute-start.5 = (bf16[64,1344]{1,0:T(8,128)(2,1)S(1)}, bf16[64,1344]{1,0:T(8,128)(2,1)S(1)}, u32[]{:S(2)}, u32[]{:S(2)}) collective-permute-start(bf16[64,1344]{1,0:T(8,128)(2,1)S(1)} %sum.1.refs_2_), channel_id=1, source_target_pairs={{0,4},{4,0},{8,12},{12,8},{1,5},{5,1},{9,13},{13,9},{2,6},{6,2},{1... | collective-permute-start | bytes 516104 | tf_op jit(solution)/shard_map/ppermute | solution.py:638
  30.6 3.4 %collective-permute-done.1.refs_1_ = bf16[1344,512]{1,0:T(8,128)(2,1)S(1)} collective-permute-done((bf16[1344,512]{1,0:T(8,128)(2,1)}, bf16[1344,512]{1,0:T(8,128)(2,1)S(1)}, u32[]{:S(2)}, u32[]{:S(2)}) %collective-permute-start.1) | collective-permute-done | bytes 1376288 | tf_op jit(solution)/shard_map/ppermute | solution.py:666
  34.7 2.4 %collective-permute-done.8.refs_2_ = bf16[1344,512]{1,0:T(8,128)(2,1)S(1)} collective-permute-done((bf16[1344,512]{1,0:T(8,128)(2,1)S(1)}, bf16[1344,512]{1,0:T(8,128)(2,1)S(1)}, u32[]{:S(2)}, u32[]{:S(2)}) %collective-permute-start.8) | collective-permute-done | bytes 1376288 | tf_op jit(solution)/shard_map/ppermute | solution.py:669
  37.1 2.0 %far.2 = (f32[512,256]{1,0:T(8,128)S(1)}, bf16[512,256]{1,0:T(8,128)(2,1)S(1)}) custom-call(f32[256,1024]{1,0:T(8,128)S(1)} %get-tuple-element.43.refs_0_, bf16[1344,512]{1,0:T(8,128)(2,1)S(1)} %collective-permute-done.1.refs_1_, bf16[1344,512]{1,0:T(8,128)(2,1)S(1)} %collective-permute-done.8.refs_2_, bf16[2,1344,256]{2,1,0:T(8,128)(2,1)S(1)} %get-tuple-element.40.refs_3_, ...), custom_call_target="tpu_custom_call" | custom-call | flops 1000 | bytes 1000 | tf_op jit(solution)/shard_map/far/pallas_call | solution.py:312
  39.2 2.0 %far.3 = (f32[512,256]{1,0:T(8,128)S(1)}, bf16[512,256]{1,0:T(8,128)(2,1)S(1)}) custom-call(f32[256,1024]{1,0:T(8,128)S(1)} %get-tuple-element.34.refs_4_.refs_0_, bf16[1344,512]{1,0:T(8,128)(2,1)S(1)} %collective-permute-done.1.refs_1_, bf16[1344,512]{1,0:T(8,128)(2,1)S(1)} %collective-permute-done.8.refs_2_, ...), custom_call_target="tpu_custom_call" | custom-call | flops 1000 | bytes 1000 | tf_op jit(solution)/shard_map/far/pallas_call | solution.py:312
  42.5 3.8 %collective-permute-start.13 = (bf16[512,256]{1,0:T(8,128)(2,1)S(1)}, bf16[512,256]{1,0:T(8,128)(2,1)S(1)}, u32[]{:S(2)}, u32[]{:S(2)}) collective-permute-start(bf16[512,256]{1,0:T(8,128)(2,1)S(1)} %get-tuple-element.44.refs_6_.refs_4_), channel_id=1, source_target_pairs={{0,4},{4,8},{8,12},{12,0},{1,5},{5,9},{9,13},{13,1},{2,6},{6,10},{... | collective-permute-start | bytes 786440 | tf_op jit(solution)/shard_map/ppermute | solution.py:672
  47.5 1.6 %collective-permute-start.12 = (bf16[512,256]{1,0:T(8,128)(2,1)S(1)}, bf16[512,256]{1,0:T(8,128)(2,1)S(1)}, u32[]{:S(2)}, u32[]{:S(2)}) collective-permute-start(bf16[512,256]{1,0:T(8,128)(2,1)S(1)} %get-tuple-element.47.refs_6_.refs_3_), channel_id=1, source_target_pairs={{0,4},{4,8},{8,12},{12,0},{1,5},{5,9},{9,13},{13,1},{2,6},{6,10},{... | collective-permute-start | bytes 786440 | tf_op jit(solution)/shard_map/ppermute | solution.py:672
  49.1 4.3 %collective-permute-done.11 = f32[96,512]{1,0:T(8,128)S(1)} collective-permute-done((f32[96,512]{1,0:T(8,128)S(1)}, f32[96,512]{1,0:T(8,128)S(1)}, u32[]{:S(2)}, u32[]{:S(2)}) %collective-permute-start.11) | collective-permute-done | bytes 196640 | tf_op jit(solution)/shard_map/ppermute | solution.py:666
  53.4 1.6 %collective-permute-start.14 = (bf16[64,512]{1,0:T(8,128)(2,1)S(1)}, bf16[64,512]{1,0:T(8,128)(2,1)S(1)}, u32[]{:S(2)}, u32[]{:S(2)}) collective-permute-start(bf16[64,512]{1,0:T(8,128)(2,1)S(1)} %slice.7), channel_id=1, source_target_pairs={{0,4},{4,8},{8,12},{12,0},{1,5},{5,9},{9,13},{13,1},{2,6},{6,10},{... | collective-permute-start | bytes 196616 | tf_op jit(solution)/shard_map/ppermute | solution.py:672
  55.0 1.3 %collective-permute-start.16 = (bf16[512,256]{1,0:T(8,128)(2,1)S(1)}, bf16[512,256]{1,0:T(8,128)(2,1)S(1)}, u32[]{:S(2)}, u32[]{:S(2)}) collective-permute-start(bf16[512,256]{1,0:T(8,128)(2,1)S(1)} %collective-permute-done.13.refs_5_), channel_id=1, source_target_pairs={{0,4},{4,8},{8,12},{12,0},{1,5},{5,9},{9,13},{13,1},{2,6},{6,10},{... | collective-permute-start | bytes 786440 | tf_op jit(solution)/shard_map/ppermute | solution.py:672
  56.4 5.0 %attend_own.1 = (bf16[512,512]{1,0:T(8,128)(2,1)S(1)}, f32[512,512]{1,0:T(8,128)S(1)}, f32[8,512]{1,0:T(8,128)S(1)}, bf16[1344,2048]{1,0:T(8,128)(2,1)S(1)}) custom-call(s32[21]{0:T(128)S(1)} %concatenate.3.refs_0_, f32[512,256]{1,0:T(8,128)S(1)} %get-tuple-element.45.refs_1_, f32[512,256]{1,0:T(8,128)S(1)} %get-tuple-element.46.refs_2_, ...), custom_call_target="tpu_custom_call" | custom-call | flops 1000 | bytes 1000 | tf_op jit(solution)/shard_map/attend_own/pallas_call | solution.py:312
  62.4 1.6 %collective-permute-start.17 = (bf16[64,512]{1,0:T(8,128)(2,1)S(1)}, bf16[64,512]{1,0:T(8,128)(2,1)S(1)}, u32[]{:S(2)}, u32[]{:S(2)}) collective-permute-start(bf16[64,512]{1,0:T(8,128)(2,1)S(1)} %collective-permute-done.14.refs_6_), channel_id=1, source_target_pairs={{0,4},{4,8},{8,12},{12,0},{1,5},{5,9},{9,13},{13,1},{2,6},{6,10},{... | collective-permute-start | bytes 196616 | tf_op jit(solution)/shard_map/ppermute | solution.py:672
  64.0 1.9 %collective-permute-start.18 = (bf16[64,512]{1,0:T(8,128)(2,1)S(1)}, bf16[64,512]{1,0:T(8,128)(2,1)S(1)}, u32[]{:S(2)}, u32[]{:S(2)}) collective-permute-start(bf16[64,512]{1,0:T(8,128)(2,1)S(1)} %get-tuple-element.38.refs_3_), channel_id=1, source_target_pairs={{0,8},{4,12},{8,0},{12,4},{1,9},{5,13},{9,1},{13,5},{2,10},{6,14},... | collective-permute-start | bytes 196616 | tf_op jit(solution)/shard_map/ppermute | solution.py:681
  65.9 3.5 %attend_prev.1 = (f32[512,512]{1,0:T(8,128)S(1)}, f32[8,512]{1,0:T(8,128)S(1)}) custom-call(s32[21]{0:T(128)S(1)} %concatenate.3.refs_0_, bf16[512,512]{1,0:T(8,128)(2,1)S(1)} %get-tuple-element.50.refs_1_, f32[512,512]{1,0:T(8,128)S(1)} %get-tuple-element.51.refs_2_, f32[8,512]{1,0:T(8,128)S(1)} %get-tuple-element.52.refs_3_, ...), custom_call_target="tpu_custom_call" | custom-call | flops 1000 | bytes 1000 | tf_op jit(solution)/shard_map/attend_prev/pallas_call | solution.py:312
  69.4 4.3 %collective-permute-done.17.refs_5_.refs_6_ = bf16[64,512]{1,0:T(8,128)(2,1)S(1)} collective-permute-done((bf16[64,512]{1,0:T(8,128)(2,1)S(1)}, bf16[64,512]{1,0:T(8,128)(2,1)S(1)}, u32[]{:S(2)}, u32[]{:S(2)}) %collective-permute-start.17) | collective-permute-done | bytes 65568 | tf_op jit(solution)/shard_map/ppermute | solution.py:672
  73.7 1.7 %attend_far.2.refs_11_.refs_1_.refs_2_ = bf16[512,256]{1,0:T(8,128)(2,1)S(1)} custom-call(s32[21]{0:T(128)S(1)} %concatenate.3.refs_0_, bf16[512,512]{1,0:T(8,128)(2,1)S(1)} %get-tuple-element.50.refs_1_, f32[512,512]{1,0:T(8,128)S(1)} %get-tuple-element.53.refs_2_, f32[8,512]{1,0:T(8,128)S(1)} %get-tuple-element.54.refs_3_, ...), custom_call_target="tpu_custom_call" | custom-call | flops 1000 | bytes 1000 | tf_op jit(solution)/shard_map/attend_far/pallas_call | solution.py:312
  75.7 2.1 %attend_far.3.refs_4_.refs_1_ = bf16[512,256]{1,0:T(8,128)(2,1)S(1)} custom-call(s32[21]{0:T(128)S(1)} %concatenate.3.refs_0_, bf16[512,512]{1,0:T(8,128)(2,1)S(1)} %get-tuple-element.50.refs_1_, f32[512,512]{1,0:T(8,128)S(1)} %get-tuple-element.53.refs_2_, f32[8,512]{1,0:T(8,128)S(1)} %get-tuple-element.54.refs_3_, ...), custom_call_target="tpu_custom_call" | custom-call | flops 1000 | bytes 1000 | tf_op jit(solution)/shard_map/attend_far/pallas_call | solution.py:312
  78.1 1.4 %collective-permute-start.26 = (bf16[512,256]{1,0:T(8,128)(2,1)S(1)}, bf16[512,256]{1,0:T(8,128)(2,1)S(1)}, u32[]{:S(2)}, u32[]{:S(2)}) collective-permute-start(bf16[512,256]{1,0:T(8,128)(2,1)S(1)} %attend_far.2.refs_11_.refs_1_.refs_2_), channel_id=1, source_target_pairs={{0,2},{2,0},{1,3},{3,1},{4,6},{6,4},{5,7},{7,5},{8,10},{10,8},{9,1... | collective-permute-start | bytes 786440 | tf_op jit(solution)/shard_map/ppermute | solution.py:666
  80.1 3.8 %collective-permute-start.24 = (bf16[64,1344]{1,0:T(8,128)(2,1)S(1)}, bf16[64,1344]{1,0:T(8,128)(2,1)S(1)}, u32[]{:S(2)}, u32[]{:S(2)}) collective-permute-start(bf16[64,1344]{1,0:T(8,128)(2,1)S(1)} %get-tuple-element.58.refs_6_), channel_id=1, source_target_pairs={{0,8},{4,12},{8,0},{12,4},{1,9},{5,13},{9,1},{13,5},{2,10},{6,14},... | collective-permute-start | bytes 516104 | tf_op jit(solution)/shard_map/ppermute | solution.py:681
  83.9 1.4 %out_near.2.refs_5_.refs_4_ = f32[1344,256]{1,0:T(8,128)S(1)} custom-call(s32[21]{0:T(128)S(1)} %concatenate.3.refs_0_, bf16[512,256]{1,0:T(8,128)(2,1)S(1)} %attend_far.2.refs_11_.refs_1_.refs_2_, bf16[512,256]{1,0:T(8,128)(2,1)S(1)} %collective-permute-done.21.refs_2_, bf16[1344,2048]{1,0:T(8,128)(2,1)S(1)} %get-tuple-element.57.refs_3_, ...), custom_call_target="tpu_custom_call" | custom-call | flops 1000 | bytes 1000 | tf_op jit(solution)/shard_map/out_near/pallas_call | solution.py:312
  85.4 1.4 %out_near.3.refs_5_.refs_4_ = f32[1344,256]{1,0:T(8,128)S(1)} custom-call(s32[21]{0:T(128)S(1)} %concatenate.3.refs_0_, bf16[512,256]{1,0:T(8,128)(2,1)S(1)} %attend_far.3.refs_4_.refs_1_, bf16[512,256]{1,0:T(8,128)(2,1)S(1)} %collective-permute-done.20.refs_2_, bf16[1344,2048]{1,0:T(8,128)(2,1)S(1)} %get-tuple-element.57.refs_3_, ...), custom_call_target="tpu_custom_call" | custom-call | flops 1000 | bytes 1000 | tf_op jit(solution)/shard_map/out_near/pallas_call | solution.py:312
  87.6 1.2 %collective-permute-done.22 = f32[32,512]{1,0:T(8,128)S(1)} collective-permute-done((f32[32,512]{1,0:T(8,128)S(1)}, f32[32,512]{1,0:T(8,128)S(1)}, u32[]{:S(2)}, u32[]{:S(2)}) %collective-permute-start.22) | collective-permute-done | bytes 65568 | tf_op jit(solution)/shard_map/ppermute | solution.py:669
  90.0 3.6 %collective-permute-done.23 = f32[32,512]{1,0:T(8,128)S(1)} collective-permute-done((f32[32,512]{1,0:T(8,128)S(1)}, f32[32,512]{1,0:T(8,128)S(1)}, u32[]{:S(2)}, u32[]{:S(2)}) %collective-permute-start.23) | collective-permute-done | bytes 65568 | tf_op jit(solution)/shard_map/ppermute | solution.py:666
  95.2 2.6 %out_far.2.refs_8_ = bf16[1344,512]{1,0:T(8,128)(2,1)} custom-call(s32[21]{0:T(128)S(1)} %concatenate.3.refs_0_, bf16[512,256]{1,0:T(8,128)(2,1)S(1)} %collective-permute-done.26.refs_1_, bf16[512,256]{1,0:T(8,128)(2,1)S(1)} %collective-permute-done.27.refs_2_, bf16[1344,2048]{1,0:T(8,128)(2,1)S(1)} %get-tuple-element.57.refs_3_, ...), custom_call_target="tpu_custom_call" | custom-call | flops 1000 | bytes 1000 | tf_op jit(solution)/shard_map/out_far/pallas_call | solution.py:312
  97.8 2.6 %out_far.3 = bf16[1344,512]{1,0:T(8,128)(2,1)} custom-call(s32[21]{0:T(128)S(1)} %concatenate.3.refs_0_, bf16[512,256]{1,0:T(8,128)(2,1)S(1)} %collective-permute-done.19.refs_1_, bf16[512,256]{1,0:T(8,128)(2,1)S(1)} %collective-permute-done.25.refs_2_, bf16[1344,2048]{1,0:T(8,128)(2,1)S(1)} %get-tuple-element.57.refs_3_, ...), custom_call_target="tpu_custom_call", output_to_operand_aliasing={{}: (8, {})} | custom-call | flops 1000 | bytes 1000 | tf_op jit(solution)/shard_map/out_far/pallas_call | solution.py:312
  (67 shorter events, 15.8 us)
Async XLA Ops:
  0.0 17.1 %copy-start = (bf16[512,1344]{0,1:T(8,128)(2,1)S(1)}, bf16[512,1344]{0,1:T(8,128)(2,1)}, u32[]{:S(2)}) copy-start(bf16[512,1344]{0,1:T(8,128)(2,1)} %param.14) | copy-start | bytes 4128772
  0.0 14.8 %collective-permute-start = (bf16[1344,512]{1,0:T(8,128)(2,1)}, bf16[1344,512]{1,0:T(8,128)(2,1)}, u32[]{:S(2)}, u32[]{:S(2)}) collective-permute-start(bf16[1344,512]{1,0:T(8,128)(2,1)} %bitcast.10), channel_id=1, source_target_pairs={{0,1},{1,0},{2,3},{3,2},{4,5},{5,4},{6,7},{7,6},{8,9},{9,8},{10,11... | collective-permute-start | bytes 4128776 | tf_op jit(solution)/shard_map/ppermute | solution.py:669
  0.5 33.5 %collective-permute-start.1 = (bf16[1344,512]{1,0:T(8,128)(2,1)}, bf16[1344,512]{1,0:T(8,128)(2,1)S(1)}, u32[]{:S(2)}, u32[]{:S(2)}) collective-permute-start(bf16[1344,512]{1,0:T(8,128)(2,1)} %bitcast.11), channel_id=1, source_target_pairs={{0,2},{2,0},{1,3},{3,1},{4,6},{6,4},{5,7},{7,5},{8,10},{10,8},{9,1... | collective-permute-start | bytes 4128776 | tf_op jit(solution)/shard_map/ppermute | solution.py:666
  3.7 13.3 %copy-start.5 = (s32[2]{0:T(128)S(1)}, s32[2]{0:T(128)}, u32[]{:S(2)}) copy-start(s32[2]{0:T(128)} %refs_0_.3) | copy-start | bytes 28
  6.2 17.6 %collective-permute-start.2 = (bf16[64,1344]{1,0:T(8,128)(2,1)}, bf16[64,1344]{1,0:T(8,128)(2,1)}, u32[]{:S(2)}, u32[]{:S(2)}) collective-permute-start(bf16[64,1344]{1,0:T(8,128)(2,1)} %get-tuple-element.35), channel_id=1, source_target_pairs={{0,4},{4,0},{8,12},{12,8},{1,5},{5,1},{9,13},{13,9},{2,6},{6,2},{1... | collective-permute-start | bytes 516104 | tf_op jit(solution)/shard_map/ppermute | solution.py:634
  7.8 16.4 %collective-permute-start.3 = (bf16[64,1344]{1,0:T(8,128)(2,1)}, bf16[64,1344]{1,0:T(8,128)(2,1)}, u32[]{:S(2)}, u32[]{:S(2)}) collective-permute-start(bf16[64,1344]{1,0:T(8,128)(2,1)} %get-tuple-element.36), channel_id=1, source_target_pairs={{0,8},{4,12},{8,0},{12,4},{1,9},{5,13},{9,1},{13,5},{2,10},{6,14},... | collective-permute-start | bytes 516104 | tf_op jit(solution)/shard_map/ppermute | solution.py:634
  10.4 13.8 %collective-permute-start.4 = (bf16[64,1344]{1,0:T(8,128)(2,1)}, bf16[64,1344]{1,0:T(8,128)(2,1)}, u32[]{:S(2)}, u32[]{:S(2)}) collective-permute-start(bf16[64,1344]{1,0:T(8,128)(2,1)} %get-tuple-element.37), channel_id=1, source_target_pairs={{0,12},{4,8},{8,4},{12,0},{1,13},{5,9},{9,5},{13,1},{2,14},{6,10},... | collective-permute-start | bytes 516104 | tf_op jit(solution)/shard_map/ppermute | solution.py:634
  14.8 14.7 %collective-permute-start.7 = (bf16[64,1920]{1,0:T(8,128)(2,1)}, bf16[64,1920]{1,0:T(8,128)(2,1)}, u32[]{:S(2)}, u32[]{:S(2)}) collective-permute-start(bf16[64,1920]{1,0:T(8,128)(2,1)} %pack_out.1.refs_6_.refs_0_), channel_id=1, source_target_pairs={{0,4},{4,0},{8,12},{12,8},{1,5},{5,1},{9,13},{13,9},{2,6},{6,2},{1... | collective-permute-start | bytes 737288 | tf_op jit(solution)/shard_map/ppermute | solution.py:681
  25.4 8.6 %collective-permute-start.5 = (bf16[64,1344]{1,0:T(8,128)(2,1)S(1)}, bf16[64,1344]{1,0:T(8,128)(2,1)S(1)}, u32[]{:S(2)}, u32[]{:S(2)}) collective-permute-start(bf16[64,1344]{1,0:T(8,128)(2,1)S(1)} %sum.1.refs_2_), channel_id=1, source_target_pairs={{0,4},{4,0},{8,12},{12,8},{1,5},{5,1},{9,13},{13,9},{2,6},{6,2},{1... | collective-permute-start | bytes 516104 | tf_op jit(solution)/shard_map/ppermute | solution.py:638
  28.8 5.2 %collective-permute-start.6 = (bf16[64,1344]{1,0:T(8,128)(2,1)S(1)}, bf16[64,1344]{1,0:T(8,128)(2,1)S(1)}, u32[]{:S(2)}, u32[]{:S(2)}) collective-permute-start(bf16[64,1344]{1,0:T(8,128)(2,1)S(1)} %sum.1.refs_2_), channel_id=1, source_target_pairs={{4,8},{8,4},{5,9},{9,5},{6,10},{10,6},{7,11},{11,7},{20,24},{24,20... | collective-permute-start | bytes 516104 | tf_op jit(solution)/shard_map/ppermute | solution.py:640
  34.0 3.1 %collective-permute-start.8 = (bf16[1344,512]{1,0:T(8,128)(2,1)S(1)}, bf16[1344,512]{1,0:T(8,128)(2,1)S(1)}, u32[]{:S(2)}, u32[]{:S(2)}) collective-permute-start(bf16[1344,512]{1,0:T(8,128)(2,1)S(1)} %collective-permute-done.1.refs_1_), channel_id=1, source_target_pairs={{0,1},{1,0},{2,3},{3,2},{4,5},{5,4},{6,7},{7,6},{8,9},{9,8},{10,11... | collective-permute-start | bytes 4128776 | tf_op jit(solution)/shard_map/ppermute | solution.py:669
  34.0 7.2 %collective-permute-start.9 = (bf16[64,1344]{1,0:T(8,128)(2,1)S(1)}, bf16[64,1344]{1,0:T(8,128)(2,1)S(1)}, u32[]{:S(2)}, u32[]{:S(2)}) collective-permute-start(bf16[64,1344]{1,0:T(8,128)(2,1)S(1)} %collective-permute-done.5.refs_6_.refs_3_), channel_id=1, source_target_pairs={{4,8},{8,4},{5,9},{9,5},{6,10},{10,6},{7,11},{11,7},{20,24},{24,20... | collective-permute-start | bytes 516104 | tf_op jit(solution)/shard_map/ppermute | solution.py:640
  41.2 15.1 %copy-start.3 = (f32[128]{0:T(128)S(1)}, f32[128]{0:T(128)}, u32[]{:S(2)}) copy-start(f32[128]{0:T(128)} %param.20) | copy-start | bytes 1540
  41.2 15.1 %copy-start.6 = (f32[128]{0:T(128)S(1)}, f32[128]{0:T(128)}, u32[]{:S(2)}) copy-start(f32[128]{0:T(128)} %param.19) | copy-start | bytes 1540
  42.3 4.0 %collective-permute-start.10 = (f32[96,512]{1,0:T(8,128)S(1)}, f32[96,512]{1,0:T(8,128)S(1)}, u32[]{:S(2)}, u32[]{:S(2)}) collective-permute-start(f32[96,512]{1,0:T(8,128)S(1)} %get-tuple-element.48), channel_id=1, source_target_pairs={{0,1},{1,0},{2,3},{3,2},{4,5},{5,4},{6,7},{7,6},{8,9},{9,8},{10,11... | collective-permute-start | bytes 589832 | tf_op jit(solution)/shard_map/ppermute | solution.py:669
  42.5 12.5 %collective-permute-start.13 = (bf16[512,256]{1,0:T(8,128)(2,1)S(1)}, bf16[512,256]{1,0:T(8,128)(2,1)S(1)}, u32[]{:S(2)}, u32[]{:S(2)}) collective-permute-start(bf16[512,256]{1,0:T(8,128)(2,1)S(1)} %get-tuple-element.44.refs_6_.refs_4_), channel_id=1, source_target_pairs={{0,4},{4,8},{8,12},{12,0},{1,5},{5,9},{9,13},{13,1},{2,6},{6,10},{... | collective-permute-start | bytes 786440 | tf_op jit(solution)/shard_map/ppermute | solution.py:672
  46.3 7.0 %collective-permute-start.11 = (f32[96,512]{1,0:T(8,128)S(1)}, f32[96,512]{1,0:T(8,128)S(1)}, u32[]{:S(2)}, u32[]{:S(2)}) collective-permute-start(f32[96,512]{1,0:T(8,128)S(1)} %add.25), channel_id=1, source_target_pairs={{0,2},{2,0},{1,3},{3,1},{4,6},{6,4},{5,7},{7,5},{8,10},{10,8},{9,1... | collective-permute-start | bytes 589832 | tf_op jit(solution)/shard_map/ppermute | solution.py:666
  47.5 13.9 %collective-permute-start.12 = (bf16[512,256]{1,0:T(8,128)(2,1)S(1)}, bf16[512,256]{1,0:T(8,128)(2,1)S(1)}, u32[]{:S(2)}, u32[]{:S(2)}) collective-permute-start(bf16[512,256]{1,0:T(8,128)(2,1)S(1)} %get-tuple-element.47.refs_6_.refs_3_), channel_id=1, source_target_pairs={{0,4},{4,8},{8,12},{12,0},{1,5},{5,9},{9,13},{13,1},{2,6},{6,10},{... | collective-permute-start | bytes 786440 | tf_op jit(solution)/shard_map/ppermute | solution.py:672
  53.4 8.0 %collective-permute-start.14 = (bf16[64,512]{1,0:T(8,128)(2,1)S(1)}, bf16[64,512]{1,0:T(8,128)(2,1)S(1)}, u32[]{:S(2)}, u32[]{:S(2)}) collective-permute-start(bf16[64,512]{1,0:T(8,128)(2,1)S(1)} %slice.7), channel_id=1, source_target_pairs={{0,4},{4,8},{8,12},{12,0},{1,5},{5,9},{9,13},{13,1},{2,6},{6,10},{... | collective-permute-start | bytes 196616 | tf_op jit(solution)/shard_map/ppermute | solution.py:672
  55.0 14.3 %collective-permute-start.16 = (bf16[512,256]{1,0:T(8,128)(2,1)S(1)}, bf16[512,256]{1,0:T(8,128)(2,1)S(1)}, u32[]{:S(2)}, u32[]{:S(2)}) collective-permute-start(bf16[512,256]{1,0:T(8,128)(2,1)S(1)} %collective-permute-done.13.refs_5_), channel_id=1, source_target_pairs={{0,4},{4,8},{8,12},{12,0},{1,5},{5,9},{9,13},{13,1},{2,6},{6,10},{... | collective-permute-start | bytes 786440 | tf_op jit(solution)/shard_map/ppermute | solution.py:672
  61.4 14.3 %collective-permute-start.15 = (bf16[512,256]{1,0:T(8,128)(2,1)S(1)}, bf16[512,256]{1,0:T(8,128)(2,1)S(1)}, u32[]{:S(2)}, u32[]{:S(2)}) collective-permute-start(bf16[512,256]{1,0:T(8,128)(2,1)S(1)} %collective-permute-done.12.refs_4_), channel_id=1, source_target_pairs={{0,4},{4,8},{8,12},{12,0},{1,5},{5,9},{9,13},{13,1},{2,6},{6,10},{... | collective-permute-start | bytes 786440 | tf_op jit(solution)/shard_map/ppermute | solution.py:672
  62.4 11.3 %collective-permute-start.17 = (bf16[64,512]{1,0:T(8,128)(2,1)S(1)}, bf16[64,512]{1,0:T(8,128)(2,1)S(1)}, u32[]{:S(2)}, u32[]{:S(2)}) collective-permute-start(bf16[64,512]{1,0:T(8,128)(2,1)S(1)} %collective-permute-done.14.refs_6_), channel_id=1, source_target_pairs={{0,4},{4,8},{8,12},{12,0},{1,5},{5,9},{9,13},{13,1},{2,6},{6,10},{... | collective-permute-start | bytes 196616 | tf_op jit(solution)/shard_map/ppermute | solution.py:672
  64.0 11.7 %collective-permute-start.18 = (bf16[64,512]{1,0:T(8,128)(2,1)S(1)}, bf16[64,512]{1,0:T(8,128)(2,1)S(1)}, u32[]{:S(2)}, u32[]{:S(2)}) collective-permute-start(bf16[64,512]{1,0:T(8,128)(2,1)S(1)} %get-tuple-element.38.refs_3_), channel_id=1, source_target_pairs={{0,8},{4,12},{8,0},{12,4},{1,9},{5,13},{9,1},{13,5},{2,10},{6,14},... | collective-permute-start | bytes 196616 | tf_op jit(solution)/shard_map/ppermute | solution.py:681
  75.4 8.5 %collective-permute-start.21 = (bf16[512,256]{1,0:T(8,128)(2,1)S(1)}, bf16[512,256]{1,0:T(8,128)(2,1)S(1)}, u32[]{:S(2)}, u32[]{:S(2)}) collective-permute-start(bf16[512,256]{1,0:T(8,128)(2,1)S(1)} %attend_far.2.refs_11_.refs_1_.refs_2_), channel_id=1, source_target_pairs={{0,1},{1,0},{2,3},{3,2},{4,5},{5,4},{6,7},{7,6},{8,9},{9,8},{10,11... | collective-permute-start | bytes 786440 | tf_op jit(solution)/shard_map/ppermute | solution.py:669
  77.8 7.6 %collective-permute-start.20 = (bf16[512,256]{1,0:T(8,128)(2,1)S(1)}, bf16[512,256]{1,0:T(8,128)(2,1)S(1)}, u32[]{:S(2)}, u32[]{:S(2)}) collective-permute-start(bf16[512,256]{1,0:T(8,128)(2,1)S(1)} %attend_far.3.refs_4_.refs_1_), channel_id=1, source_target_pairs={{0,1},{1,0},{2,3},{3,2},{4,5},{5,4},{6,7},{7,6},{8,9},{9,8},{10,11... | collective-permute-start | bytes 786440 | tf_op jit(solution)/shard_map/ppermute | solution.py:669
  78.1 15.5 %collective-permute-start.26 = (bf16[512,256]{1,0:T(8,128)(2,1)S(1)}, bf16[512,256]{1,0:T(8,128)(2,1)S(1)}, u32[]{:S(2)}, u32[]{:S(2)}) collective-permute-start(bf16[512,256]{1,0:T(8,128)(2,1)S(1)} %attend_far.2.refs_11_.refs_1_.refs_2_), channel_id=1, source_target_pairs={{0,2},{2,0},{1,3},{3,1},{4,6},{6,4},{5,7},{7,5},{8,10},{10,8},{9,1... | collective-permute-start | bytes 786440 | tf_op jit(solution)/shard_map/ppermute | solution.py:666
  79.6 14.2 %collective-permute-start.19 = (bf16[512,256]{1,0:T(8,128)(2,1)S(1)}, bf16[512,256]{1,0:T(8,128)(2,1)S(1)}, u32[]{:S(2)}, u32[]{:S(2)}) collective-permute-start(bf16[512,256]{1,0:T(8,128)(2,1)S(1)} %attend_far.3.refs_4_.refs_1_), channel_id=1, source_target_pairs={{0,2},{2,0},{1,3},{3,1},{4,6},{6,4},{5,7},{7,5},{8,10},{10,8},{9,1... | collective-permute-start | bytes 786440 | tf_op jit(solution)/shard_map/ppermute | solution.py:666
  80.1 13.5 %collective-permute-start.24 = (bf16[64,1344]{1,0:T(8,128)(2,1)S(1)}, bf16[64,1344]{1,0:T(8,128)(2,1)S(1)}, u32[]{:S(2)}, u32[]{:S(2)}) collective-permute-start(bf16[64,1344]{1,0:T(8,128)(2,1)S(1)} %get-tuple-element.58.refs_6_), channel_id=1, source_target_pairs={{0,8},{4,12},{8,0},{12,4},{1,9},{5,13},{9,1},{13,5},{2,10},{6,14},... | collective-permute-start | bytes 516104 | tf_op jit(solution)/shard_map/ppermute | solution.py:681
  87.5 1.3 %collective-permute-start.22 = (f32[32,512]{1,0:T(8,128)S(1)}, f32[32,512]{1,0:T(8,128)S(1)}, u32[]{:S(2)}, u32[]{:S(2)}) collective-permute-start(f32[32,512]{1,0:T(8,128)S(1)} %out_low.1), channel_id=1, source_target_pairs={{0,1},{1,0},{2,3},{3,2},{4,5},{5,4},{6,7},{7,6},{8,9},{9,8},{10,11... | collective-permute-start | bytes 196616 | tf_op jit(solution)/shard_map/ppermute | solution.py:669
  88.9 4.7 %collective-permute-start.23 = (f32[32,512]{1,0:T(8,128)S(1)}, f32[32,512]{1,0:T(8,128)S(1)}, u32[]{:S(2)}, u32[]{:S(2)}) collective-permute-start(f32[32,512]{1,0:T(8,128)S(1)} %add.27), channel_id=1, source_target_pairs={{0,2},{2,0},{1,3},{3,1},{4,6},{6,4},{5,7},{7,5},{8,10},{10,8},{9,1... | collective-permute-start | bytes 196616 | tf_op jit(solution)/shard_map/ppermute | solution.py:666
  93.6 1.6 %collective-permute-start.27 = (bf16[512,256]{1,0:T(8,128)(2,1)S(1)}, bf16[512,256]{1,0:T(8,128)(2,1)S(1)}, u32[]{:S(2)}, u32[]{:S(2)}) collective-permute-start(bf16[512,256]{1,0:T(8,128)(2,1)S(1)} %collective-permute-done.26.refs_1_), channel_id=1, source_target_pairs={{0,1},{1,0},{2,3},{3,2},{4,5},{5,4},{6,7},{7,6},{8,9},{9,8},{10,11... | collective-permute-start | bytes 786440 | tf_op jit(solution)/shard_map/ppermute | solution.py:669
  93.7 4.1 %collective-permute-start.25 = (bf16[512,256]{1,0:T(8,128)(2,1)S(1)}, bf16[512,256]{1,0:T(8,128)(2,1)S(1)}, u32[]{:S(2)}, u32[]{:S(2)}) collective-permute-start(bf16[512,256]{1,0:T(8,128)(2,1)S(1)} %collective-permute-done.19.refs_1_), channel_id=1, source_target_pairs={{0,1},{1,0},{2,3},{3,2},{4,5},{5,4},{6,7},{7,6},{8,9},{9,8},{10,11... | collective-permute-start | bytes 786440 | tf_op jit(solution)/shard_map/ppermute | solution.py:669
  (4 other events, 18.4 us)

commit v6 on v5

--- a/solution.py
+++ b/solution.py
@@ -755,7 +755,6 @@
     down_rest = swapped(down_pair, 2)
     far_other = core(after(far_own, pieces[1], pieces[2], down_pair))
     late_q, late_kv = project(1, pieces[1])
-    early_q, early_kv = project(0, late_kv)
     partial_low, ups = call(
         low_kernel,
         "low",
@@ -763,9 +762,10 @@
         [SM] + [VM] * 5,
         [meta, tokens, *pieces],
         [pltpu.VMEM((4, 64, width), BF16)],
-        after=[early_kv],
+        after=[late_kv],
     )
     chip_low = partial_low + core(partial_low)
+    early_q, early_kv = project(0, chip_low)
     low = chip_low + across(chip_low)
 
     prev_late, prev_early = up(late_kv), up(early_kv)

time: 101 us -> 101 us (level)
  starting transfers between devices: 35.1 us -> 36.5 us
    ppermute x6, starting transfers between devices: 10.9 us -> 12.4 us  [up(): return lax.ppermute(value, 'seq', [(i, (i + by) % 4) for i in range(4)])]
    ppermute x5, waiting for transfers between devices: 11.3 us -> 9.83 us  [across(): return lax.ppermute(value, 'head', SWAP)]
  transfers between devices with their start and end apart: 28 -> 28, of which waited for: 9 -> 10; matrix products, arithmetic and copies ran while one was open for 2% -> 2% of each run, Pallas kernels for 36% -> 36%
where the time goes in v6:
time: 101 us
  Pallas kernels  39.8 us (39%)
  starting transfers between devices  36.5 us (36%)
  waiting for transfers between devices  20.2 us (20%)
  other arithmetic  2.16 us (2%)
  local copies, waits for them, and re-layouts  1.44 us (1%)
    pallas_call x17, Pallas kernels, call(): pl.pallas_call(body, out_shape=out_shape, in_specs=list(in_specs) + [HB]...  39.8 us
    ppermute x6, starting transfers between devices, up(): return lax.ppermute(value, 'seq', [(i, (i + by) % 4) for i in range(4)])  12.4 us
    ppermute x5, waiting for transfers between devices, across(): return lax.ppermute(value, 'head', SWAP)  9.83 us
    ppermute x5, starting transfers between devices, across(): return lax.ppermute(value, 'head', SWAP)  6.91 us
    ppermute x3, starting transfers between devices, swapped(): return lax.ppermute(value, 'seq', [(j, j ^ by) for j in range(4)])  6.26 us
    ppermute x6, waiting for transfers between devices, up(): return lax.ppermute(value, 'seq', [(i, (i + by) % 4) for i in range(4)])  5.01 us
    ppermute x8, waiting for transfers between devices, core(): return lax.ppermute(value, 'rep', SWAP)  4.72 us
    ppermute x3, starting transfers between devices, exchange_quarters(): lax.ppermute(quarters[s], 'seq', [(j, j ^ s) for j in range(4)])  4.45 us
  transfers between devices with their start and end apart: 28, of which 10 were waited for; matrix products, arithmetic and copies ran while one was open for 2% of the time, Pallas kernels for 36%

profile of v6, /device:TPU:0, one launch (start us, length us, event | category | flops | bytes accessed | tf_op | source)
XLA Modules:
  0.0 101.0 jit_solution(18041022983903355550)
XLA Ops:
  0.5 2.5 %collective-permute-start.1 = (bf16[1344,512]{1,0:T(8,128)(2,1)}, bf16[1344,512]{1,0:T(8,128)(2,1)S(1)}, u32[]{:S(2)}, u32[]{:S(2)}) collective-permute-start(bf16[1344,512]{1,0:T(8,128)(2,1)} %bitcast.11), channel_id=1, source_target_pairs={{0,2},{2,0},{1,3},{3,1},{4,6},{6,4},{5,7},{7,5},{8,10},{10,8},{9,1... | collective-permute-start | bytes 4128776 | tf_op jit(solution)/shard_map/ppermute | solution.py:666
  3.7 2.5 %pack.1 = (bf16[64,1344]{1,0:T(8,128)(2,1)S(1)}, bf16[64,1344]{1,0:T(8,128)(2,1)}, bf16[64,1344]{1,0:T(8,128)(2,1)}, bf16[64,1344]{1,0:T(8,128)(2,1)}) custom-call(s32[2]{0:T(128)S(1)} %copy-done.4, bf16[2,96,1344]{2,1,0:T(8,128)(2,1)} %bitcast.20, bf16[2,32,512]{2,1,0:T(8,128)(2,1)} %refs_2_.2, bf16[2,2,32,512]{3,2,1,0:T(8,128)(2,1)} %refs_3_.2), custom_call_target="tpu_custom_call" | custom-call | flops 1000 | bytes 1000 | tf_op jit(solution)/shard_map/pack/pallas_call | solution.py:312
  6.2 1.6 %collective-permute-start.2 = (bf16[64,1344]{1,0:T(8,128)(2,1)}, bf16[64,1344]{1,0:T(8,128)(2,1)}, u32[]{:S(2)}, u32[]{:S(2)}) collective-permute-start(bf16[64,1344]{1,0:T(8,128)(2,1)} %get-tuple-element.35), channel_id=1, source_target_pairs={{0,4},{4,0},{8,12},{12,8},{1,5},{5,1},{9,13},{13,9},{2,6},{6,2},{1... | collective-permute-start | bytes 516104 | tf_op jit(solution)/shard_map/ppermute | solution.py:634
  7.8 2.6 %collective-permute-start.3 = (bf16[64,1344]{1,0:T(8,128)(2,1)}, bf16[64,1344]{1,0:T(8,128)(2,1)}, u32[]{:S(2)}, u32[]{:S(2)}) collective-permute-start(bf16[64,1344]{1,0:T(8,128)(2,1)} %get-tuple-element.36), channel_id=1, source_target_pairs={{0,8},{4,12},{8,0},{12,4},{1,9},{5,13},{9,1},{13,5},{2,10},{6,14},... | collective-permute-start | bytes 516104 | tf_op jit(solution)/shard_map/ppermute | solution.py:634
  10.6 2.3 %pack_out.1.refs_6_.refs_0_ = bf16[64,1920]{1,0:T(8,128)(2,1)} custom-call(s32[2]{0:T(128)S(1)} %copy-done.4, bf16[2,32,512]{2,1,0:T(8,128)(2,1)} %bitcast.21, bf16[2,32,1344]{2,1,0:T(8,128)(2,1)} %refs_2_.3, bf16[64,1344]{1,0:T(8,128)(2,1)S(1)} %get-tuple-element.33.refs_3_.refs_0_), custom_call_target="tpu_custom_call" | custom-call | flops 1000 | bytes 1000 | tf_op jit(solution)/shard_map/pack_out/pallas_call | solution.py:312
  15.5 1.4 %multiply_sine_fusion = (f32[64,1536]{1,0:T(8,128)S(1)}, f32[64,1536]{1,0:T(8,128)S(1)}) fusion(f32[1536]{0:T(1024)S(1)} %fusion, f32[64]{0:T(128)S(1)} %multiply_power_fusion), kind=kLoop, calls=%fused_computation | loop fusion | flops 98304 | bytes 792832 | tf_op jit(solution)/shard_map/sin | solution.py:741
  17.1 6.7 %near.1 = (f32[256,1024]{1,0:T(8,128)S(1)}, f32[256,1024]{1,0:T(8,128)S(1)}, bf16[2,1344,256]{2,1,0:T(8,128)(2,1)S(1)}, bf16[2,1344,256]{2,1,0:T(8,128)(2,1)S(1)}, bf16[2,1344,512]{2,1,0:T(8,128)(2,1)S(1)}) custom-call(s32[21]{0:T(128)S(1)} %concatenate.3.refs_0_, bf16[1344,512]{1,0:T(8,128)(2,1)S(1)} %bitcast.12, ...), custom_call_target="tpu_custom_call" | custom-call | flops 1000 | bytes 1000 | tf_op jit(solution)/shard_map/near/pallas_call | solution.py:312
  25.4 3.4 %collective-permute-start.5 = (bf16[64,1344]{1,0:T(8,128)(2,1)S(1)}, bf16[64,1344]{1,0:T(8,128)(2,1)S(1)}, u32[]{:S(2)}, u32[]{:S(2)}) collective-permute-start(bf16[64,1344]{1,0:T(8,128)(2,1)S(1)} %sum.1.refs_2_), channel_id=1, source_target_pairs={{0,4},{4,0},{8,12},{12,8},{1,5},{5,1},{9,13},{13,9},{2,6},{6,2},{1... | collective-permute-start | bytes 516104 | tf_op jit(solution)/shard_map/ppermute | solution.py:638
  30.6 3.4 %collective-permute-done.1.refs_1_ = bf16[1344,512]{1,0:T(8,128)(2,1)S(1)} collective-permute-done((bf16[1344,512]{1,0:T(8,128)(2,1)}, bf16[1344,512]{1,0:T(8,128)(2,1)S(1)}, u32[]{:S(2)}, u32[]{:S(2)}) %collective-permute-start.1) | collective-permute-done | bytes 1376288 | tf_op jit(solution)/shard_map/ppermute | solution.py:666
  34.7 2.4 %collective-permute-done.8.refs_2_ = bf16[1344,512]{1,0:T(8,128)(2,1)S(1)} collective-permute-done((bf16[1344,512]{1,0:T(8,128)(2,1)S(1)}, bf16[1344,512]{1,0:T(8,128)(2,1)S(1)}, u32[]{:S(2)}, u32[]{:S(2)}) %collective-permute-start.8) | collective-permute-done | bytes 1376288 | tf_op jit(solution)/shard_map/ppermute | solution.py:669
  37.1 2.0 %far.2 = (f32[512,256]{1,0:T(8,128)S(1)}, bf16[512,256]{1,0:T(8,128)(2,1)S(1)}) custom-call(f32[256,1024]{1,0:T(8,128)S(1)} %get-tuple-element.43.refs_0_, bf16[1344,512]{1,0:T(8,128)(2,1)S(1)} %collective-permute-done.1.refs_1_, bf16[1344,512]{1,0:T(8,128)(2,1)S(1)} %collective-permute-done.8.refs_2_, bf16[2,1344,256]{2,1,0:T(8,128)(2,1)S(1)} %get-tuple-element.40.refs_3_, ...), custom_call_target="tpu_custom_call" | custom-call | flops 1000 | bytes 1000 | tf_op jit(solution)/shard_map/far/pallas_call | solution.py:312
  40.5 5.8 %collective-permute-start.13 = (bf16[512,256]{1,0:T(8,128)(2,1)S(1)}, bf16[512,256]{1,0:T(8,128)(2,1)S(1)}, u32[]{:S(2)}, u32[]{:S(2)}) collective-permute-start(bf16[512,256]{1,0:T(8,128)(2,1)S(1)} %get-tuple-element.44.refs_6_.refs_4_), channel_id=1, source_target_pairs={{0,4},{4,8},{8,12},{12,0},{1,5},{5,9},{9,13},{13,1},{2,6},{6,10},{... | collective-permute-start | bytes 786440 | tf_op jit(solution)/shard_map/ppermute | solution.py:672
  47.5 2.0 %far.3 = (f32[512,256]{1,0:T(8,128)S(1)}, bf16[512,256]{1,0:T(8,128)(2,1)S(1)}) custom-call(f32[256,1024]{1,0:T(8,128)S(1)} %get-tuple-element.34.refs_4_.refs_0_, bf16[1344,512]{1,0:T(8,128)(2,1)S(1)} %collective-permute-done.1.refs_1_, bf16[1344,512]{1,0:T(8,128)(2,1)S(1)} %collective-permute-done.8.refs_2_, ...), custom_call_target="tpu_custom_call" | custom-call | flops 1000 | bytes 1000 | tf_op jit(solution)/shard_map/far/pallas_call | solution.py:312
  49.5 1.6 %collective-permute-start.12 = (bf16[512,256]{1,0:T(8,128)(2,1)S(1)}, bf16[512,256]{1,0:T(8,128)(2,1)S(1)}, u32[]{:S(2)}, u32[]{:S(2)}) collective-permute-start(bf16[512,256]{1,0:T(8,128)(2,1)S(1)} %get-tuple-element.48.refs_3_), channel_id=1, source_target_pairs={{0,4},{4,8},{8,12},{12,0},{1,5},{5,9},{9,13},{13,1},{2,6},{6,10},{... | collective-permute-start | bytes 786440 | tf_op jit(solution)/shard_map/ppermute | solution.py:672
  51.2 2.2 %collective-permute-done.11 = f32[96,512]{1,0:T(8,128)S(1)} collective-permute-done((f32[96,512]{1,0:T(8,128)S(1)}, f32[96,512]{1,0:T(8,128)S(1)}, u32[]{:S(2)}, u32[]{:S(2)}) %collective-permute-start.11) | collective-permute-done | bytes 196640 | tf_op jit(solution)/shard_map/ppermute | solution.py:666
  53.4 1.6 %collective-permute-start.14 = (bf16[64,512]{1,0:T(8,128)(2,1)S(1)}, bf16[64,512]{1,0:T(8,128)(2,1)S(1)}, u32[]{:S(2)}, u32[]{:S(2)}) collective-permute-start(bf16[64,512]{1,0:T(8,128)(2,1)S(1)} %slice.7), channel_id=1, source_target_pairs={{0,4},{4,8},{8,12},{12,0},{1,5},{5,9},{9,13},{13,1},{2,6},{6,10},{... | collective-permute-start | bytes 196616 | tf_op jit(solution)/shard_map/ppermute | solution.py:672
  55.1 1.3 %collective-permute-start.16 = (bf16[512,256]{1,0:T(8,128)(2,1)S(1)}, bf16[512,256]{1,0:T(8,128)(2,1)S(1)}, u32[]{:S(2)}, u32[]{:S(2)}) collective-permute-start(bf16[512,256]{1,0:T(8,128)(2,1)S(1)} %collective-permute-done.13.refs_5_), channel_id=1, source_target_pairs={{0,4},{4,8},{8,12},{12,0},{1,5},{5,9},{9,13},{13,1},{2,6},{6,10},{... | collective-permute-start | bytes 786440 | tf_op jit(solution)/shard_map/ppermute | solution.py:672
  56.4 5.0 %attend_own.1 = (bf16[512,512]{1,0:T(8,128)(2,1)S(1)}, f32[512,512]{1,0:T(8,128)S(1)}, f32[8,512]{1,0:T(8,128)S(1)}, bf16[1344,2048]{1,0:T(8,128)(2,1)S(1)}) custom-call(s32[21]{0:T(128)S(1)} %concatenate.3.refs_0_, f32[512,256]{1,0:T(8,128)S(1)} %get-tuple-element.46.refs_1_, f32[512,256]{1,0:T(8,128)S(1)} %get-tuple-element.47.refs_2_, ...), custom_call_target="tpu_custom_call" | custom-call | flops 1000 | bytes 1000 | tf_op jit(solution)/shard_map/attend_own/pallas_call | solution.py:312
  62.4 1.6 %collective-permute-start.17 = (bf16[64,512]{1,0:T(8,128)(2,1)S(1)}, bf16[64,512]{1,0:T(8,128)(2,1)S(1)}, u32[]{:S(2)}, u32[]{:S(2)}) collective-permute-start(bf16[64,512]{1,0:T(8,128)(2,1)S(1)} %collective-permute-done.14.refs_6_), channel_id=1, source_target_pairs={{0,4},{4,8},{8,12},{12,0},{1,5},{5,9},{9,13},{13,1},{2,6},{6,10},{... | collective-permute-start | bytes 196616 | tf_op jit(solution)/shard_map/ppermute | solution.py:672
  64.0 2.4 %collective-permute-start.18 = (bf16[64,512]{1,0:T(8,128)(2,1)S(1)}, bf16[64,512]{1,0:T(8,128)(2,1)S(1)}, u32[]{:S(2)}, u32[]{:S(2)}) collective-permute-start(bf16[64,512]{1,0:T(8,128)(2,1)S(1)} %get-tuple-element.38.refs_3_), channel_id=1, source_target_pairs={{0,8},{4,12},{8,0},{12,4},{1,9},{5,13},{9,1},{13,5},{2,10},{6,14},... | collective-permute-start | bytes 196616 | tf_op jit(solution)/shard_map/ppermute | solution.py:681
  66.4 3.5 %attend_prev.1 = (f32[512,512]{1,0:T(8,128)S(1)}, f32[8,512]{1,0:T(8,128)S(1)}) custom-call(s32[21]{0:T(128)S(1)} %concatenate.3.refs_0_, bf16[512,512]{1,0:T(8,128)(2,1)S(1)} %get-tuple-element.50.refs_1_, f32[512,512]{1,0:T(8,128)S(1)} %get-tuple-element.51.refs_2_, f32[8,512]{1,0:T(8,128)S(1)} %get-tuple-element.52.refs_3_, ...), custom_call_target="tpu_custom_call" | custom-call | flops 1000 | bytes 1000 | tf_op jit(solution)/shard_map/attend_prev/pallas_call | solution.py:312
  69.9 4.5 %collective-permute-done.17.refs_5_.refs_6_ = bf16[64,512]{1,0:T(8,128)(2,1)S(1)} collective-permute-done((bf16[64,512]{1,0:T(8,128)(2,1)S(1)}, bf16[64,512]{1,0:T(8,128)(2,1)S(1)}, u32[]{:S(2)}, u32[]{:S(2)}) %collective-permute-start.17) | collective-permute-done | bytes 65568 | tf_op jit(solution)/shard_map/ppermute | solution.py:672
  74.3 1.7 %attend_far.2.refs_11_.refs_1_.refs_2_ = bf16[512,256]{1,0:T(8,128)(2,1)S(1)} custom-call(s32[21]{0:T(128)S(1)} %concatenate.3.refs_0_, bf16[512,512]{1,0:T(8,128)(2,1)S(1)} %get-tuple-element.50.refs_1_, f32[512,512]{1,0:T(8,128)S(1)} %get-tuple-element.53.refs_2_, f32[8,512]{1,0:T(8,128)S(1)} %get-tuple-element.54.refs_3_, ...), custom_call_target="tpu_custom_call" | custom-call | flops 1000 | bytes 1000 | tf_op jit(solution)/shard_map/attend_far/pallas_call | solution.py:312
  76.3 2.1 %attend_far.3.refs_4_.refs_1_ = bf16[512,256]{1,0:T(8,128)(2,1)S(1)} custom-call(s32[21]{0:T(128)S(1)} %concatenate.3.refs_0_, bf16[512,512]{1,0:T(8,128)(2,1)S(1)} %get-tuple-element.50.refs_1_, f32[512,512]{1,0:T(8,128)S(1)} %get-tuple-element.53.refs_2_, f32[8,512]{1,0:T(8,128)S(1)} %get-tuple-element.54.refs_3_, ...), custom_call_target="tpu_custom_call" | custom-call | flops 1000 | bytes 1000 | tf_op jit(solution)/shard_map/attend_far/pallas_call | solution.py:312
  80.8 3.1 %collective-permute-start.24 = (bf16[64,1344]{1,0:T(8,128)(2,1)S(1)}, bf16[64,1344]{1,0:T(8,128)(2,1)S(1)}, u32[]{:S(2)}, u32[]{:S(2)}) collective-permute-start(bf16[64,1344]{1,0:T(8,128)(2,1)S(1)} %get-tuple-element.58.refs_6_), channel_id=1, source_target_pairs={{0,8},{4,12},{8,0},{12,4},{1,9},{5,13},{9,1},{13,5},{2,10},{6,14},... | collective-permute-start | bytes 516104 | tf_op jit(solution)/shard_map/ppermute | solution.py:681
  83.9 1.4 %out_near.2.refs_5_.refs_4_ = f32[1344,256]{1,0:T(8,128)S(1)} custom-call(s32[21]{0:T(128)S(1)} %concatenate.3.refs_0_, bf16[512,256]{1,0:T(8,128)(2,1)S(1)} %attend_far.2.refs_11_.refs_1_.refs_2_, bf16[512,256]{1,0:T(8,128)(2,1)S(1)} %collective-permute-done.21.refs_2_, bf16[1344,2048]{1,0:T(8,128)(2,1)S(1)} %get-tuple-element.57.refs_3_, ...), custom_call_target="tpu_custom_call" | custom-call | flops 1000 | bytes 1000 | tf_op jit(solution)/shard_map/out_near/pallas_call | solution.py:312
  85.3 1.4 %out_near.3.refs_5_.refs_4_ = f32[1344,256]{1,0:T(8,128)S(1)} custom-call(s32[21]{0:T(128)S(1)} %concatenate.3.refs_0_, bf16[512,256]{1,0:T(8,128)(2,1)S(1)} %attend_far.3.refs_4_.refs_1_, bf16[512,256]{1,0:T(8,128)(2,1)S(1)} %collective-permute-done.20.refs_2_, bf16[1344,2048]{1,0:T(8,128)(2,1)S(1)} %get-tuple-element.57.refs_3_, ...), custom_call_target="tpu_custom_call" | custom-call | flops 1000 | bytes 1000 | tf_op jit(solution)/shard_map/out_near/pallas_call | solution.py:312
  87.6 1.2 %collective-permute-done.22 = f32[32,512]{1,0:T(8,128)S(1)} collective-permute-done((f32[32,512]{1,0:T(8,128)S(1)}, f32[32,512]{1,0:T(8,128)S(1)}, u32[]{:S(2)}, u32[]{:S(2)}) %collective-permute-start.22) | collective-permute-done | bytes 65568 | tf_op jit(solution)/shard_map/ppermute | solution.py:669
  88.9 1.2 %collective-permute-start.23 = (f32[32,512]{1,0:T(8,128)S(1)}, f32[32,512]{1,0:T(8,128)S(1)}, u32[]{:S(2)}, u32[]{:S(2)}) collective-permute-start(f32[32,512]{1,0:T(8,128)S(1)} %add.27), channel_id=1, source_target_pairs={{0,2},{2,0},{1,3},{3,1},{4,6},{6,4},{5,7},{7,5},{8,10},{10,8},{9,1... | collective-permute-start | bytes 196616 | tf_op jit(solution)/shard_map/ppermute | solution.py:666
  90.0 4.2 %collective-permute-done.23 = f32[32,512]{1,0:T(8,128)S(1)} collective-permute-done((f32[32,512]{1,0:T(8,128)S(1)}, f32[32,512]{1,0:T(8,128)S(1)}, u32[]{:S(2)}, u32[]{:S(2)}) %collective-permute-start.23) | collective-permute-done | bytes 65568 | tf_op jit(solution)/shard_map/ppermute | solution.py:666
  95.9 2.6 %out_far.2.refs_8_ = bf16[1344,512]{1,0:T(8,128)(2,1)} custom-call(s32[21]{0:T(128)S(1)} %concatenate.3.refs_0_, bf16[512,256]{1,0:T(8,128)(2,1)S(1)} %collective-permute-done.26.refs_1_, bf16[512,256]{1,0:T(8,128)(2,1)S(1)} %collective-permute-done.27.refs_2_, bf16[1344,2048]{1,0:T(8,128)(2,1)S(1)} %get-tuple-element.57.refs_3_, ...), custom_call_target="tpu_custom_call" | custom-call | flops 1000 | bytes 1000 | tf_op jit(solution)/shard_map/out_far/pallas_call | solution.py:312
  98.4 2.6 %out_far.3 = bf16[1344,512]{1,0:T(8,128)(2,1)} custom-call(s32[21]{0:T(128)S(1)} %concatenate.3.refs_0_, bf16[512,256]{1,0:T(8,128)(2,1)S(1)} %collective-permute-done.19.refs_1_, bf16[512,256]{1,0:T(8,128)(2,1)S(1)} %collective-permute-done.25.refs_2_, bf16[1344,2048]{1,0:T(8,128)(2,1)S(1)} %get-tuple-element.57.refs_3_, ...), custom_call_target="tpu_custom_call", output_to_operand_aliasing={{}: (8, {})} | custom-call | flops 1000 | bytes 1000 | tf_op jit(solution)/shard_map/out_far/pallas_call | solution.py:312
  (67 shorter events, 16.1 us)
Async XLA Ops:
  0.0 17.1 %copy-start = (bf16[512,1344]{0,1:T(8,128)(2,1)S(1)}, bf16[512,1344]{0,1:T(8,128)(2,1)}, u32[]{:S(2)}) copy-start(bf16[512,1344]{0,1:T(8,128)(2,1)} %param.14) | copy-start | bytes 4128772
  0.0 14.8 %collective-permute-start = (bf16[1344,512]{1,0:T(8,128)(2,1)}, bf16[1344,512]{1,0:T(8,128)(2,1)}, u32[]{:S(2)}, u32[]{:S(2)}) collective-permute-start(bf16[1344,512]{1,0:T(8,128)(2,1)} %bitcast.10), channel_id=1, source_target_pairs={{0,1},{1,0},{2,3},{3,2},{4,5},{5,4},{6,7},{7,6},{8,9},{9,8},{10,11... | collective-permute-start | bytes 4128776 | tf_op jit(solution)/shard_map/ppermute | solution.py:669
  0.5 33.5 %collective-permute-start.1 = (bf16[1344,512]{1,0:T(8,128)(2,1)}, bf16[1344,512]{1,0:T(8,128)(2,1)S(1)}, u32[]{:S(2)}, u32[]{:S(2)}) collective-permute-start(bf16[1344,512]{1,0:T(8,128)(2,1)} %bitcast.11), channel_id=1, source_target_pairs={{0,2},{2,0},{1,3},{3,1},{4,6},{6,4},{5,7},{7,5},{8,10},{10,8},{9,1... | collective-permute-start | bytes 4128776 | tf_op jit(solution)/shard_map/ppermute | solution.py:666
  3.7 13.3 %copy-start.5 = (s32[2]{0:T(128)S(1)}, s32[2]{0:T(128)}, u32[]{:S(2)}) copy-start(s32[2]{0:T(128)} %refs_0_.3) | copy-start | bytes 28
  6.2 17.6 %collective-permute-start.2 = (bf16[64,1344]{1,0:T(8,128)(2,1)}, bf16[64,1344]{1,0:T(8,128)(2,1)}, u32[]{:S(2)}, u32[]{:S(2)}) collective-permute-start(bf16[64,1344]{1,0:T(8,128)(2,1)} %get-tuple-element.35), channel_id=1, source_target_pairs={{0,4},{4,0},{8,12},{12,8},{1,5},{5,1},{9,13},{13,9},{2,6},{6,2},{1... | collective-permute-start | bytes 516104 | tf_op jit(solution)/shard_map/ppermute | solution.py:634
  7.8 16.4 %collective-permute-start.3 = (bf16[64,1344]{1,0:T(8,128)(2,1)}, bf16[64,1344]{1,0:T(8,128)(2,1)}, u32[]{:S(2)}, u32[]{:S(2)}) collective-permute-start(bf16[64,1344]{1,0:T(8,128)(2,1)} %get-tuple-element.36), channel_id=1, source_target_pairs={{0,8},{4,12},{8,0},{12,4},{1,9},{5,13},{9,1},{13,5},{2,10},{6,14},... | collective-permute-start | bytes 516104 | tf_op jit(solution)/shard_map/ppermute | solution.py:634
  10.4 13.8 %collective-permute-start.4 = (bf16[64,1344]{1,0:T(8,128)(2,1)}, bf16[64,1344]{1,0:T(8,128)(2,1)}, u32[]{:S(2)}, u32[]{:S(2)}) collective-permute-start(bf16[64,1344]{1,0:T(8,128)(2,1)} %get-tuple-element.37), channel_id=1, source_target_pairs={{0,12},{4,8},{8,4},{12,0},{1,13},{5,9},{9,5},{13,1},{2,14},{6,10},... | collective-permute-start | bytes 516104 | tf_op jit(solution)/shard_map/ppermute | solution.py:634
  14.8 14.7 %collective-permute-start.7 = (bf16[64,1920]{1,0:T(8,128)(2,1)}, bf16[64,1920]{1,0:T(8,128)(2,1)}, u32[]{:S(2)}, u32[]{:S(2)}) collective-permute-start(bf16[64,1920]{1,0:T(8,128)(2,1)} %pack_out.1.refs_6_.refs_0_), channel_id=1, source_target_pairs={{0,4},{4,0},{8,12},{12,8},{1,5},{5,1},{9,13},{13,9},{2,6},{6,2},{1... | collective-permute-start | bytes 737288 | tf_op jit(solution)/shard_map/ppermute | solution.py:681
  25.4 8.6 %collective-permute-start.5 = (bf16[64,1344]{1,0:T(8,128)(2,1)S(1)}, bf16[64,1344]{1,0:T(8,128)(2,1)S(1)}, u32[]{:S(2)}, u32[]{:S(2)}) collective-permute-start(bf16[64,1344]{1,0:T(8,128)(2,1)S(1)} %sum.1.refs_2_), channel_id=1, source_target_pairs={{0,4},{4,0},{8,12},{12,8},{1,5},{5,1},{9,13},{13,9},{2,6},{6,2},{1... | collective-permute-start | bytes 516104 | tf_op jit(solution)/shard_map/ppermute | solution.py:638
  28.8 5.2 %collective-permute-start.6 = (bf16[64,1344]{1,0:T(8,128)(2,1)S(1)}, bf16[64,1344]{1,0:T(8,128)(2,1)S(1)}, u32[]{:S(2)}, u32[]{:S(2)}) collective-permute-start(bf16[64,1344]{1,0:T(8,128)(2,1)S(1)} %sum.1.refs_2_), channel_id=1, source_target_pairs={{4,8},{8,4},{5,9},{9,5},{6,10},{10,6},{7,11},{11,7},{20,24},{24,20... | collective-permute-start | bytes 516104 | tf_op jit(solution)/shard_map/ppermute | solution.py:640
  34.0 3.1 %collective-permute-start.8 = (bf16[1344,512]{1,0:T(8,128)(2,1)S(1)}, bf16[1344,512]{1,0:T(8,128)(2,1)S(1)}, u32[]{:S(2)}, u32[]{:S(2)}) collective-permute-start(bf16[1344,512]{1,0:T(8,128)(2,1)S(1)} %collective-permute-done.1.refs_1_), channel_id=1, source_target_pairs={{0,1},{1,0},{2,3},{3,2},{4,5},{5,4},{6,7},{7,6},{8,9},{9,8},{10,11... | collective-permute-start | bytes 4128776 | tf_op jit(solution)/shard_map/ppermute | solution.py:669
  34.0 5.2 %collective-permute-start.9 = (bf16[64,1344]{1,0:T(8,128)(2,1)S(1)}, bf16[64,1344]{1,0:T(8,128)(2,1)S(1)}, u32[]{:S(2)}, u32[]{:S(2)}) collective-permute-start(bf16[64,1344]{1,0:T(8,128)(2,1)S(1)} %collective-permute-done.5.refs_6_.refs_3_), channel_id=1, source_target_pairs={{4,8},{8,4},{5,9},{9,5},{6,10},{10,6},{7,11},{11,7},{20,24},{24,20... | collective-permute-start | bytes 516104 | tf_op jit(solution)/shard_map/ppermute | solution.py:640
  40.3 6.0 %collective-permute-start.10 = (f32[96,512]{1,0:T(8,128)S(1)}, f32[96,512]{1,0:T(8,128)S(1)}, u32[]{:S(2)}, u32[]{:S(2)}) collective-permute-start(f32[96,512]{1,0:T(8,128)S(1)} %get-tuple-element.45), channel_id=1, source_target_pairs={{0,1},{1,0},{2,3},{3,2},{4,5},{5,4},{6,7},{7,6},{8,9},{9,8},{10,11... | collective-permute-start | bytes 589832 | tf_op jit(solution)/shard_map/ppermute | solution.py:669
  40.5 14.6 %collective-permute-start.13 = (bf16[512,256]{1,0:T(8,128)(2,1)S(1)}, bf16[512,256]{1,0:T(8,128)(2,1)S(1)}, u32[]{:S(2)}, u32[]{:S(2)}) collective-permute-start(bf16[512,256]{1,0:T(8,128)(2,1)S(1)} %get-tuple-element.44.refs_6_.refs_4_), channel_id=1, source_target_pairs={{0,4},{4,8},{8,12},{12,0},{1,5},{5,9},{9,13},{13,1},{2,6},{6,10},{... | collective-permute-start | bytes 786440 | tf_op jit(solution)/shard_map/ppermute | solution.py:672
  46.3 10.1 %copy-start.3 = (f32[128]{0:T(128)S(1)}, f32[128]{0:T(128)}, u32[]{:S(2)}) copy-start(f32[128]{0:T(128)} %param.20) | copy-start | bytes 1540
  46.3 10.1 %copy-start.6 = (f32[128]{0:T(128)S(1)}, f32[128]{0:T(128)}, u32[]{:S(2)}) copy-start(f32[128]{0:T(128)} %param.19) | copy-start | bytes 1540
  46.3 7.0 %collective-permute-start.11 = (f32[96,512]{1,0:T(8,128)S(1)}, f32[96,512]{1,0:T(8,128)S(1)}, u32[]{:S(2)}, u32[]{:S(2)}) collective-permute-start(f32[96,512]{1,0:T(8,128)S(1)} %add.25.refs_6_), channel_id=1, source_target_pairs={{0,2},{2,0},{1,3},{3,1},{4,6},{6,4},{5,7},{7,5},{8,10},{10,8},{9,1... | collective-permute-start | bytes 589832 | tf_op jit(solution)/shard_map/ppermute | solution.py:666
  49.5 12.4 %collective-permute-start.12 = (bf16[512,256]{1,0:T(8,128)(2,1)S(1)}, bf16[512,256]{1,0:T(8,128)(2,1)S(1)}, u32[]{:S(2)}, u32[]{:S(2)}) collective-permute-start(bf16[512,256]{1,0:T(8,128)(2,1)S(1)} %get-tuple-element.48.refs_3_), channel_id=1, source_target_pairs={{0,4},{4,8},{8,12},{12,0},{1,5},{5,9},{9,13},{13,1},{2,6},{6,10},{... | collective-permute-start | bytes 786440 | tf_op jit(solution)/shard_map/ppermute | solution.py:672
  53.4 8.6 %collective-permute-start.14 = (bf16[64,512]{1,0:T(8,128)(2,1)S(1)}, bf16[64,512]{1,0:T(8,128)(2,1)S(1)}, u32[]{:S(2)}, u32[]{:S(2)}) collective-permute-start(bf16[64,512]{1,0:T(8,128)(2,1)S(1)} %slice.7), channel_id=1, source_target_pairs={{0,4},{4,8},{8,12},{12,0},{1,5},{5,9},{9,13},{13,1},{2,6},{6,10},{... | collective-permute-start | bytes 196616 | tf_op jit(solution)/shard_map/ppermute | solution.py:672
  55.1 14.8 %collective-permute-start.16 = (bf16[512,256]{1,0:T(8,128)(2,1)S(1)}, bf16[512,256]{1,0:T(8,128)(2,1)S(1)}, u32[]{:S(2)}, u32[]{:S(2)}) collective-permute-start(bf16[512,256]{1,0:T(8,128)(2,1)S(1)} %collective-permute-done.13.refs_5_), channel_id=1, source_target_pairs={{0,4},{4,8},{8,12},{12,0},{1,5},{5,9},{9,13},{13,1},{2,6},{6,10},{... | collective-permute-start | bytes 786440 | tf_op jit(solution)/shard_map/ppermute | solution.py:672
  62.0 14.4 %collective-permute-start.15 = (bf16[512,256]{1,0:T(8,128)(2,1)S(1)}, bf16[512,256]{1,0:T(8,128)(2,1)S(1)}, u32[]{:S(2)}, u32[]{:S(2)}) collective-permute-start(bf16[512,256]{1,0:T(8,128)(2,1)S(1)} %collective-permute-done.12.refs_4_), channel_id=1, source_target_pairs={{0,4},{4,8},{8,12},{12,0},{1,5},{5,9},{9,13},{13,1},{2,6},{6,10},{... | collective-permute-start | bytes 786440 | tf_op jit(solution)/shard_map/ppermute | solution.py:672
  62.4 11.9 %collective-permute-start.17 = (bf16[64,512]{1,0:T(8,128)(2,1)S(1)}, bf16[64,512]{1,0:T(8,128)(2,1)S(1)}, u32[]{:S(2)}, u32[]{:S(2)}) collective-permute-start(bf16[64,512]{1,0:T(8,128)(2,1)S(1)} %collective-permute-done.14.refs_6_), channel_id=1, source_target_pairs={{0,4},{4,8},{8,12},{12,0},{1,5},{5,9},{9,13},{13,1},{2,6},{6,10},{... | collective-permute-start | bytes 196616 | tf_op jit(solution)/shard_map/ppermute | solution.py:672
  64.0 12.4 %collective-permute-start.18 = (bf16[64,512]{1,0:T(8,128)(2,1)S(1)}, bf16[64,512]{1,0:T(8,128)(2,1)S(1)}, u32[]{:S(2)}, u32[]{:S(2)}) collective-permute-start(bf16[64,512]{1,0:T(8,128)(2,1)S(1)} %get-tuple-element.38.refs_3_), channel_id=1, source_target_pairs={{0,8},{4,12},{8,0},{12,4},{1,9},{5,13},{9,1},{13,5},{2,10},{6,14},... | collective-permute-start | bytes 196616 | tf_op jit(solution)/shard_map/ppermute | solution.py:681
  76.0 7.9 %collective-permute-start.21 = (bf16[512,256]{1,0:T(8,128)(2,1)S(1)}, bf16[512,256]{1,0:T(8,128)(2,1)S(1)}, u32[]{:S(2)}, u32[]{:S(2)}) collective-permute-start(bf16[512,256]{1,0:T(8,128)(2,1)S(1)} %attend_far.2.refs_11_.refs_1_.refs_2_), channel_id=1, source_target_pairs={{0,1},{1,0},{2,3},{3,2},{4,5},{5,4},{6,7},{7,6},{8,9},{9,8},{10,11... | collective-permute-start | bytes 786440 | tf_op jit(solution)/shard_map/ppermute | solution.py:669
  78.4 6.9 %collective-permute-start.20 = (bf16[512,256]{1,0:T(8,128)(2,1)S(1)}, bf16[512,256]{1,0:T(8,128)(2,1)S(1)}, u32[]{:S(2)}, u32[]{:S(2)}) collective-permute-start(bf16[512,256]{1,0:T(8,128)(2,1)S(1)} %attend_far.3.refs_4_.refs_1_), channel_id=1, source_target_pairs={{0,1},{1,0},{2,3},{3,2},{4,5},{5,4},{6,7},{7,6},{8,9},{9,8},{10,11... | collective-permute-start | bytes 786440 | tf_op jit(solution)/shard_map/ppermute | solution.py:669
  78.8 15.5 %collective-permute-start.26 = (bf16[512,256]{1,0:T(8,128)(2,1)S(1)}, bf16[512,256]{1,0:T(8,128)(2,1)S(1)}, u32[]{:S(2)}, u32[]{:S(2)}) collective-permute-start(bf16[512,256]{1,0:T(8,128)(2,1)S(1)} %attend_far.2.refs_11_.refs_1_.refs_2_), channel_id=1, source_target_pairs={{0,2},{2,0},{1,3},{3,1},{4,6},{6,4},{5,7},{7,5},{8,10},{10,8},{9,1... | collective-permute-start | bytes 786440 | tf_op jit(solution)/shard_map/ppermute | solution.py:666
  79.7 14.7 %collective-permute-start.19 = (bf16[512,256]{1,0:T(8,128)(2,1)S(1)}, bf16[512,256]{1,0:T(8,128)(2,1)S(1)}, u32[]{:S(2)}, u32[]{:S(2)}) collective-permute-start(bf16[512,256]{1,0:T(8,128)(2,1)S(1)} %attend_far.3.refs_4_.refs_1_), channel_id=1, source_target_pairs={{0,2},{2,0},{1,3},{3,1},{4,6},{6,4},{5,7},{7,5},{8,10},{10,8},{9,1... | collective-permute-start | bytes 786440 | tf_op jit(solution)/shard_map/ppermute | solution.py:666
  80.8 13.5 %collective-permute-start.24 = (bf16[64,1344]{1,0:T(8,128)(2,1)S(1)}, bf16[64,1344]{1,0:T(8,128)(2,1)S(1)}, u32[]{:S(2)}, u32[]{:S(2)}) collective-permute-start(bf16[64,1344]{1,0:T(8,128)(2,1)S(1)} %get-tuple-element.58.refs_6_), channel_id=1, source_target_pairs={{0,8},{4,12},{8,0},{12,4},{1,9},{5,13},{9,1},{13,5},{2,10},{6,14},... | collective-permute-start | bytes 516104 | tf_op jit(solution)/shard_map/ppermute | solution.py:681
  87.5 1.3 %collective-permute-start.22 = (f32[32,512]{1,0:T(8,128)S(1)}, f32[32,512]{1,0:T(8,128)S(1)}, u32[]{:S(2)}, u32[]{:S(2)}) collective-permute-start(f32[32,512]{1,0:T(8,128)S(1)} %out_low.1), channel_id=1, source_target_pairs={{0,1},{1,0},{2,3},{3,2},{4,5},{5,4},{6,7},{7,6},{8,9},{9,8},{10,11... | collective-permute-start | bytes 196616 | tf_op jit(solution)/shard_map/ppermute | solution.py:669
  88.9 5.4 %collective-permute-start.23 = (f32[32,512]{1,0:T(8,128)S(1)}, f32[32,512]{1,0:T(8,128)S(1)}, u32[]{:S(2)}, u32[]{:S(2)}) collective-permute-start(f32[32,512]{1,0:T(8,128)S(1)} %add.27), channel_id=1, source_target_pairs={{0,2},{2,0},{1,3},{3,1},{4,6},{6,4},{5,7},{7,5},{8,10},{10,8},{9,1... | collective-permute-start | bytes 196616 | tf_op jit(solution)/shard_map/ppermute | solution.py:666
  94.3 1.6 %collective-permute-start.27 = (bf16[512,256]{1,0:T(8,128)(2,1)S(1)}, bf16[512,256]{1,0:T(8,128)(2,1)S(1)}, u32[]{:S(2)}, u32[]{:S(2)}) collective-permute-start(bf16[512,256]{1,0:T(8,128)(2,1)S(1)} %collective-permute-done.26.refs_1_), channel_id=1, source_target_pairs={{0,1},{1,0},{2,3},{3,2},{4,5},{5,4},{6,7},{7,6},{8,9},{9,8},{10,11... | collective-permute-start | bytes 786440 | tf_op jit(solution)/shard_map/ppermute | solution.py:669
  94.4 4.1 %collective-permute-start.25 = (bf16[512,256]{1,0:T(8,128)(2,1)S(1)}, bf16[512,256]{1,0:T(8,128)(2,1)S(1)}, u32[]{:S(2)}, u32[]{:S(2)}) collective-permute-start(bf16[512,256]{1,0:T(8,128)(2,1)S(1)} %collective-permute-done.19.refs_1_), channel_id=1, source_target_pairs={{0,1},{1,0},{2,3},{3,2},{4,5},{5,4},{6,7},{7,6},{8,9},{9,8},{10,11... | collective-permute-start | bytes 786440 | tf_op jit(solution)/shard_map/ppermute | solution.py:669
  (4 other events, 18.4 us)
